TPU v7x, 32 devices: a whole 2x2x4 slice. The times are simulated.
32 devices in a mesh: level: 2 (over x), gx: 4 (over z), gy: 4 (over y, core).
Axes of the slice: x: 2, y: 2, z: 4, core: 2. Of those that a mesh axis runs over, the one named last changes fastest.
Arguments:
- u_init: float32 [32, 128, 256], P('gx', 'gy'), may hold values from -6 to 6
- v_init: float32 [32, 128, 256], P('gx', 'gy'), may hold values from -6 to 6
- speed_sq: float32 [32, 128, 256], P('gx', 'gy'), may hold values from 0.25 to 1
Outputs:
- final_u: float32 [2, 32, 128, 256], P('level', 'gx', 'gy')
- final_v: float32 [2, 32, 128, 256], P('level', 'gx', 'gy')
All inputs are finite; a program needn't handle non-finite values.
Results may differ from a plain program's by a relative error of at most 0.00002.
Values sent between devices are 32-bit elements; how exact they have to be, the bound alone decides.
No kernel may reach another device: no remote copies, remote signals or barrier semaphores. Data moves between devices by JAX's collectives and lax.ppermute only.
A program may use at most 64 MiB of HBM per device.

v0:
```python
import jax
import jax.numpy as jnp
from jax import lax
from jax.sharding import PartitionSpec as P

STEPS = 8


time_step = 0.12
half_step = 0.06
damping = 0.05


def with_halo(block, sides, width):
    for axis, dim in sides:
        count = lax.axis_size(axis)
        forward = [(i, i + 1) for i in range(count - 1)]
        forward.append((count - 1, 0))
        backward = [(target, source) for source, target in forward]
        low = lax.ppermute(
            lax.slice_in_dim(block, block.shape[dim] - width, None, axis=dim), axis, forward
        )
        high = lax.ppermute(lax.slice_in_dim(block, 0, width, axis=dim), axis, backward)
        block = jnp.concatenate([low, block, high], axis=dim)
    return block


def neighbours(fields):
    return with_halo(fields, (("gx", 1), ("gy", 2)), 2)


def stencil(padded):
    width = padded.shape[1] - 4
    height = padded.shape[2] - 4
    centre = padded[:, 2 : 2 + width, 2 : 2 + height, :]
    total = -7.5 * centre
    near_x = (
        padded[:, 1 : 1 + width, 2 : 2 + height, :] + padded[:, 3 : 3 + width, 2 : 2 + height, :]
    )
    far_x = padded[:, 0:width, 2 : 2 + height, :] + padded[:, 4 : 4 + width, 2 : 2 + height, :]
    near_y = (
        padded[:, 2 : 2 + width, 1 : 1 + height, :] + padded[:, 2 : 2 + width, 3 : 3 + height, :]
    )
    far_y = padded[:, 2 : 2 + width, 0:height, :] + padded[:, 2 : 2 + width, 4 : 4 + height, :]
    near_z = jnp.roll(centre, 1, 3) + jnp.roll(centre, -1, 3)
    far_z = jnp.roll(centre, 2, 3) + jnp.roll(centre, -2, 3)
    total = total + 4.0 / 3.0 * near_x - far_x / 12.0
    total = total + 4.0 / 3.0 * near_y - far_y / 12.0
    total = total + 4.0 / 3.0 * near_z - far_z / 12.0
    return total


def body(u_init, v_init, speed_sq):
    leading = lax.axis_index("level") == 0
    laplace = stencil(neighbours(jnp.stack([u_init, v_init])))
    accel_prev = speed_sq * laplace[0] + damping * laplace[1]
    pred_u, pred_v = (u_init, v_init)
    corr_u, corr_v = (u_init, v_init)
    for moment in range(STEPS):
        next_u = pred_u + time_step * pred_v
        next_v = pred_v + time_step * accel_prev
        laplace = stencil(neighbours(jnp.stack([next_u, next_v, corr_u, corr_v])))
        accel_next = speed_sq * laplace[0] + damping * laplace[1]
        own_accel = speed_sq * laplace[2] + damping * laplace[3]
        corr_u = corr_u + time_step * corr_v + half_step * (next_v - pred_v)
        corr_v = corr_v + time_step * own_accel + half_step * (accel_next - accel_prev)
        pred_u, pred_v, accel_prev = (next_u, next_v, accel_next)
    out_u = jnp.where(leading, pred_u, corr_u)
    out_v = jnp.where(leading, pred_v, corr_v)
    return (out_u[None], out_v[None])


def solution(mesh):
    placed = (P("gx", "gy", None), P("gx", "gy", None), P("gx", "gy", None))
    return jax.shard_map(
        body,
        mesh=mesh,
        in_specs=placed,
        out_specs=(P("level", "gx", "gy", None), P("level", "gx", "gy", None)),
        check_vma=False,
    )
```

profile of v0, /device:TPU:0, one launch (start us, length us, event | category | flops | bytes accessed | tf_op | source)
XLA Modules:
  0.0 207.6 jit_solution(12209604005744443251)
XLA Ops:
  0.7 1.7 fusion.198
  2.3 3.1 %collective-permute-start = (f32[2,2,32,256]{3,2,1,0:T(8,128)}, f32[2,2,32,256]{3,2,1,0:T(8,128)S(1)}, u32[]{:S(2)}, u32[]{:S(2)}) collective-permute-start(f32[2,2,32,256]{3,2,1,0:T(8,128)} %get-tuple-element.176), channel_id=1, source_target_pairs={{0,4},{4,8},{8,12},{12,0},{1,5},{5,9},{9,13},{13,1},{2,6},{6,10},{... | collective-permute-start | bytes 393224 | tf_op jit(solution)/shard_map/ppermute | solution.py:20
  5.4 2.0 collective-permute-start.1
  7.4 1.4 fusion.99
  9.3 2.6 %collective-permute-done = f32[2,2,32,256]{3,2,1,0:T(8,128)S(1)} collective-permute-done((f32[2,2,32,256]{3,2,1,0:T(8,128)}, f32[2,2,32,256]{3,2,1,0:T(8,128)S(1)}, u32[]{:S(2)}, u32[]{:S(2)}) %collective-permute-start) | collective-permute-done | bytes 131104 | tf_op jit(solution)/shard_map/ppermute | solution.py:20
  12.0 1.2 collective-permute-done.1
  13.2 1.7 collective-permute-start.3
  15.1 1.6 collective-permute-done.2
  19.1 1.4 collective-permute-start.4
  20.5 2.5 %collective-permute-start.5 = (f32[4,2,32,256]{3,2,1,0:T(8,128)S(1)}, f32[4,2,32,256]{3,2,1,0:T(8,128)S(1)}, u32[]{:S(2)}, u32[]{:S(2)}) collective-permute-start(f32[4,2,32,256]{3,2,1,0:T(8,128)S(1)} %get-tuple-element.159), channel_id=1, source_target_pairs={{4,0},{8,4},{12,8},{0,12},{5,1},{9,5},{13,9},{1,13},{6,2},{10,6},{... | collective-permute-start | bytes 786440 | tf_op jit(solution)/shard_map/ppermute | solution.py:23
  23.2 6.4 %collective-permute-done.4 = f32[4,2,32,256]{3,2,1,0:T(8,128)S(1)} collective-permute-done((f32[4,2,32,256]{3,2,1,0:T(8,128)S(1)}, f32[4,2,32,256]{3,2,1,0:T(8,128)S(1)}, u32[]{:S(2)}, u32[]{:S(2)}) %collective-permute-start.4) | collective-permute-done | bytes 262176 | tf_op jit(solution)/shard_map/ppermute | solution.py:20
  29.6 5.3 %collective-permute-done.5 = f32[4,2,32,256]{3,2,1,0:T(8,128)S(1)} collective-permute-done((f32[4,2,32,256]{3,2,1,0:T(8,128)S(1)}, f32[4,2,32,256]{3,2,1,0:T(8,128)S(1)}, u32[]{:S(2)}, u32[]{:S(2)}) %collective-permute-start.5) | collective-permute-done | bytes 262176 | tf_op jit(solution)/shard_map/ppermute | solution.py:23
  35.2 1.5 collective-permute-start.7
  37.1 2.0 collective-permute-done.6
  39.6 1.6 fusion.73
  43.4 3.1 %collective-permute-start.9 = (f32[4,2,32,256]{3,2,1,0:T(8,128)S(1)}, f32[4,2,32,256]{3,2,1,0:T(8,128)S(1)}, u32[]{:S(2)}, u32[]{:S(2)}) collective-permute-start(f32[4,2,32,256]{3,2,1,0:T(8,128)S(1)} %get-tuple-element.147), channel_id=1, source_target_pairs={{4,0},{8,4},{12,8},{0,12},{5,1},{9,5},{13,9},{1,13},{6,2},{10,6},{... | collective-permute-start | bytes 786440 | tf_op jit(solution)/shard_map/ppermute | solution.py:23
  46.7 6.6 %collective-permute-done.8 = f32[4,2,32,256]{3,2,1,0:T(8,128)S(1)} collective-permute-done((f32[4,2,32,256]{3,2,1,0:T(8,128)S(1)}, f32[4,2,32,256]{3,2,1,0:T(8,128)S(1)}, u32[]{:S(2)}, u32[]{:S(2)}) %collective-permute-start.8) | collective-permute-done | bytes 262176 | tf_op jit(solution)/shard_map/ppermute | solution.py:20
  53.3 4.8 %collective-permute-done.9 = f32[4,2,32,256]{3,2,1,0:T(8,128)S(1)} collective-permute-done((f32[4,2,32,256]{3,2,1,0:T(8,128)S(1)}, f32[4,2,32,256]{3,2,1,0:T(8,128)S(1)}, u32[]{:S(2)}, u32[]{:S(2)}) %collective-permute-start.9) | collective-permute-done | bytes 262176 | tf_op jit(solution)/shard_map/ppermute | solution.py:23
  58.3 1.6 collective-permute-start.11
  60.3 2.0 collective-permute-done.10
  62.8 1.6 fusion.63
  66.1 0.9 collective-permute-start.12
  66.9 3.0 %collective-permute-start.13 = (f32[4,2,32,256]{3,2,1,0:T(8,128)S(1)}, f32[4,2,32,256]{3,2,1,0:T(8,128)S(1)}, u32[]{:S(2)}, u32[]{:S(2)}) collective-permute-start(f32[4,2,32,256]{3,2,1,0:T(8,128)S(1)} %get-tuple-element.135), channel_id=1, source_target_pairs={{4,0},{8,4},{12,8},{0,12},{5,1},{9,5},{13,9},{1,13},{6,2},{10,6},{... | collective-permute-start | bytes 786440 | tf_op jit(solution)/shard_map/ppermute | solution.py:23
  70.1 6.9 %collective-permute-done.12 = f32[4,2,32,256]{3,2,1,0:T(8,128)S(1)} collective-permute-done((f32[4,2,32,256]{3,2,1,0:T(8,128)S(1)}, f32[4,2,32,256]{3,2,1,0:T(8,128)S(1)}, u32[]{:S(2)}, u32[]{:S(2)}) %collective-permute-start.12) | collective-permute-done | bytes 262176 | tf_op jit(solution)/shard_map/ppermute | solution.py:20
  77.0 4.5 %collective-permute-done.13 = f32[4,2,32,256]{3,2,1,0:T(8,128)S(1)} collective-permute-done((f32[4,2,32,256]{3,2,1,0:T(8,128)S(1)}, f32[4,2,32,256]{3,2,1,0:T(8,128)S(1)}, u32[]{:S(2)}, u32[]{:S(2)}) %collective-permute-start.13) | collective-permute-done | bytes 262176 | tf_op jit(solution)/shard_map/ppermute | solution.py:23
  81.8 1.6 collective-permute-start.15
  83.7 2.0 collective-permute-done.14
  86.3 1.6 fusion.53
  89.2 1.2 collective-permute-start.16
  90.4 2.6 %collective-permute-start.17 = (f32[4,2,32,256]{3,2,1,0:T(8,128)S(1)}, f32[4,2,32,256]{3,2,1,0:T(8,128)S(1)}, u32[]{:S(2)}, u32[]{:S(2)}) collective-permute-start(f32[4,2,32,256]{3,2,1,0:T(8,128)S(1)} %get-tuple-element.123), channel_id=1, source_target_pairs={{4,0},{8,4},{12,8},{0,12},{5,1},{9,5},{13,9},{1,13},{6,2},{10,6},{... | collective-permute-start | bytes 786440 | tf_op jit(solution)/shard_map/ppermute | solution.py:23
  93.3 6.7 %collective-permute-done.16 = f32[4,2,32,256]{3,2,1,0:T(8,128)S(1)} collective-permute-done((f32[4,2,32,256]{3,2,1,0:T(8,128)S(1)}, f32[4,2,32,256]{3,2,1,0:T(8,128)S(1)}, u32[]{:S(2)}, u32[]{:S(2)}) %collective-permute-start.16) | collective-permute-done | bytes 262176 | tf_op jit(solution)/shard_map/ppermute | solution.py:20
  100.0 5.0 %collective-permute-done.17 = f32[4,2,32,256]{3,2,1,0:T(8,128)S(1)} collective-permute-done((f32[4,2,32,256]{3,2,1,0:T(8,128)S(1)}, f32[4,2,32,256]{3,2,1,0:T(8,128)S(1)}, u32[]{:S(2)}, u32[]{:S(2)}) %collective-permute-start.17) | collective-permute-done | bytes 262176 | tf_op jit(solution)/shard_map/ppermute | solution.py:23
  105.3 1.6 collective-permute-start.19
  107.2 2.0 collective-permute-done.18
  109.8 1.6 fusion.43
  113.1 1.1 collective-permute-start.20
  114.2 2.7 %collective-permute-start.21 = (f32[4,2,32,256]{3,2,1,0:T(8,128)S(1)}, f32[4,2,32,256]{3,2,1,0:T(8,128)S(1)}, u32[]{:S(2)}, u32[]{:S(2)}) collective-permute-start(f32[4,2,32,256]{3,2,1,0:T(8,128)S(1)} %get-tuple-element.111), channel_id=1, source_target_pairs={{4,0},{8,4},{12,8},{0,12},{5,1},{9,5},{13,9},{1,13},{6,2},{10,6},{... | collective-permute-start | bytes 786440 | tf_op jit(solution)/shard_map/ppermute | solution.py:23
  117.2 6.7 %collective-permute-done.20 = f32[4,2,32,256]{3,2,1,0:T(8,128)S(1)} collective-permute-done((f32[4,2,32,256]{3,2,1,0:T(8,128)S(1)}, f32[4,2,32,256]{3,2,1,0:T(8,128)S(1)}, u32[]{:S(2)}, u32[]{:S(2)}) %collective-permute-start.20) | collective-permute-done | bytes 262176 | tf_op jit(solution)/shard_map/ppermute | solution.py:20
  123.9 5.0 %collective-permute-done.21 = f32[4,2,32,256]{3,2,1,0:T(8,128)S(1)} collective-permute-done((f32[4,2,32,256]{3,2,1,0:T(8,128)S(1)}, f32[4,2,32,256]{3,2,1,0:T(8,128)S(1)}, u32[]{:S(2)}, u32[]{:S(2)}) %collective-permute-start.21) | collective-permute-done | bytes 262176 | tf_op jit(solution)/shard_map/ppermute | solution.py:23
  129.1 1.7 collective-permute-start.23
  131.1 2.0 collective-permute-done.22
  133.7 1.6 fusion.33
  137.1 3.4 %collective-permute-start.25 = (f32[4,2,32,256]{3,2,1,0:T(8,128)S(1)}, f32[4,2,32,256]{3,2,1,0:T(8,128)S(1)}, u32[]{:S(2)}, u32[]{:S(2)}) collective-permute-start(f32[4,2,32,256]{3,2,1,0:T(8,128)S(1)} %get-tuple-element.99), channel_id=1, source_target_pairs={{4,0},{8,4},{12,8},{0,12},{5,1},{9,5},{13,9},{1,13},{6,2},{10,6},{... | collective-permute-start | bytes 786440 | tf_op jit(solution)/shard_map/ppermute | solution.py:23
  140.7 6.9 %collective-permute-done.24 = f32[4,2,32,256]{3,2,1,0:T(8,128)S(1)} collective-permute-done((f32[4,2,32,256]{3,2,1,0:T(8,128)S(1)}, f32[4,2,32,256]{3,2,1,0:T(8,128)S(1)}, u32[]{:S(2)}, u32[]{:S(2)}) %collective-permute-start.24) | collective-permute-done | bytes 262176 | tf_op jit(solution)/shard_map/ppermute | solution.py:20
  147.6 4.1 %collective-permute-done.25 = f32[4,2,32,256]{3,2,1,0:T(8,128)S(1)} collective-permute-done((f32[4,2,32,256]{3,2,1,0:T(8,128)S(1)}, f32[4,2,32,256]{3,2,1,0:T(8,128)S(1)}, u32[]{:S(2)}, u32[]{:S(2)}) %collective-permute-start.25) | collective-permute-done | bytes 262176 | tf_op jit(solution)/shard_map/ppermute | solution.py:23
  152.0 1.6 collective-permute-start.27
  153.9 2.0 collective-permute-done.26
  156.5 1.6 fusion.23
  159.8 1.2 collective-permute-start.28
  161.0 2.7 %collective-permute-start.29 = (f32[4,2,32,256]{3,2,1,0:T(8,128)S(1)}, f32[4,2,32,256]{3,2,1,0:T(8,128)S(1)}, u32[]{:S(2)}, u32[]{:S(2)}) collective-permute-start(f32[4,2,32,256]{3,2,1,0:T(8,128)S(1)} %get-tuple-element.87), channel_id=1, source_target_pairs={{4,0},{8,4},{12,8},{0,12},{5,1},{9,5},{13,9},{1,13},{6,2},{10,6},{... | collective-permute-start | bytes 786440 | tf_op jit(solution)/shard_map/ppermute | solution.py:23
  163.9 6.7 %collective-permute-done.28 = f32[4,2,32,256]{3,2,1,0:T(8,128)S(1)} collective-permute-done((f32[4,2,32,256]{3,2,1,0:T(8,128)S(1)}, f32[4,2,32,256]{3,2,1,0:T(8,128)S(1)}, u32[]{:S(2)}, u32[]{:S(2)}) %collective-permute-start.28) | collective-permute-done | bytes 262176 | tf_op jit(solution)/shard_map/ppermute | solution.py:20
  170.6 5.0 %collective-permute-done.29 = f32[4,2,32,256]{3,2,1,0:T(8,128)S(1)} collective-permute-done((f32[4,2,32,256]{3,2,1,0:T(8,128)S(1)}, f32[4,2,32,256]{3,2,1,0:T(8,128)S(1)}, u32[]{:S(2)}, u32[]{:S(2)}) %collective-permute-start.29) | collective-permute-done | bytes 262176 | tf_op jit(solution)/shard_map/ppermute | solution.py:23
  175.8 1.6 collective-permute-start.31
  177.8 2.0 collective-permute-done.30
  180.4 1.6 fusion.13
  182.0 1.0 select_bitcast_fusion
  184.1 1.5 collective-permute-start.32
  185.6 2.4 %collective-permute-start.33 = (f32[4,2,32,256]{3,2,1,0:T(8,128)S(1)}, f32[4,2,32,256]{3,2,1,0:T(8,128)S(1)}, u32[]{:S(2)}, u32[]{:S(2)}) collective-permute-start(f32[4,2,32,256]{3,2,1,0:T(8,128)S(1)} %get-tuple-element.75), channel_id=1, source_target_pairs={{4,0},{8,4},{12,8},{0,12},{5,1},{9,5},{13,9},{1,13},{6,2},{10,6},{... | collective-permute-start | bytes 786440 | tf_op jit(solution)/shard_map/ppermute | solution.py:23
  188.2 6.7 %collective-permute-done.32 = f32[4,2,32,256]{3,2,1,0:T(8,128)S(1)} collective-permute-done((f32[4,2,32,256]{3,2,1,0:T(8,128)S(1)}, f32[4,2,32,256]{3,2,1,0:T(8,128)S(1)}, u32[]{:S(2)}, u32[]{:S(2)}) %collective-permute-start.32) | collective-permute-done | bytes 262176 | tf_op jit(solution)/shard_map/ppermute | solution.py:20
  194.9 5.4 %collective-permute-done.33 = f32[4,2,32,256]{3,2,1,0:T(8,128)S(1)} collective-permute-done((f32[4,2,32,256]{3,2,1,0:T(8,128)S(1)}, f32[4,2,32,256]{3,2,1,0:T(8,128)S(1)}, u32[]{:S(2)}, u32[]{:S(2)}) %collective-permute-start.33) | collective-permute-done | bytes 262176 | tf_op jit(solution)/shard_map/ppermute | solution.py:23
  200.5 1.7 collective-permute-start.35
  202.5 2.0 collective-permute-done.34
  205.1 1.6 fusion.3
  206.7 0.9 fusion.123
  (116 shorter events, 25.2 us)
Async XLA Ops:
  0.6 8.2 %copy-start.1 = (f32[8,32,256]{2,1,0:T(8,128)S(1)}, f32[8,32,256]{2,1,0:T(8,128)}, u32[]{:S(2)}) copy-start(f32[8,32,256]{2,1,0:T(8,128)} %param.3) | copy-start | bytes 786436
  0.6 8.2 %copy-start = (f32[8,32,256]{2,1,0:T(8,128)S(1)}, f32[8,32,256]{2,1,0:T(8,128)}, u32[]{:S(2)}) copy-start(f32[8,32,256]{2,1,0:T(8,128)} %param.4) | copy-start | bytes 786436
  2.3 9.7 %collective-permute-start = (f32[2,2,32,256]{3,2,1,0:T(8,128)}, f32[2,2,32,256]{3,2,1,0:T(8,128)S(1)}, u32[]{:S(2)}, u32[]{:S(2)}) collective-permute-start(f32[2,2,32,256]{3,2,1,0:T(8,128)} %get-tuple-element.176), channel_id=1, source_target_pairs={{0,4},{4,8},{8,12},{12,0},{1,5},{5,9},{9,13},{13,1},{2,6},{6,10},{... | collective-permute-start | bytes 393224 | tf_op jit(solution)/shard_map/ppermute | solution.py:20
  5.4 7.8 %collective-permute-start.1 = (f32[2,2,32,256]{3,2,1,0:T(8,128)S(1)}, f32[2,2,32,256]{3,2,1,0:T(8,128)S(1)}, u32[]{:S(2)}, u32[]{:S(2)}) collective-permute-start(f32[2,2,32,256]{3,2,1,0:T(8,128)S(1)} %get-tuple-element.177), channel_id=1, source_target_pairs={{4,0},{8,4},{12,8},{0,12},{5,1},{9,5},{13,9},{1,13},{6,2},{10,6},{... | collective-permute-start | bytes 393224 | tf_op jit(solution)/shard_map/ppermute | solution.py:23
  13.2 3.6 %collective-permute-start.2 = (f32[2,12,2,256]{3,2,1,0:T(2,128)S(1)}, f32[2,12,2,256]{3,2,1,0:T(2,128)S(1)}, u32[]{:S(2)}, u32[]{:S(2)}) collective-permute-start(f32[2,12,2,256]{3,2,1,0:T(2,128)S(1)} %get-tuple-element.162), channel_id=1, source_target_pairs={{0,1},{1,2},{2,3},{3,0},{4,5},{5,6},{6,7},{7,4},{8,9},{9,10},{10,1... | collective-permute-start | bytes 147464 | tf_op jit(solution)/shard_map/ppermute | solution.py:20
  13.2 3.5 %collective-permute-start.3 = (f32[2,12,2,256]{3,2,1,0:T(2,128)S(1)}, f32[2,12,2,256]{3,2,1,0:T(2,128)S(1)}, u32[]{:S(2)}, u32[]{:S(2)}) collective-permute-start(f32[2,12,2,256]{3,2,1,0:T(2,128)S(1)} %get-tuple-element.163), channel_id=1, source_target_pairs={{1,0},{2,1},{3,2},{0,3},{5,4},{6,5},{7,6},{4,7},{9,8},{10,9},{11,1... | collective-permute-start | bytes 147464 | tf_op jit(solution)/shard_map/ppermute | solution.py:23
  16.9 1.0 copy-start.2
  19.1 10.5 %collective-permute-start.4 = (f32[4,2,32,256]{3,2,1,0:T(8,128)S(1)}, f32[4,2,32,256]{3,2,1,0:T(8,128)S(1)}, u32[]{:S(2)}, u32[]{:S(2)}) collective-permute-start(f32[4,2,32,256]{3,2,1,0:T(8,128)S(1)} %get-tuple-element.158), channel_id=1, source_target_pairs={{0,4},{4,8},{8,12},{12,0},{1,5},{5,9},{9,13},{13,1},{2,6},{6,10},{... | collective-permute-start | bytes 786440 | tf_op jit(solution)/shard_map/ppermute | solution.py:20
  20.5 14.4 %collective-permute-start.5 = (f32[4,2,32,256]{3,2,1,0:T(8,128)S(1)}, f32[4,2,32,256]{3,2,1,0:T(8,128)S(1)}, u32[]{:S(2)}, u32[]{:S(2)}) collective-permute-start(f32[4,2,32,256]{3,2,1,0:T(8,128)S(1)} %get-tuple-element.159), channel_id=1, source_target_pairs={{4,0},{8,4},{12,8},{0,12},{5,1},{9,5},{13,9},{1,13},{6,2},{10,6},{... | collective-permute-start | bytes 786440 | tf_op jit(solution)/shard_map/ppermute | solution.py:23
  35.0 4.1 %collective-permute-start.6 = (f32[4,12,2,256]{3,2,1,0:T(2,128)S(1)}, f32[4,12,2,256]{3,2,1,0:T(2,128)S(1)}, u32[]{:S(2)}, u32[]{:S(2)}) collective-permute-start(f32[4,12,2,256]{3,2,1,0:T(2,128)S(1)} %get-tuple-element.56), channel_id=1, source_target_pairs={{0,1},{1,2},{2,3},{3,0},{4,5},{5,6},{6,7},{7,4},{8,9},{9,10},{10,1... | collective-permute-start | bytes 294920 | tf_op jit(solution)/shard_map/ppermute | solution.py:20
  35.2 3.8 %collective-permute-start.7 = (f32[4,12,2,256]{3,2,1,0:T(2,128)S(1)}, f32[4,12,2,256]{3,2,1,0:T(2,128)S(1)}, u32[]{:S(2)}, u32[]{:S(2)}) collective-permute-start(f32[4,12,2,256]{3,2,1,0:T(2,128)S(1)} %get-tuple-element.57), channel_id=1, source_target_pairs={{1,0},{2,1},{3,2},{0,3},{5,4},{6,5},{7,6},{4,7},{9,8},{10,9},{11,1... | collective-permute-start | bytes 294920 | tf_op jit(solution)/shard_map/ppermute | solution.py:23
  42.6 10.7 %collective-permute-start.8 = (f32[4,2,32,256]{3,2,1,0:T(8,128)S(1)}, f32[4,2,32,256]{3,2,1,0:T(8,128)S(1)}, u32[]{:S(2)}, u32[]{:S(2)}) collective-permute-start(f32[4,2,32,256]{3,2,1,0:T(8,128)S(1)} %get-tuple-element.146), channel_id=1, source_target_pairs={{0,4},{4,8},{8,12},{12,0},{1,5},{5,9},{9,13},{13,1},{2,6},{6,10},{... | collective-permute-start | bytes 786440 | tf_op jit(solution)/shard_map/ppermute | solution.py:20
  43.4 14.7 %collective-permute-start.9 = (f32[4,2,32,256]{3,2,1,0:T(8,128)S(1)}, f32[4,2,32,256]{3,2,1,0:T(8,128)S(1)}, u32[]{:S(2)}, u32[]{:S(2)}) collective-permute-start(f32[4,2,32,256]{3,2,1,0:T(8,128)S(1)} %get-tuple-element.147), channel_id=1, source_target_pairs={{4,0},{8,4},{12,8},{0,12},{5,1},{9,5},{13,9},{1,13},{6,2},{10,6},{... | collective-permute-start | bytes 786440 | tf_op jit(solution)/shard_map/ppermute | solution.py:23
  58.1 4.1 %collective-permute-start.10 = (f32[4,12,2,256]{3,2,1,0:T(2,128)S(1)}, f32[4,12,2,256]{3,2,1,0:T(2,128)S(1)}, u32[]{:S(2)}, u32[]{:S(2)}) collective-permute-start(f32[4,12,2,256]{3,2,1,0:T(2,128)S(1)} %get-tuple-element.52), channel_id=1, source_target_pairs={{0,1},{1,2},{2,3},{3,0},{4,5},{5,6},{6,7},{7,4},{8,9},{9,10},{10,1... | collective-permute-start | bytes 294920 | tf_op jit(solution)/shard_map/ppermute | solution.py:20
  58.3 3.9 %collective-permute-start.11 = (f32[4,12,2,256]{3,2,1,0:T(2,128)S(1)}, f32[4,12,2,256]{3,2,1,0:T(2,128)S(1)}, u32[]{:S(2)}, u32[]{:S(2)}) collective-permute-start(f32[4,12,2,256]{3,2,1,0:T(2,128)S(1)} %get-tuple-element.53), channel_id=1, source_target_pairs={{1,0},{2,1},{3,2},{0,3},{5,4},{6,5},{7,6},{4,7},{9,8},{10,9},{11,1... | collective-permute-start | bytes 294920 | tf_op jit(solution)/shard_map/ppermute | solution.py:23
  66.1 11.0 %collective-permute-start.12 = (f32[4,2,32,256]{3,2,1,0:T(8,128)S(1)}, f32[4,2,32,256]{3,2,1,0:T(8,128)S(1)}, u32[]{:S(2)}, u32[]{:S(2)}) collective-permute-start(f32[4,2,32,256]{3,2,1,0:T(8,128)S(1)} %get-tuple-element.134), channel_id=1, source_target_pairs={{0,4},{4,8},{8,12},{12,0},{1,5},{5,9},{9,13},{13,1},{2,6},{6,10},{... | collective-permute-start | bytes 786440 | tf_op jit(solution)/shard_map/ppermute | solution.py:20
  66.9 14.6 %collective-permute-start.13 = (f32[4,2,32,256]{3,2,1,0:T(8,128)S(1)}, f32[4,2,32,256]{3,2,1,0:T(8,128)S(1)}, u32[]{:S(2)}, u32[]{:S(2)}) collective-permute-start(f32[4,2,32,256]{3,2,1,0:T(8,128)S(1)} %get-tuple-element.135), channel_id=1, source_target_pairs={{4,0},{8,4},{12,8},{0,12},{5,1},{9,5},{13,9},{1,13},{6,2},{10,6},{... | collective-permute-start | bytes 786440 | tf_op jit(solution)/shard_map/ppermute | solution.py:23
  81.6 4.1 %collective-permute-start.14 = (f32[4,12,2,256]{3,2,1,0:T(2,128)S(1)}, f32[4,12,2,256]{3,2,1,0:T(2,128)S(1)}, u32[]{:S(2)}, u32[]{:S(2)}) collective-permute-start(f32[4,12,2,256]{3,2,1,0:T(2,128)S(1)} %get-tuple-element.48), channel_id=1, source_target_pairs={{0,1},{1,2},{2,3},{3,0},{4,5},{5,6},{6,7},{7,4},{8,9},{9,10},{10,1... | collective-permute-start | bytes 294920 | tf_op jit(solution)/shard_map/ppermute | solution.py:20
  81.8 3.9 %collective-permute-start.15 = (f32[4,12,2,256]{3,2,1,0:T(2,128)S(1)}, f32[4,12,2,256]{3,2,1,0:T(2,128)S(1)}, u32[]{:S(2)}, u32[]{:S(2)}) collective-permute-start(f32[4,12,2,256]{3,2,1,0:T(2,128)S(1)} %get-tuple-element.49), channel_id=1, source_target_pairs={{1,0},{2,1},{3,2},{0,3},{5,4},{6,5},{7,6},{4,7},{9,8},{10,9},{11,1... | collective-permute-start | bytes 294920 | tf_op jit(solution)/shard_map/ppermute | solution.py:23
  89.2 10.8 %collective-permute-start.16 = (f32[4,2,32,256]{3,2,1,0:T(8,128)S(1)}, f32[4,2,32,256]{3,2,1,0:T(8,128)S(1)}, u32[]{:S(2)}, u32[]{:S(2)}) collective-permute-start(f32[4,2,32,256]{3,2,1,0:T(8,128)S(1)} %get-tuple-element.122), channel_id=1, source_target_pairs={{0,4},{4,8},{8,12},{12,0},{1,5},{5,9},{9,13},{13,1},{2,6},{6,10},{... | collective-permute-start | bytes 786440 | tf_op jit(solution)/shard_map/ppermute | solution.py:20
  90.4 14.6 %collective-permute-start.17 = (f32[4,2,32,256]{3,2,1,0:T(8,128)S(1)}, f32[4,2,32,256]{3,2,1,0:T(8,128)S(1)}, u32[]{:S(2)}, u32[]{:S(2)}) collective-permute-start(f32[4,2,32,256]{3,2,1,0:T(8,128)S(1)} %get-tuple-element.123), channel_id=1, source_target_pairs={{4,0},{8,4},{12,8},{0,12},{5,1},{9,5},{13,9},{1,13},{6,2},{10,6},{... | collective-permute-start | bytes 786440 | tf_op jit(solution)/shard_map/ppermute | solution.py:23
  105.1 4.1 %collective-permute-start.18 = (f32[4,12,2,256]{3,2,1,0:T(2,128)S(1)}, f32[4,12,2,256]{3,2,1,0:T(2,128)S(1)}, u32[]{:S(2)}, u32[]{:S(2)}) collective-permute-start(f32[4,12,2,256]{3,2,1,0:T(2,128)S(1)} %get-tuple-element.44), channel_id=1, source_target_pairs={{0,1},{1,2},{2,3},{3,0},{4,5},{5,6},{6,7},{7,4},{8,9},{9,10},{10,1... | collective-permute-start | bytes 294920 | tf_op jit(solution)/shard_map/ppermute | solution.py:20
  105.3 3.9 %collective-permute-start.19 = (f32[4,12,2,256]{3,2,1,0:T(2,128)S(1)}, f32[4,12,2,256]{3,2,1,0:T(2,128)S(1)}, u32[]{:S(2)}, u32[]{:S(2)}) collective-permute-start(f32[4,12,2,256]{3,2,1,0:T(2,128)S(1)} %get-tuple-element.45), channel_id=1, source_target_pairs={{1,0},{2,1},{3,2},{0,3},{5,4},{6,5},{7,6},{4,7},{9,8},{10,9},{11,1... | collective-permute-start | bytes 294920 | tf_op jit(solution)/shard_map/ppermute | solution.py:23
  113.1 10.8 %collective-permute-start.20 = (f32[4,2,32,256]{3,2,1,0:T(8,128)S(1)}, f32[4,2,32,256]{3,2,1,0:T(8,128)S(1)}, u32[]{:S(2)}, u32[]{:S(2)}) collective-permute-start(f32[4,2,32,256]{3,2,1,0:T(8,128)S(1)} %get-tuple-element.110), channel_id=1, source_target_pairs={{0,4},{4,8},{8,12},{12,0},{1,5},{5,9},{9,13},{13,1},{2,6},{6,10},{... | collective-permute-start | bytes 786440 | tf_op jit(solution)/shard_map/ppermute | solution.py:20
  114.2 14.7 %collective-permute-start.21 = (f32[4,2,32,256]{3,2,1,0:T(8,128)S(1)}, f32[4,2,32,256]{3,2,1,0:T(8,128)S(1)}, u32[]{:S(2)}, u32[]{:S(2)}) collective-permute-start(f32[4,2,32,256]{3,2,1,0:T(8,128)S(1)} %get-tuple-element.111), channel_id=1, source_target_pairs={{4,0},{8,4},{12,8},{0,12},{5,1},{9,5},{13,9},{1,13},{6,2},{10,6},{... | collective-permute-start | bytes 786440 | tf_op jit(solution)/shard_map/ppermute | solution.py:23
  129.0 4.1 %collective-permute-start.22 = (f32[4,12,2,256]{3,2,1,0:T(2,128)S(1)}, f32[4,12,2,256]{3,2,1,0:T(2,128)S(1)}, u32[]{:S(2)}, u32[]{:S(2)}) collective-permute-start(f32[4,12,2,256]{3,2,1,0:T(2,128)S(1)} %get-tuple-element.40), channel_id=1, source_target_pairs={{0,1},{1,2},{2,3},{3,0},{4,5},{5,6},{6,7},{7,4},{8,9},{9,10},{10,1... | collective-permute-start | bytes 294920 | tf_op jit(solution)/shard_map/ppermute | solution.py:20
  129.1 4.0 %collective-permute-start.23 = (f32[4,12,2,256]{3,2,1,0:T(2,128)S(1)}, f32[4,12,2,256]{3,2,1,0:T(2,128)S(1)}, u32[]{:S(2)}, u32[]{:S(2)}) collective-permute-start(f32[4,12,2,256]{3,2,1,0:T(2,128)S(1)} %get-tuple-element.41), channel_id=1, source_target_pairs={{1,0},{2,1},{3,2},{0,3},{5,4},{6,5},{7,6},{4,7},{9,8},{10,9},{11,1... | collective-permute-start | bytes 294920 | tf_op jit(solution)/shard_map/ppermute | solution.py:23
  136.6 11.0 %collective-permute-start.24 = (f32[4,2,32,256]{3,2,1,0:T(8,128)S(1)}, f32[4,2,32,256]{3,2,1,0:T(8,128)S(1)}, u32[]{:S(2)}, u32[]{:S(2)}) collective-permute-start(f32[4,2,32,256]{3,2,1,0:T(8,128)S(1)} %get-tuple-element.98), channel_id=1, source_target_pairs={{0,4},{4,8},{8,12},{12,0},{1,5},{5,9},{9,13},{13,1},{2,6},{6,10},{... | collective-permute-start | bytes 786440 | tf_op jit(solution)/shard_map/ppermute | solution.py:20
  137.1 14.6 %collective-permute-start.25 = (f32[4,2,32,256]{3,2,1,0:T(8,128)S(1)}, f32[4,2,32,256]{3,2,1,0:T(8,128)S(1)}, u32[]{:S(2)}, u32[]{:S(2)}) collective-permute-start(f32[4,2,32,256]{3,2,1,0:T(8,128)S(1)} %get-tuple-element.99), channel_id=1, source_target_pairs={{4,0},{8,4},{12,8},{0,12},{5,1},{9,5},{13,9},{1,13},{6,2},{10,6},{... | collective-permute-start | bytes 786440 | tf_op jit(solution)/shard_map/ppermute | solution.py:23
  151.8 4.1 %collective-permute-start.26 = (f32[4,12,2,256]{3,2,1,0:T(2,128)S(1)}, f32[4,12,2,256]{3,2,1,0:T(2,128)S(1)}, u32[]{:S(2)}, u32[]{:S(2)}) collective-permute-start(f32[4,12,2,256]{3,2,1,0:T(2,128)S(1)} %get-tuple-element.36), channel_id=1, source_target_pairs={{0,1},{1,2},{2,3},{3,0},{4,5},{5,6},{6,7},{7,4},{8,9},{9,10},{10,1... | collective-permute-start | bytes 294920 | tf_op jit(solution)/shard_map/ppermute | solution.py:20
  152.0 3.9 %collective-permute-start.27 = (f32[4,12,2,256]{3,2,1,0:T(2,128)S(1)}, f32[4,12,2,256]{3,2,1,0:T(2,128)S(1)}, u32[]{:S(2)}, u32[]{:S(2)}) collective-permute-start(f32[4,12,2,256]{3,2,1,0:T(2,128)S(1)} %get-tuple-element.37), channel_id=1, source_target_pairs={{1,0},{2,1},{3,2},{0,3},{5,4},{6,5},{7,6},{4,7},{9,8},{10,9},{11,1... | collective-permute-start | bytes 294920 | tf_op jit(solution)/shard_map/ppermute | solution.py:23
  159.8 10.8 %collective-permute-start.28 = (f32[4,2,32,256]{3,2,1,0:T(8,128)S(1)}, f32[4,2,32,256]{3,2,1,0:T(8,128)S(1)}, u32[]{:S(2)}, u32[]{:S(2)}) collective-permute-start(f32[4,2,32,256]{3,2,1,0:T(8,128)S(1)} %get-tuple-element.86), channel_id=1, source_target_pairs={{0,4},{4,8},{8,12},{12,0},{1,5},{5,9},{9,13},{13,1},{2,6},{6,10},{... | collective-permute-start | bytes 786440 | tf_op jit(solution)/shard_map/ppermute | solution.py:20
  161.0 14.6 %collective-permute-start.29 = (f32[4,2,32,256]{3,2,1,0:T(8,128)S(1)}, f32[4,2,32,256]{3,2,1,0:T(8,128)S(1)}, u32[]{:S(2)}, u32[]{:S(2)}) collective-permute-start(f32[4,2,32,256]{3,2,1,0:T(8,128)S(1)} %get-tuple-element.87), channel_id=1, source_target_pairs={{4,0},{8,4},{12,8},{0,12},{5,1},{9,5},{13,9},{1,13},{6,2},{10,6},{... | collective-permute-start | bytes 786440 | tf_op jit(solution)/shard_map/ppermute | solution.py:23
  175.7 4.1 %collective-permute-start.30 = (f32[4,12,2,256]{3,2,1,0:T(2,128)S(1)}, f32[4,12,2,256]{3,2,1,0:T(2,128)S(1)}, u32[]{:S(2)}, u32[]{:S(2)}) collective-permute-start(f32[4,12,2,256]{3,2,1,0:T(2,128)S(1)} %get-tuple-element.32), channel_id=1, source_target_pairs={{0,1},{1,2},{2,3},{3,0},{4,5},{5,6},{6,7},{7,4},{8,9},{9,10},{10,1... | collective-permute-start | bytes 294920 | tf_op jit(solution)/shard_map/ppermute | solution.py:20
  175.8 3.9 %collective-permute-start.31 = (f32[4,12,2,256]{3,2,1,0:T(2,128)S(1)}, f32[4,12,2,256]{3,2,1,0:T(2,128)S(1)}, u32[]{:S(2)}, u32[]{:S(2)}) collective-permute-start(f32[4,12,2,256]{3,2,1,0:T(2,128)S(1)} %get-tuple-element.33), channel_id=1, source_target_pairs={{1,0},{2,1},{3,2},{0,3},{5,4},{6,5},{7,6},{4,7},{9,8},{10,9},{11,1... | collective-permute-start | bytes 294920 | tf_op jit(solution)/shard_map/ppermute | solution.py:23
  184.1 10.8 %collective-permute-start.32 = (f32[4,2,32,256]{3,2,1,0:T(8,128)S(1)}, f32[4,2,32,256]{3,2,1,0:T(8,128)S(1)}, u32[]{:S(2)}, u32[]{:S(2)}) collective-permute-start(f32[4,2,32,256]{3,2,1,0:T(8,128)S(1)} %get-tuple-element.74), channel_id=1, source_target_pairs={{0,4},{4,8},{8,12},{12,0},{1,5},{5,9},{9,13},{13,1},{2,6},{6,10},{... | collective-permute-start | bytes 786440 | tf_op jit(solution)/shard_map/ppermute | solution.py:20
  185.6 14.7 %collective-permute-start.33 = (f32[4,2,32,256]{3,2,1,0:T(8,128)S(1)}, f32[4,2,32,256]{3,2,1,0:T(8,128)S(1)}, u32[]{:S(2)}, u32[]{:S(2)}) collective-permute-start(f32[4,2,32,256]{3,2,1,0:T(8,128)S(1)} %get-tuple-element.75), channel_id=1, source_target_pairs={{4,0},{8,4},{12,8},{0,12},{5,1},{9,5},{13,9},{1,13},{6,2},{10,6},{... | collective-permute-start | bytes 786440 | tf_op jit(solution)/shard_map/ppermute | solution.py:23
  200.4 4.1 %collective-permute-start.34 = (f32[4,12,2,256]{3,2,1,0:T(2,128)S(1)}, f32[4,12,2,256]{3,2,1,0:T(2,128)S(1)}, u32[]{:S(2)}, u32[]{:S(2)}) collective-permute-start(f32[4,12,2,256]{3,2,1,0:T(2,128)S(1)} %get-tuple-element.28), channel_id=1, source_target_pairs={{0,1},{1,2},{2,3},{3,0},{4,5},{5,6},{6,7},{7,4},{8,9},{9,10},{10,1... | collective-permute-start | bytes 294920 | tf_op jit(solution)/shard_map/ppermute | solution.py:20
  200.5 4.0 %collective-permute-start.35 = (f32[4,12,2,256]{3,2,1,0:T(2,128)S(1)}, f32[4,12,2,256]{3,2,1,0:T(2,128)S(1)}, u32[]{:S(2)}, u32[]{:S(2)}) collective-permute-start(f32[4,12,2,256]{3,2,1,0:T(2,128)S(1)} %get-tuple-element.29), channel_id=1, source_target_pairs={{1,0},{2,1},{3,2},{0,3},{5,4},{6,5},{7,6},{4,7},{9,8},{10,9},{11,1... | collective-permute-start | bytes 294920 | tf_op jit(solution)/shard_map/ppermute | solution.py:23
where the time goes:
time: 208 us
  waiting for transfers between devices  114 us (55%)
  starting transfers between devices  52.3 us (25%)
  other arithmetic  30.3 us (15%)
  local copies, waits for them, and re-layouts  9.76 us (5%)
    ppermute x18, waiting for transfers between devices, with_halo(): lax.ppermute(lax.slice_in_dim(block, block.shape[dim] - width, None, axis...  73.6 us
    ppermute x18, waiting for transfers between devices, with_halo(): lax.ppermute(lax.slice_in_dim(block, 0, width, axis=dim), axis, backward)  40.3 us
    ppermute x18, starting transfers between devices, with_halo(): lax.ppermute(lax.slice_in_dim(block, 0, width, axis=dim), axis, backward)  39.2 us
    sub x9, other arithmetic, stencil(): total = total + 4.0 / 3.0 * near_z - far_z / 12.0  13.2 us
    ppermute x18, starting transfers between devices, with_halo(): lax.ppermute(lax.slice_in_dim(block, block.shape[dim] - width, None, axis...  13 us
    concatenate x18, other arithmetic, with_halo(): block = jnp.concatenate([low, block, high], axis=dim)  7.69 us
    slice x16, local copies, waits for them, and re-layouts, stencil(): far_z = jnp.roll(centre, 2, 3) + jnp.roll(centre, -2, 3)  4.59 us
    slice x16, local copies, waits for them, and re-layouts, stencil(): near_z = jnp.roll(centre, 1, 3) + jnp.roll(centre, -1, 3)  4.58 us
  transfers between devices with their start and end apart: 36, of which 27 were waited for; matrix products, arithmetic and copies ran while one was open for 3% of the time, Pallas kernels for 0%

commit v1 on v0

v1 whole, which is shorter than its diff:
```python
import functools

import jax
import jax.numpy as jnp
from jax import lax
from jax.experimental import pallas as pl
from jax.experimental.pallas import tpu as pltpu
from jax.sharding import PartitionSpec as P

STEPS = 8

time_step = 0.12
damping = 0.05
second = 0.5 * STEPS * time_step * time_step

NEAR = 4.0 / 3.0
FAR = -1.0 / 12.0

VMEM = pl.BlockSpec(memory_space=pltpu.VMEM)


def call(kernel, outs, args, flops):
    moved = 4 * (sum(a.size for a in args) + sum(o.size for o in outs))
    return pl.pallas_call(
        kernel,
        out_shape=outs,
        in_specs=[VMEM] * len(args),
        out_specs=[VMEM] * len(outs),
        compiler_params=pltpu.CompilerParams(vmem_limit_bytes=6 << 20),
        cost_estimate=pl.CostEstimate(flops=flops, bytes_accessed=moved, transcendentals=0),
    )(*args)


def spec(*shape):
    return jax.ShapeDtypeStruct(shape, jnp.float32)


def edge_specs(planes, rows, depth, count):
    pair = [spec(count * 2, rows, depth)] * 2 + [spec(count * planes, 2, depth)] * 2
    return pair


def local_lap(w_ref, out_ref):
    planes, rows, depth = w_ref.shape
    row = lax.broadcasted_iota(jnp.int32, (rows, depth), 0)
    for i in range(planes):
        w = w_ref[i]
        near = pltpu.roll(w, 1, 1) + pltpu.roll(w, depth - 1, 1)
        far = pltpu.roll(w, 2, 1) + pltpu.roll(w, depth - 2, 1)
        near += jnp.where(row >= 1, pltpu.roll(w, 1, 0), 0.0)
        near += jnp.where(row < rows - 1, pltpu.roll(w, rows - 1, 0), 0.0)
        far += jnp.where(row >= 2, pltpu.roll(w, 2, 0), 0.0)
        far += jnp.where(row < rows - 2, pltpu.roll(w, rows - 2, 0), 0.0)
        for shift in (-1, 1):
            if 0 <= i + shift < planes:
                near += w_ref[i + shift]
            if 0 <= i + 2 * shift < planes:
                far += w_ref[i + 2 * shift]
        out_ref[i] = -7.5 * w + NEAR * near + FAR * far


def edges(w_ref, x_up, x_down, y_up, y_down, part=0):
    planes, rows, _ = w_ref.shape
    a = 2 * part
    x_up[a] = NEAR * w_ref[planes - 1] + FAR * w_ref[planes - 2]
    x_up[a + 1] = FAR * w_ref[planes - 1]
    x_down[a] = FAR * w_ref[0]
    x_down[a + 1] = NEAR * w_ref[0] + FAR * w_ref[1]
    b = pl.ds(part * planes, planes)
    last, second_last = w_ref[:, rows - 1 :, :], w_ref[:, rows - 2 : rows - 1, :]
    y_up[b, 0:1, :] = NEAR * last + FAR * second_last
    y_up[b, 1:2, :] = FAR * last
    first, following = w_ref[:, 0:1, :], w_ref[:, 1:2, :]
    y_down[b, 0:1, :] = FAR * first
    y_down[b, 1:2, :] = NEAR * first + FAR * following


def finish_lap(lap_ref, x_low, x_high, y_low, y_high, part=0):
    planes, rows, _ = lap_ref.shape
    a, b = pl.ds(2 * part, 2), pl.ds(part * planes, planes)
    lap_ref[0:2] += x_low[a]
    lap_ref[planes - 2 :] += x_high[a]
    lap_ref[:, 0:2, :] += y_low[b]
    lap_ref[:, rows - 2 :, :] += y_high[b]


def first_edges(u, v, *outs):
    edges(u, *outs, part=0)
    edges(v, *outs, part=1)


def first_local(u, v, lap_u, lap_v):
    local_lap(u, lap_u)
    local_lap(v, lap_v)


def first_finish(lap_u, lap_v, v, s, xl, xh, yl, yh, q, lap, new_v, *outs):
    q[...] = lap_u[...]
    lap[...] = lap_v[...]
    finish_lap(q, xl, xh, yl, yh, part=0)
    finish_lap(lap, xl, xh, yl, yh, part=1)
    new_v[...] = v[...] + time_step * (s[...] * q[...] + damping * lap[...])
    edges(new_v, *outs)


def middle_local(new_v, u, v, q, lap, part, new_u, new_q):
    local_lap(new_v, part)
    new_u[...] = u[...] + time_step * v[...]
    new_q[...] = q[...] + time_step * lap[...]


def middle_finish(part, v, q, s, xl, xh, yl, yh, lap, new_v, *outs):
    lap[...] = part[...]
    finish_lap(lap, xl, xh, yl, yh)
    new_v[...] = v[...] + time_step * (s[...] * q[...] + damping * lap[...])
    edges(new_v, *outs)


def rate_finish(part, q, s, xl, xh, yl, yh, lap, rate, *outs):
    lap[...] = part[...]
    finish_lap(lap, xl, xh, yl, yh)
    rate[...] = s[...] * q[...] + damping * lap[...]
    edges(rate, *outs)


def last_local(scale, u, v, s, lap, rate, part, out_u, base_v):
    local_lap(rate, part)
    r = rate[...]
    out_u[...] = u[...] + time_step * v[...] + scale[0] * r
    base_v[...] = v[...] + time_step * r + scale[0] * (s[...] * lap[...])


def last_finish(scale, part, base_v, xl, xh, yl, yh, out_v):
    out_v[...] = part[...]
    finish_lap(out_v, xl, xh, yl, yh)
    out_v[...] = base_v[...] + (scale[0] * damping) * out_v[...]


def call_scaled(kernel, scale, outs, args, flops):
    moved = 4 * (sum(a.size for a in args) + sum(o.size for o in outs))
    return pl.pallas_call(
        kernel,
        out_shape=outs,
        in_specs=[pl.BlockSpec(memory_space=pltpu.SMEM)] + [VMEM] * len(args),
        out_specs=[VMEM] * len(outs),
        compiler_params=pltpu.CompilerParams(vmem_limit_bytes=6 << 20),
        cost_estimate=pl.CostEstimate(flops=flops, bytes_accessed=moved, transcendentals=0),
    )(scale, *args)


def exchange(x_up, x_down, y_up, y_down):
    def ring(axis, step):
        n = lax.axis_size(axis)
        return [(i, (i + step) % n) for i in range(n)]

    x_low = lax.ppermute(x_up, "gx", ring("gx", 1))
    x_high = lax.ppermute(x_down, "gx", ring("gx", -1))
    y_low = lax.ppermute(y_up, "gy", ring("gy", 1))
    y_high = lax.ppermute(y_down, "gy", ring("gy", -1))
    return x_low, x_high, y_low, y_high


def body(u, v, s):
    planes, rows, depth = u.shape
    block = spec(planes, rows, depth)
    work = 40 * u.size
    one = edge_specs(planes, rows, depth, 1)
    two = edge_specs(planes, rows, depth, 2)
    scale = jnp.where(lax.axis_index("level") == 0, 0.0, second).astype(jnp.float32).reshape(1)

    got = exchange(*call(first_edges, two, (u, v), u.size))
    lap_u, lap_v = call(first_local, [block] * 2, (u, v), 2 * work)
    q, lap, new_v, *sent = call(first_finish, [block] * 3 + one, (lap_u, lap_v, v, s, *got), work)
    for moment in range(1, STEPS):
        got = exchange(*sent)
        part, u, q = call(middle_local, [block] * 3, (new_v, u, v, q, lap), work)
        v = new_v
        if moment < STEPS - 1:
            lap, new_v, *sent = call(middle_finish, [block] * 2 + one, (part, v, q, s, *got), work)
        else:
            lap, rate, *sent = call(rate_finish, [block] * 2 + one, (part, q, s, *got), work)
    got = exchange(*sent)
    part, out_u, base_v = call_scaled(last_local, scale, [block] * 3, (u, v, s, lap, rate), work)
    (out_v,) = call_scaled(last_finish, scale, [block], (part, base_v, *got), work)
    return out_u[None], out_v[None]


def solution(mesh):
    placed = (P("gx", "gy", None),) * 3
    return jax.shard_map(
        body,
        mesh=mesh,
        in_specs=placed,
        out_specs=(P("level", "gx", "gy", None), P("level", "gx", "gy", None)),
        check_vma=False,
    )
```

time: 208 us -> 73.4 us (0.35)
  waiting for transfers between devices: 114 us -> 11.1 us
  other arithmetic: 30.3 us -> 0 us
  local copies, waits for them, and re-layouts: 9.76 us -> 1.9 us
  Pallas kernels: 0 us -> 6.47 us
    ppermute x36, waiting for transfers between devices: 114 us -> 11.1 us  [the longest x9 8.45 us: exchange(): y_low = lax.ppermute(y_up, 'gy', ring('gy', 1))]
    sub x9 -> x0, other arithmetic: 13.2 us -> none  [stencil(): total = total + 4.0 / 3.0 * near_z - far_z / 12.0]
    slice x40 -> x0, local copies, waits for them, and re-layouts: 9.47 us -> none  [the longest x16 4.59 us: stencil(): far_z = jnp.roll(centre, 2, 3) + jnp.roll(centre, -2, 3)]
    concatenate x18 -> x0, other arithmetic: 7.69 us -> none  [with_halo(): block = jnp.concatenate([low, block, high], axis=dim)]
    pallas_call x0 -> x19, Pallas kernels: none -> 6.47 us  [the longest x17 4.59 us: call(): pl.pallas_call(kernel, out_shape=outs, in_specs=[VMEM] * len(args), out_s...]
    another operation x21 -> x0, other arithmetic: 6.12 us -> none  [the longest x5 3.55 us: body(): laplace = stencil(neighbours(jnp.stack([u_init, v_init])))]
  transfers between devices with their start and end apart: 36 -> 36, of which waited for: 27 -> 12; matrix products, arithmetic and copies ran while one was open for 3% -> 0% of each run, Pallas kernels for 0% -> 6%
where the time goes in v1:
time: 73.4 us; the launch traced here: 72.2 us
  starting transfers between devices  51.9 us (71%)
  waiting for transfers between devices  11.1 us (15%)
  Pallas kernels  6.47 us (9%)
  local copies, waits for them, and re-layouts  1.9 us (3%)
  between operations  0.79 us (1%)
    ppermute x9, starting transfers between devices, exchange(): x_high = lax.ppermute(x_down, 'gx', ring('gx', -1))  26.3 us
    ppermute x9, starting transfers between devices, exchange(): x_low = lax.ppermute(x_up, 'gx', ring('gx', 1))  9.93 us
    ppermute x9, starting transfers between devices, exchange(): y_high = lax.ppermute(y_down, 'gy', ring('gy', -1))  8.58 us
    ppermute x9, waiting for transfers between devices, exchange(): y_low = lax.ppermute(y_up, 'gy', ring('gy', 1))  8.45 us
    ppermute x9, starting transfers between devices, exchange(): y_low = lax.ppermute(y_up, 'gy', ring('gy', 1))  7.13 us
    pallas_call x17, Pallas kernels, call(): pl.pallas_call(kernel, out_shape=outs, in_specs=[VMEM] * len(args), out_s...  4.59 us
    unnamed x8, local copies, waits for them, and re-layouts  1.9 us
    pallas_call x2, Pallas kernels, call_scaled(): pl.pallas_call(kernel, out_shape=outs, in_specs=[pl.BlockSpec(memory_spac...  1.88 us
  transfers between devices with their start and end apart: 36, of which 12 were waited for; matrix products, arithmetic and copies ran while one was open for 0% of the time, Pallas kernels for 6%

profile of v1, /device:TPU:0, one launch (start us, length us, event | category | flops | bytes accessed | tf_op | source)
XLA Modules:
  0.0 72.2 jit_solution(11227837941070315977)
XLA Ops:
  0.6 0.9 %copy-done.1 = f32[8,32,256]{2,1,0:T(8,128)S(1)} copy-done((f32[8,32,256]{2,1,0:T(8,128)S(1)}, f32[8,32,256]{2,1,0:T(8,128)}, u32[]{:S(2)}) %copy-start.1) | copy-done | bytes 262168
  1.6 0.9 %copy-done.3 = f32[8,32,256]{2,1,0:T(8,128)S(1)} copy-done((f32[8,32,256]{2,1,0:T(8,128)S(1)}, f32[8,32,256]{2,1,0:T(8,128)}, u32[]{:S(2)}) %copy-start.3) | copy-done | bytes 262168
  2.6 3.1 %collective-permute-start = (f32[4,32,256]{2,1,0:T(8,128)S(1)}, f32[4,32,256]{2,1,0:T(8,128)S(1)}, u32[]{:S(2)}, u32[]{:S(2)}) collective-permute-start(f32[4,32,256]{2,1,0:T(8,128)S(1)} %get-tuple-element.83), channel_id=1, source_target_pairs={{0,4},{4,8},{8,12},{12,0},{1,5},{5,9},{9,13},{13,1},{2,6},{6,10},{... | collective-permute-start | bytes 393224 | tf_op jit(solution)/shard_map/ppermute | solution.py:156
  5.7 2.1 %collective-permute-start.1 = (f32[4,32,256]{2,1,0:T(8,128)S(1)}, f32[4,32,256]{2,1,0:T(8,128)S(1)}, u32[]{:S(2)}, u32[]{:S(2)}) collective-permute-start(f32[4,32,256]{2,1,0:T(8,128)S(1)} %get-tuple-element.84), channel_id=1, source_target_pairs={{0,12},{4,0},{8,4},{12,8},{1,13},{5,1},{9,5},{13,9},{2,14},{6,2},{... | collective-permute-start | bytes 393224 | tf_op jit(solution)/shard_map/ppermute | solution.py:157
  7.8 1.7 %collective-permute-start.3 = (f32[16,2,256]{2,1,0:T(2,128)S(1)}, f32[16,2,256]{2,1,0:T(2,128)S(1)}, u32[]{:S(2)}, u32[]{:S(2)}) collective-permute-start(f32[16,2,256]{2,1,0:T(2,128)S(1)} %get-tuple-element.86), channel_id=1, source_target_pairs={{0,3},{1,0},{2,1},{3,2},{4,7},{5,4},{6,5},{7,6},{8,11},{9,8},{10,9... | collective-permute-start | bytes 98312 | tf_op jit(solution)/shard_map/ppermute | solution.py:159
  9.6 0.6 shard_map.50
  10.2 1.0 %collective-permute-done.2.yl = f32[16,2,256]{2,1,0:T(2,128)S(1)} collective-permute-done((f32[16,2,256]{2,1,0:T(2,128)S(1)}, f32[16,2,256]{2,1,0:T(2,128)S(1)}, u32[]{:S(2)}, u32[]{:S(2)}) %collective-permute-start.2) | collective-permute-done | bytes 32800 | tf_op jit(solution)/shard_map/ppermute | solution.py:158
  11.2 0.9 %collective-permute-done.xl = f32[4,32,256]{2,1,0:T(8,128)S(1)} collective-permute-done((f32[4,32,256]{2,1,0:T(8,128)S(1)}, f32[4,32,256]{2,1,0:T(8,128)S(1)}, u32[]{:S(2)}, u32[]{:S(2)}) %collective-permute-start) | collective-permute-done | bytes 131104 | tf_op jit(solution)/shard_map/ppermute | solution.py:156
  12.1 1.4 %collective-permute-done.1.xh = f32[4,32,256]{2,1,0:T(8,128)S(1)} collective-permute-done((f32[4,32,256]{2,1,0:T(8,128)S(1)}, f32[4,32,256]{2,1,0:T(8,128)S(1)}, u32[]{:S(2)}, u32[]{:S(2)}) %collective-permute-start.1) | collective-permute-done | bytes 131104 | tf_op jit(solution)/shard_map/ppermute | solution.py:157
  13.5 0.2 shard_map.52
  13.7 1.2 %collective-permute-start.4 = (f32[2,32,256]{2,1,0:T(8,128)S(1)}, f32[2,32,256]{2,1,0:T(8,128)S(1)}, u32[]{:S(2)}, u32[]{:S(2)}) collective-permute-start(f32[2,32,256]{2,1,0:T(8,128)S(1)} %get-tuple-element.92), channel_id=1, source_target_pairs={{0,4},{4,8},{8,12},{12,0},{1,5},{5,9},{9,13},{13,1},{2,6},{6,10},{... | collective-permute-start | bytes 196616 | tf_op jit(solution)/shard_map/ppermute | solution.py:156
  14.9 2.7 %collective-permute-start.5 = (f32[2,32,256]{2,1,0:T(8,128)S(1)}, f32[2,32,256]{2,1,0:T(8,128)S(1)}, u32[]{:S(2)}, u32[]{:S(2)}) collective-permute-start(f32[2,32,256]{2,1,0:T(8,128)S(1)} %get-tuple-element.93), channel_id=1, source_target_pairs={{0,12},{4,0},{8,4},{12,8},{1,13},{5,1},{9,5},{13,9},{2,14},{6,2},{... | collective-permute-start | bytes 196616 | tf_op jit(solution)/shard_map/ppermute | solution.py:157
  17.6 1.7 %collective-permute-start.7 = (f32[8,2,256]{2,1,0:T(2,128)S(1)}, f32[8,2,256]{2,1,0:T(2,128)S(1)}, u32[]{:S(2)}, u32[]{:S(2)}) collective-permute-start(f32[8,2,256]{2,1,0:T(2,128)S(1)} %get-tuple-element.95), channel_id=1, source_target_pairs={{0,3},{1,0},{2,1},{3,2},{4,7},{5,4},{6,5},{7,6},{8,11},{9,8},{10,9... | collective-permute-start | bytes 49160 | tf_op jit(solution)/shard_map/ppermute | solution.py:159
  19.3 0.4 shard_map.53
  19.7 1.0 %collective-permute-done.6.yl = f32[8,2,256]{2,1,0:T(2,128)S(1)} collective-permute-done((f32[8,2,256]{2,1,0:T(2,128)S(1)}, f32[8,2,256]{2,1,0:T(2,128)S(1)}, u32[]{:S(2)}, u32[]{:S(2)}) %collective-permute-start.6) | collective-permute-done | bytes 16416 | tf_op jit(solution)/shard_map/ppermute | solution.py:158
  20.8 0.1 shard_map.54
  21.0 3.8 %collective-permute-start.9 = (f32[2,32,256]{2,1,0:T(8,128)S(1)}, f32[2,32,256]{2,1,0:T(8,128)S(1)}, u32[]{:S(2)}, u32[]{:S(2)}) collective-permute-start(f32[2,32,256]{2,1,0:T(8,128)S(1)} %get-tuple-element.102), channel_id=1, source_target_pairs={{0,12},{4,0},{8,4},{12,8},{1,13},{5,1},{9,5},{13,9},{2,14},{6,2},{... | collective-permute-start | bytes 196616 | tf_op jit(solution)/shard_map/ppermute | solution.py:157
  24.8 1.0 %collective-permute-start.10 = (f32[8,2,256]{2,1,0:T(2,128)S(1)}, f32[8,2,256]{2,1,0:T(2,128)S(1)}, u32[]{:S(2)}, u32[]{:S(2)}) collective-permute-start(f32[8,2,256]{2,1,0:T(2,128)S(1)} %get-tuple-element.103), channel_id=1, source_target_pairs={{0,1},{1,2},{2,3},{3,0},{4,5},{5,6},{6,7},{7,4},{8,9},{9,10},{10,1... | collective-permute-start | bytes 49160 | tf_op jit(solution)/shard_map/ppermute | solution.py:158
  25.8 0.7 collective-permute-start.11
  26.5 0.4 shard_map.55
  26.9 1.0 %collective-permute-done.10.yl = f32[8,2,256]{2,1,0:T(2,128)S(1)} collective-permute-done((f32[8,2,256]{2,1,0:T(2,128)S(1)}, f32[8,2,256]{2,1,0:T(2,128)S(1)}, u32[]{:S(2)}, u32[]{:S(2)}) %collective-permute-start.10) | collective-permute-done | bytes 16416 | tf_op jit(solution)/shard_map/ppermute | solution.py:158
  28.0 0.1 shard_map.56
  28.1 0.5 collective-permute-start.12
  28.7 3.3 %collective-permute-start.13 = (f32[2,32,256]{2,1,0:T(8,128)S(1)}, f32[2,32,256]{2,1,0:T(8,128)S(1)}, u32[]{:S(2)}, u32[]{:S(2)}) collective-permute-start(f32[2,32,256]{2,1,0:T(8,128)S(1)} %get-tuple-element.111), channel_id=1, source_target_pairs={{0,12},{4,0},{8,4},{12,8},{1,13},{5,1},{9,5},{13,9},{2,14},{6,2},{... | collective-permute-start | bytes 196616 | tf_op jit(solution)/shard_map/ppermute | solution.py:157
  32.0 1.0 %collective-permute-start.14 = (f32[8,2,256]{2,1,0:T(2,128)S(1)}, f32[8,2,256]{2,1,0:T(2,128)S(1)}, u32[]{:S(2)}, u32[]{:S(2)}) collective-permute-start(f32[8,2,256]{2,1,0:T(2,128)S(1)} %get-tuple-element.112), channel_id=1, source_target_pairs={{0,1},{1,2},{2,3},{3,0},{4,5},{5,6},{6,7},{7,4},{8,9},{9,10},{10,1... | collective-permute-start | bytes 49160 | tf_op jit(solution)/shard_map/ppermute | solution.py:158
  33.1 0.7 collective-permute-start.15
  33.8 0.4 shard_map.57
  34.2 1.0 %collective-permute-done.14.yl = f32[8,2,256]{2,1,0:T(2,128)S(1)} collective-permute-done((f32[8,2,256]{2,1,0:T(2,128)S(1)}, f32[8,2,256]{2,1,0:T(2,128)S(1)}, u32[]{:S(2)}, u32[]{:S(2)}) %collective-permute-start.14) | collective-permute-done | bytes 16416 | tf_op jit(solution)/shard_map/ppermute | solution.py:158
  35.2 0.1 shard_map.58
  35.4 1.0 %collective-permute-start.16 = (f32[2,32,256]{2,1,0:T(8,128)S(1)}, f32[2,32,256]{2,1,0:T(8,128)S(1)}, u32[]{:S(2)}, u32[]{:S(2)}) collective-permute-start(f32[2,32,256]{2,1,0:T(8,128)S(1)} %get-tuple-element.119), channel_id=1, source_target_pairs={{0,4},{4,8},{8,12},{12,0},{1,5},{5,9},{9,13},{13,1},{2,6},{6,10},{... | collective-permute-start | bytes 196616 | tf_op jit(solution)/shard_map/ppermute | solution.py:156
  36.4 2.9 %collective-permute-start.17 = (f32[2,32,256]{2,1,0:T(8,128)S(1)}, f32[2,32,256]{2,1,0:T(8,128)S(1)}, u32[]{:S(2)}, u32[]{:S(2)}) collective-permute-start(f32[2,32,256]{2,1,0:T(8,128)S(1)} %get-tuple-element.120), channel_id=1, source_target_pairs={{0,12},{4,0},{8,4},{12,8},{1,13},{5,1},{9,5},{13,9},{2,14},{6,2},{... | collective-permute-start | bytes 196616 | tf_op jit(solution)/shard_map/ppermute | solution.py:157
  39.3 1.0 %collective-permute-start.18 = (f32[8,2,256]{2,1,0:T(2,128)S(1)}, f32[8,2,256]{2,1,0:T(2,128)S(1)}, u32[]{:S(2)}, u32[]{:S(2)}) collective-permute-start(f32[8,2,256]{2,1,0:T(2,128)S(1)} %get-tuple-element.121), channel_id=1, source_target_pairs={{0,1},{1,2},{2,3},{3,0},{4,5},{5,6},{6,7},{7,4},{8,9},{9,10},{10,1... | collective-permute-start | bytes 49160 | tf_op jit(solution)/shard_map/ppermute | solution.py:158
  40.3 0.7 collective-permute-start.19
  41.0 0.4 shard_map.59
  41.4 1.0 %collective-permute-done.18.yl = f32[8,2,256]{2,1,0:T(2,128)S(1)} collective-permute-done((f32[8,2,256]{2,1,0:T(2,128)S(1)}, f32[8,2,256]{2,1,0:T(2,128)S(1)}, u32[]{:S(2)}, u32[]{:S(2)}) %collective-permute-start.18) | collective-permute-done | bytes 16416 | tf_op jit(solution)/shard_map/ppermute | solution.py:158
  42.5 0.1 shard_map.60
  42.7 1.0 %collective-permute-start.20 = (f32[2,32,256]{2,1,0:T(8,128)S(1)}, f32[2,32,256]{2,1,0:T(8,128)S(1)}, u32[]{:S(2)}, u32[]{:S(2)}) collective-permute-start(f32[2,32,256]{2,1,0:T(8,128)S(1)} %get-tuple-element.128), channel_id=1, source_target_pairs={{0,4},{4,8},{8,12},{12,0},{1,5},{5,9},{9,13},{13,1},{2,6},{6,10},{... | collective-permute-start | bytes 196616 | tf_op jit(solution)/shard_map/ppermute | solution.py:156
  43.6 2.9 %collective-permute-start.21 = (f32[2,32,256]{2,1,0:T(8,128)S(1)}, f32[2,32,256]{2,1,0:T(8,128)S(1)}, u32[]{:S(2)}, u32[]{:S(2)}) collective-permute-start(f32[2,32,256]{2,1,0:T(8,128)S(1)} %get-tuple-element.129), channel_id=1, source_target_pairs={{0,12},{4,0},{8,4},{12,8},{1,13},{5,1},{9,5},{13,9},{2,14},{6,2},{... | collective-permute-start | bytes 196616 | tf_op jit(solution)/shard_map/ppermute | solution.py:157
  46.5 1.0 %collective-permute-start.22 = (f32[8,2,256]{2,1,0:T(2,128)S(1)}, f32[8,2,256]{2,1,0:T(2,128)S(1)}, u32[]{:S(2)}, u32[]{:S(2)}) collective-permute-start(f32[8,2,256]{2,1,0:T(2,128)S(1)} %get-tuple-element.130), channel_id=1, source_target_pairs={{0,1},{1,2},{2,3},{3,0},{4,5},{5,6},{6,7},{7,4},{8,9},{9,10},{10,1... | collective-permute-start | bytes 49160 | tf_op jit(solution)/shard_map/ppermute | solution.py:158
  47.5 0.8 %collective-permute-start.23 = (f32[8,2,256]{2,1,0:T(2,128)S(1)}, f32[8,2,256]{2,1,0:T(2,128)S(1)}, u32[]{:S(2)}, u32[]{:S(2)}) collective-permute-start(f32[8,2,256]{2,1,0:T(2,128)S(1)} %get-tuple-element.131), channel_id=1, source_target_pairs={{0,3},{1,0},{2,1},{3,2},{4,7},{5,4},{6,5},{7,6},{8,11},{9,8},{10,9... | collective-permute-start | bytes 49160 | tf_op jit(solution)/shard_map/ppermute | solution.py:159
  48.3 0.4 shard_map.61
  48.7 1.0 %collective-permute-done.22.yl = f32[8,2,256]{2,1,0:T(2,128)S(1)} collective-permute-done((f32[8,2,256]{2,1,0:T(2,128)S(1)}, f32[8,2,256]{2,1,0:T(2,128)S(1)}, u32[]{:S(2)}, u32[]{:S(2)}) %collective-permute-start.22) | collective-permute-done | bytes 16416 | tf_op jit(solution)/shard_map/ppermute | solution.py:158
  49.7 0.1 shard_map.62
  49.9 1.0 %collective-permute-start.24 = (f32[2,32,256]{2,1,0:T(8,128)S(1)}, f32[2,32,256]{2,1,0:T(8,128)S(1)}, u32[]{:S(2)}, u32[]{:S(2)}) collective-permute-start(f32[2,32,256]{2,1,0:T(8,128)S(1)} %get-tuple-element.137), channel_id=1, source_target_pairs={{0,4},{4,8},{8,12},{12,0},{1,5},{5,9},{9,13},{13,1},{2,6},{6,10},{... | collective-permute-start | bytes 196616 | tf_op jit(solution)/shard_map/ppermute | solution.py:156
  50.8 2.9 %collective-permute-start.25 = (f32[2,32,256]{2,1,0:T(8,128)S(1)}, f32[2,32,256]{2,1,0:T(8,128)S(1)}, u32[]{:S(2)}, u32[]{:S(2)}) collective-permute-start(f32[2,32,256]{2,1,0:T(8,128)S(1)} %get-tuple-element.138), channel_id=1, source_target_pairs={{0,12},{4,0},{8,4},{12,8},{1,13},{5,1},{9,5},{13,9},{2,14},{6,2},{... | collective-permute-start | bytes 196616 | tf_op jit(solution)/shard_map/ppermute | solution.py:157
  53.8 1.0 %collective-permute-start.26 = (f32[8,2,256]{2,1,0:T(2,128)S(1)}, f32[8,2,256]{2,1,0:T(2,128)S(1)}, u32[]{:S(2)}, u32[]{:S(2)}) collective-permute-start(f32[8,2,256]{2,1,0:T(2,128)S(1)} %get-tuple-element.139), channel_id=1, source_target_pairs={{0,1},{1,2},{2,3},{3,0},{4,5},{5,6},{6,7},{7,4},{8,9},{9,10},{10,1... | collective-permute-start | bytes 49160 | tf_op jit(solution)/shard_map/ppermute | solution.py:158
  54.8 0.8 %collective-permute-start.27 = (f32[8,2,256]{2,1,0:T(2,128)S(1)}, f32[8,2,256]{2,1,0:T(2,128)S(1)}, u32[]{:S(2)}, u32[]{:S(2)}) collective-permute-start(f32[8,2,256]{2,1,0:T(2,128)S(1)} %get-tuple-element.140), channel_id=1, source_target_pairs={{0,3},{1,0},{2,1},{3,2},{4,7},{5,4},{6,5},{7,6},{8,11},{9,8},{10,9... | collective-permute-start | bytes 49160 | tf_op jit(solution)/shard_map/ppermute | solution.py:159
  55.5 0.4 shard_map.63
  55.9 1.0 %collective-permute-done.26.yl = f32[8,2,256]{2,1,0:T(2,128)S(1)} collective-permute-done((f32[8,2,256]{2,1,0:T(2,128)S(1)}, f32[8,2,256]{2,1,0:T(2,128)S(1)}, u32[]{:S(2)}, u32[]{:S(2)}) %collective-permute-start.26) | collective-permute-done | bytes 16416 | tf_op jit(solution)/shard_map/ppermute | solution.py:158
  57.0 0.1 shard_map.64
  57.1 1.1 %collective-permute-start.28 = (f32[2,32,256]{2,1,0:T(8,128)S(1)}, f32[2,32,256]{2,1,0:T(8,128)S(1)}, u32[]{:S(2)}, u32[]{:S(2)}) collective-permute-start(f32[2,32,256]{2,1,0:T(8,128)S(1)} %get-tuple-element.147), channel_id=1, source_target_pairs={{0,4},{4,8},{8,12},{12,0},{1,5},{5,9},{9,13},{13,1},{2,6},{6,10},{... | collective-permute-start | bytes 196616 | tf_op jit(solution)/shard_map/ppermute | solution.py:156
  58.2 2.8 %collective-permute-start.29 = (f32[2,32,256]{2,1,0:T(8,128)S(1)}, f32[2,32,256]{2,1,0:T(8,128)S(1)}, u32[]{:S(2)}, u32[]{:S(2)}) collective-permute-start(f32[2,32,256]{2,1,0:T(8,128)S(1)} %get-tuple-element.148), channel_id=1, source_target_pairs={{0,12},{4,0},{8,4},{12,8},{1,13},{5,1},{9,5},{13,9},{2,14},{6,2},{... | collective-permute-start | bytes 196616 | tf_op jit(solution)/shard_map/ppermute | solution.py:157
  61.0 1.0 %collective-permute-start.30 = (f32[8,2,256]{2,1,0:T(2,128)S(1)}, f32[8,2,256]{2,1,0:T(2,128)S(1)}, u32[]{:S(2)}, u32[]{:S(2)}) collective-permute-start(f32[8,2,256]{2,1,0:T(2,128)S(1)} %get-tuple-element.149), channel_id=1, source_target_pairs={{0,1},{1,2},{2,3},{3,0},{4,5},{5,6},{6,7},{7,4},{8,9},{9,10},{10,1... | collective-permute-start | bytes 49160 | tf_op jit(solution)/shard_map/ppermute | solution.py:158
  62.0 0.8 %collective-permute-start.31 = (f32[8,2,256]{2,1,0:T(2,128)S(1)}, f32[8,2,256]{2,1,0:T(2,128)S(1)}, u32[]{:S(2)}, u32[]{:S(2)}) collective-permute-start(f32[8,2,256]{2,1,0:T(2,128)S(1)} %get-tuple-element.150), channel_id=1, source_target_pairs={{0,3},{1,0},{2,1},{3,2},{4,7},{5,4},{6,5},{7,6},{8,11},{9,8},{10,9... | collective-permute-start | bytes 49160 | tf_op jit(solution)/shard_map/ppermute | solution.py:159
  62.7 0.4 shard_map.65
  63.1 1.0 %collective-permute-done.30.yl = f32[8,2,256]{2,1,0:T(2,128)S(1)} collective-permute-done((f32[8,2,256]{2,1,0:T(2,128)S(1)}, f32[8,2,256]{2,1,0:T(2,128)S(1)}, u32[]{:S(2)}, u32[]{:S(2)}) %collective-permute-start.30) | collective-permute-done | bytes 16416 | tf_op jit(solution)/shard_map/ppermute | solution.py:158
  64.2 0.1 shard_map.66
  64.3 1.1 %collective-permute-start.32 = (f32[2,32,256]{2,1,0:T(8,128)S(1)}, f32[2,32,256]{2,1,0:T(8,128)S(1)}, u32[]{:S(2)}, u32[]{:S(2)}) collective-permute-start(f32[2,32,256]{2,1,0:T(8,128)S(1)} %get-tuple-element.156), channel_id=1, source_target_pairs={{0,4},{4,8},{8,12},{12,0},{1,5},{5,9},{9,13},{13,1},{2,6},{6,10},{... | collective-permute-start | bytes 196616 | tf_op jit(solution)/shard_map/ppermute | solution.py:156
  65.4 2.8 %collective-permute-start.33 = (f32[2,32,256]{2,1,0:T(8,128)S(1)}, f32[2,32,256]{2,1,0:T(8,128)S(1)}, u32[]{:S(2)}, u32[]{:S(2)}) collective-permute-start(f32[2,32,256]{2,1,0:T(8,128)S(1)} %get-tuple-element.157), channel_id=1, source_target_pairs={{0,12},{4,0},{8,4},{12,8},{1,13},{5,1},{9,5},{13,9},{2,14},{6,2},{... | collective-permute-start | bytes 196616 | tf_op jit(solution)/shard_map/ppermute | solution.py:157
  68.2 1.0 %collective-permute-start.34 = (f32[8,2,256]{2,1,0:T(2,128)S(1)}, f32[8,2,256]{2,1,0:T(2,128)S(1)}, u32[]{:S(2)}, u32[]{:S(2)}) collective-permute-start(f32[8,2,256]{2,1,0:T(2,128)S(1)} %get-tuple-element.158), channel_id=1, source_target_pairs={{0,1},{1,2},{2,3},{3,0},{4,5},{5,6},{6,7},{7,4},{8,9},{9,10},{10,1... | collective-permute-start | bytes 49160 | tf_op jit(solution)/shard_map/ppermute | solution.py:158
  69.2 0.8 %collective-permute-start.35 = (f32[8,2,256]{2,1,0:T(2,128)S(1)}, f32[8,2,256]{2,1,0:T(2,128)S(1)}, u32[]{:S(2)}, u32[]{:S(2)}) collective-permute-start(f32[8,2,256]{2,1,0:T(2,128)S(1)} %get-tuple-element.159), channel_id=1, source_target_pairs={{0,3},{1,0},{2,1},{3,2},{4,7},{5,4},{6,5},{7,6},{8,11},{9,8},{10,9... | collective-permute-start | bytes 49160 | tf_op jit(solution)/shard_map/ppermute | solution.py:159
  69.9 1.1 %shard_map.67 = (f32[8,32,256]{2,1,0:T(8,128)S(1)}, f32[8,32,256]{2,1,0:T(8,128)}, f32[8,32,256]{2,1,0:T(8,128)S(1)}) custom-call(f32[1]{0:T(128)} %bitcast.scale, f32[8,32,256]{2,1,0:T(8,128)S(1)} %get-tuple-element.144.u, f32[8,32,256]{2,1,0:T(8,128)S(1)} %get-tuple-element.141.new_v.v, f32[8,32,256]{2,1,0:T(8,128)S(1)} %copy-done, ...), custom_call_target="tpu_custom_call" | custom-call | flops 2621440 | bytes 2097152 | tf_op jit(solution)/shard_map/pallas_call | solution.py:141
  71.0 0.3 collective-permute-done.34.yl
  71.4 0.8 %shard_map.68 = f32[8,32,256]{2,1,0:T(8,128)} custom-call(f32[1]{0:T(128)} %bitcast.scale, f32[8,32,256]{2,1,0:T(8,128)S(1)} %get-tuple-element.154.part, f32[8,32,256]{2,1,0:T(8,128)S(1)} %get-tuple-element.155.base_v, f32[2,32,256]{2,1,0:T(8,128)S(1)} %collective-permute-done.32.xl, f32[2,32,256]{2,1,0:T(8,128)S(1)} %collective-permute-done.33.xh, ...), custom_call_target="tpu_custom_call" | custom-call | flops 2621440 | bytes 950272 | tf_op jit(solution)/shard_map/pallas_call | solution.py:141
  (35 shorter events, 0.5 us)
Async XLA Ops:
  0.6 1.0 %copy-start.1 = (f32[8,32,256]{2,1,0:T(8,128)S(1)}, f32[8,32,256]{2,1,0:T(8,128)}, u32[]{:S(2)}) copy-start(f32[8,32,256]{2,1,0:T(8,128)} %v.7) | copy-start | bytes 786436
  1.6 0.9 %copy-start.3 = (f32[8,32,256]{2,1,0:T(8,128)S(1)}, f32[8,32,256]{2,1,0:T(8,128)}, u32[]{:S(2)}) copy-start(f32[8,32,256]{2,1,0:T(8,128)} %u.5) | copy-start | bytes 786436
  2.6 9.5 %collective-permute-start = (f32[4,32,256]{2,1,0:T(8,128)S(1)}, f32[4,32,256]{2,1,0:T(8,128)S(1)}, u32[]{:S(2)}, u32[]{:S(2)}) collective-permute-start(f32[4,32,256]{2,1,0:T(8,128)S(1)} %get-tuple-element.83), channel_id=1, source_target_pairs={{0,4},{4,8},{8,12},{12,0},{1,5},{5,9},{9,13},{13,1},{2,6},{6,10},{... | collective-permute-start | bytes 393224 | tf_op jit(solution)/shard_map/ppermute | solution.py:156
  5.7 7.8 %collective-permute-start.1 = (f32[4,32,256]{2,1,0:T(8,128)S(1)}, f32[4,32,256]{2,1,0:T(8,128)S(1)}, u32[]{:S(2)}, u32[]{:S(2)}) collective-permute-start(f32[4,32,256]{2,1,0:T(8,128)S(1)} %get-tuple-element.84), channel_id=1, source_target_pairs={{0,12},{4,0},{8,4},{12,8},{1,13},{5,1},{9,5},{13,9},{2,14},{6,2},{... | collective-permute-start | bytes 393224 | tf_op jit(solution)/shard_map/ppermute | solution.py:157
  7.8 3.3 %collective-permute-start.2 = (f32[16,2,256]{2,1,0:T(2,128)S(1)}, f32[16,2,256]{2,1,0:T(2,128)S(1)}, u32[]{:S(2)}, u32[]{:S(2)}) collective-permute-start(f32[16,2,256]{2,1,0:T(2,128)S(1)} %get-tuple-element.85), channel_id=1, source_target_pairs={{0,1},{1,2},{2,3},{3,0},{4,5},{5,6},{6,7},{7,4},{8,9},{9,10},{10,1... | collective-permute-start | bytes 98312 | tf_op jit(solution)/shard_map/ppermute | solution.py:158
  7.8 5.7 %copy-start = (f32[8,32,256]{2,1,0:T(8,128)S(1)}, f32[8,32,256]{2,1,0:T(8,128)}, u32[]{:S(2)}) copy-start(f32[8,32,256]{2,1,0:T(8,128)} %s.17) | copy-start | bytes 786436
  7.8 5.7 %copy-start.2 = (f32[8,32,256]{2,1,0:T(8,128)S(1)}, f32[8,32,256]{2,1,0:T(8,128)}, u32[]{:S(2)}) copy-start(f32[8,32,256]{2,1,0:T(8,128)} %v.7) | copy-start | bytes 786436
  7.8 3.3 %collective-permute-start.3 = (f32[16,2,256]{2,1,0:T(2,128)S(1)}, f32[16,2,256]{2,1,0:T(2,128)S(1)}, u32[]{:S(2)}, u32[]{:S(2)}) collective-permute-start(f32[16,2,256]{2,1,0:T(2,128)S(1)} %get-tuple-element.86), channel_id=1, source_target_pairs={{0,3},{1,0},{2,1},{3,2},{4,7},{5,4},{6,5},{7,6},{8,11},{9,8},{10,9... | collective-permute-start | bytes 98312 | tf_op jit(solution)/shard_map/ppermute | solution.py:159
  13.7 7.1 %collective-permute-start.4 = (f32[2,32,256]{2,1,0:T(8,128)S(1)}, f32[2,32,256]{2,1,0:T(8,128)S(1)}, u32[]{:S(2)}, u32[]{:S(2)}) collective-permute-start(f32[2,32,256]{2,1,0:T(8,128)S(1)} %get-tuple-element.92), channel_id=1, source_target_pairs={{0,4},{4,8},{8,12},{12,0},{1,5},{5,9},{9,13},{13,1},{2,6},{6,10},{... | collective-permute-start | bytes 196616 | tf_op jit(solution)/shard_map/ppermute | solution.py:156
  14.9 5.9 %collective-permute-start.5 = (f32[2,32,256]{2,1,0:T(8,128)S(1)}, f32[2,32,256]{2,1,0:T(8,128)S(1)}, u32[]{:S(2)}, u32[]{:S(2)}) collective-permute-start(f32[2,32,256]{2,1,0:T(8,128)S(1)} %get-tuple-element.93), channel_id=1, source_target_pairs={{0,12},{4,0},{8,4},{12,8},{1,13},{5,1},{9,5},{13,9},{2,14},{6,2},{... | collective-permute-start | bytes 196616 | tf_op jit(solution)/shard_map/ppermute | solution.py:157
  17.6 3.2 %collective-permute-start.6 = (f32[8,2,256]{2,1,0:T(2,128)S(1)}, f32[8,2,256]{2,1,0:T(2,128)S(1)}, u32[]{:S(2)}, u32[]{:S(2)}) collective-permute-start(f32[8,2,256]{2,1,0:T(2,128)S(1)} %get-tuple-element.94), channel_id=1, source_target_pairs={{0,1},{1,2},{2,3},{3,0},{4,5},{5,6},{6,7},{7,4},{8,9},{9,10},{10,1... | collective-permute-start | bytes 49160 | tf_op jit(solution)/shard_map/ppermute | solution.py:158
  17.6 3.2 %collective-permute-start.7 = (f32[8,2,256]{2,1,0:T(2,128)S(1)}, f32[8,2,256]{2,1,0:T(2,128)S(1)}, u32[]{:S(2)}, u32[]{:S(2)}) collective-permute-start(f32[8,2,256]{2,1,0:T(2,128)S(1)} %get-tuple-element.95), channel_id=1, source_target_pairs={{0,3},{1,0},{2,1},{3,2},{4,7},{5,4},{6,5},{7,6},{8,11},{9,8},{10,9... | collective-permute-start | bytes 49160 | tf_op jit(solution)/shard_map/ppermute | solution.py:159
  20.9 7.1 %collective-permute-start.8 = (f32[2,32,256]{2,1,0:T(8,128)S(1)}, f32[2,32,256]{2,1,0:T(8,128)S(1)}, u32[]{:S(2)}, u32[]{:S(2)}) collective-permute-start(f32[2,32,256]{2,1,0:T(8,128)S(1)} %get-tuple-element.101), channel_id=1, source_target_pairs={{0,4},{4,8},{8,12},{12,0},{1,5},{5,9},{9,13},{13,1},{2,6},{6,10},{... | collective-permute-start | bytes 196616 | tf_op jit(solution)/shard_map/ppermute | solution.py:156
  21.0 7.0 %collective-permute-start.9 = (f32[2,32,256]{2,1,0:T(8,128)S(1)}, f32[2,32,256]{2,1,0:T(8,128)S(1)}, u32[]{:S(2)}, u32[]{:S(2)}) collective-permute-start(f32[2,32,256]{2,1,0:T(8,128)S(1)} %get-tuple-element.102), channel_id=1, source_target_pairs={{0,12},{4,0},{8,4},{12,8},{1,13},{5,1},{9,5},{13,9},{2,14},{6,2},{... | collective-permute-start | bytes 196616 | tf_op jit(solution)/shard_map/ppermute | solution.py:157
  24.8 3.2 %collective-permute-start.10 = (f32[8,2,256]{2,1,0:T(2,128)S(1)}, f32[8,2,256]{2,1,0:T(2,128)S(1)}, u32[]{:S(2)}, u32[]{:S(2)}) collective-permute-start(f32[8,2,256]{2,1,0:T(2,128)S(1)} %get-tuple-element.103), channel_id=1, source_target_pairs={{0,1},{1,2},{2,3},{3,0},{4,5},{5,6},{6,7},{7,4},{8,9},{9,10},{10,1... | collective-permute-start | bytes 49160 | tf_op jit(solution)/shard_map/ppermute | solution.py:158
  25.8 2.1 %collective-permute-start.11 = (f32[8,2,256]{2,1,0:T(2,128)S(1)}, f32[8,2,256]{2,1,0:T(2,128)S(1)}, u32[]{:S(2)}, u32[]{:S(2)}) collective-permute-start(f32[8,2,256]{2,1,0:T(2,128)S(1)} %get-tuple-element.104), channel_id=1, source_target_pairs={{0,3},{1,0},{2,1},{3,2},{4,7},{5,4},{6,5},{7,6},{8,11},{9,8},{10,9... | collective-permute-start | bytes 49160 | tf_op jit(solution)/shard_map/ppermute | solution.py:159
  28.1 7.1 %collective-permute-start.12 = (f32[2,32,256]{2,1,0:T(8,128)S(1)}, f32[2,32,256]{2,1,0:T(8,128)S(1)}, u32[]{:S(2)}, u32[]{:S(2)}) collective-permute-start(f32[2,32,256]{2,1,0:T(8,128)S(1)} %get-tuple-element.110), channel_id=1, source_target_pairs={{0,4},{4,8},{8,12},{12,0},{1,5},{5,9},{9,13},{13,1},{2,6},{6,10},{... | collective-permute-start | bytes 196616 | tf_op jit(solution)/shard_map/ppermute | solution.py:156
  28.7 6.5 %collective-permute-start.13 = (f32[2,32,256]{2,1,0:T(8,128)S(1)}, f32[2,32,256]{2,1,0:T(8,128)S(1)}, u32[]{:S(2)}, u32[]{:S(2)}) collective-permute-start(f32[2,32,256]{2,1,0:T(8,128)S(1)} %get-tuple-element.111), channel_id=1, source_target_pairs={{0,12},{4,0},{8,4},{12,8},{1,13},{5,1},{9,5},{13,9},{2,14},{6,2},{... | collective-permute-start | bytes 196616 | tf_op jit(solution)/shard_map/ppermute | solution.py:157
  32.0 3.2 %collective-permute-start.14 = (f32[8,2,256]{2,1,0:T(2,128)S(1)}, f32[8,2,256]{2,1,0:T(2,128)S(1)}, u32[]{:S(2)}, u32[]{:S(2)}) collective-permute-start(f32[8,2,256]{2,1,0:T(2,128)S(1)} %get-tuple-element.112), channel_id=1, source_target_pairs={{0,1},{1,2},{2,3},{3,0},{4,5},{5,6},{6,7},{7,4},{8,9},{9,10},{10,1... | collective-permute-start | bytes 49160 | tf_op jit(solution)/shard_map/ppermute | solution.py:158
  33.1 2.1 %collective-permute-start.15 = (f32[8,2,256]{2,1,0:T(2,128)S(1)}, f32[8,2,256]{2,1,0:T(2,128)S(1)}, u32[]{:S(2)}, u32[]{:S(2)}) collective-permute-start(f32[8,2,256]{2,1,0:T(2,128)S(1)} %get-tuple-element.113), channel_id=1, source_target_pairs={{0,3},{1,0},{2,1},{3,2},{4,7},{5,4},{6,5},{7,6},{8,11},{9,8},{10,9... | collective-permute-start | bytes 49160 | tf_op jit(solution)/shard_map/ppermute | solution.py:159
  35.4 7.1 %collective-permute-start.16 = (f32[2,32,256]{2,1,0:T(8,128)S(1)}, f32[2,32,256]{2,1,0:T(8,128)S(1)}, u32[]{:S(2)}, u32[]{:S(2)}) collective-permute-start(f32[2,32,256]{2,1,0:T(8,128)S(1)} %get-tuple-element.119), channel_id=1, source_target_pairs={{0,4},{4,8},{8,12},{12,0},{1,5},{5,9},{9,13},{13,1},{2,6},{6,10},{... | collective-permute-start | bytes 196616 | tf_op jit(solution)/shard_map/ppermute | solution.py:156
  36.4 6.1 %collective-permute-start.17 = (f32[2,32,256]{2,1,0:T(8,128)S(1)}, f32[2,32,256]{2,1,0:T(8,128)S(1)}, u32[]{:S(2)}, u32[]{:S(2)}) collective-permute-start(f32[2,32,256]{2,1,0:T(8,128)S(1)} %get-tuple-element.120), channel_id=1, source_target_pairs={{0,12},{4,0},{8,4},{12,8},{1,13},{5,1},{9,5},{13,9},{2,14},{6,2},{... | collective-permute-start | bytes 196616 | tf_op jit(solution)/shard_map/ppermute | solution.py:157
  39.3 3.2 %collective-permute-start.18 = (f32[8,2,256]{2,1,0:T(2,128)S(1)}, f32[8,2,256]{2,1,0:T(2,128)S(1)}, u32[]{:S(2)}, u32[]{:S(2)}) collective-permute-start(f32[8,2,256]{2,1,0:T(2,128)S(1)} %get-tuple-element.121), channel_id=1, source_target_pairs={{0,1},{1,2},{2,3},{3,0},{4,5},{5,6},{6,7},{7,4},{8,9},{9,10},{10,1... | collective-permute-start | bytes 49160 | tf_op jit(solution)/shard_map/ppermute | solution.py:158
  40.3 2.1 %collective-permute-start.19 = (f32[8,2,256]{2,1,0:T(2,128)S(1)}, f32[8,2,256]{2,1,0:T(2,128)S(1)}, u32[]{:S(2)}, u32[]{:S(2)}) collective-permute-start(f32[8,2,256]{2,1,0:T(2,128)S(1)} %get-tuple-element.122), channel_id=1, source_target_pairs={{0,3},{1,0},{2,1},{3,2},{4,7},{5,4},{6,5},{7,6},{8,11},{9,8},{10,9... | collective-permute-start | bytes 49160 | tf_op jit(solution)/shard_map/ppermute | solution.py:159
  42.7 7.1 %collective-permute-start.20 = (f32[2,32,256]{2,1,0:T(8,128)S(1)}, f32[2,32,256]{2,1,0:T(8,128)S(1)}, u32[]{:S(2)}, u32[]{:S(2)}) collective-permute-start(f32[2,32,256]{2,1,0:T(8,128)S(1)} %get-tuple-element.128), channel_id=1, source_target_pairs={{0,4},{4,8},{8,12},{12,0},{1,5},{5,9},{9,13},{13,1},{2,6},{6,10},{... | collective-permute-start | bytes 196616 | tf_op jit(solution)/shard_map/ppermute | solution.py:156
  43.6 6.1 %collective-permute-start.21 = (f32[2,32,256]{2,1,0:T(8,128)S(1)}, f32[2,32,256]{2,1,0:T(8,128)S(1)}, u32[]{:S(2)}, u32[]{:S(2)}) collective-permute-start(f32[2,32,256]{2,1,0:T(8,128)S(1)} %get-tuple-element.129), channel_id=1, source_target_pairs={{0,12},{4,0},{8,4},{12,8},{1,13},{5,1},{9,5},{13,9},{2,14},{6,2},{... | collective-permute-start | bytes 196616 | tf_op jit(solution)/shard_map/ppermute | solution.py:157
  46.5 3.2 %collective-permute-start.22 = (f32[8,2,256]{2,1,0:T(2,128)S(1)}, f32[8,2,256]{2,1,0:T(2,128)S(1)}, u32[]{:S(2)}, u32[]{:S(2)}) collective-permute-start(f32[8,2,256]{2,1,0:T(2,128)S(1)} %get-tuple-element.130), channel_id=1, source_target_pairs={{0,1},{1,2},{2,3},{3,0},{4,5},{5,6},{6,7},{7,4},{8,9},{9,10},{10,1... | collective-permute-start | bytes 49160 | tf_op jit(solution)/shard_map/ppermute | solution.py:158
  47.5 2.2 %collective-permute-start.23 = (f32[8,2,256]{2,1,0:T(2,128)S(1)}, f32[8,2,256]{2,1,0:T(2,128)S(1)}, u32[]{:S(2)}, u32[]{:S(2)}) collective-permute-start(f32[8,2,256]{2,1,0:T(2,128)S(1)} %get-tuple-element.131), channel_id=1, source_target_pairs={{0,3},{1,0},{2,1},{3,2},{4,7},{5,4},{6,5},{7,6},{8,11},{9,8},{10,9... | collective-permute-start | bytes 49160 | tf_op jit(solution)/shard_map/ppermute | solution.py:159
  49.9 7.1 %collective-permute-start.24 = (f32[2,32,256]{2,1,0:T(8,128)S(1)}, f32[2,32,256]{2,1,0:T(8,128)S(1)}, u32[]{:S(2)}, u32[]{:S(2)}) collective-permute-start(f32[2,32,256]{2,1,0:T(8,128)S(1)} %get-tuple-element.137), channel_id=1, source_target_pairs={{0,4},{4,8},{8,12},{12,0},{1,5},{5,9},{9,13},{13,1},{2,6},{6,10},{... | collective-permute-start | bytes 196616 | tf_op jit(solution)/shard_map/ppermute | solution.py:156
  50.8 6.1 %collective-permute-start.25 = (f32[2,32,256]{2,1,0:T(8,128)S(1)}, f32[2,32,256]{2,1,0:T(8,128)S(1)}, u32[]{:S(2)}, u32[]{:S(2)}) collective-permute-start(f32[2,32,256]{2,1,0:T(8,128)S(1)} %get-tuple-element.138), channel_id=1, source_target_pairs={{0,12},{4,0},{8,4},{12,8},{1,13},{5,1},{9,5},{13,9},{2,14},{6,2},{... | collective-permute-start | bytes 196616 | tf_op jit(solution)/shard_map/ppermute | solution.py:157
  53.8 3.2 %collective-permute-start.26 = (f32[8,2,256]{2,1,0:T(2,128)S(1)}, f32[8,2,256]{2,1,0:T(2,128)S(1)}, u32[]{:S(2)}, u32[]{:S(2)}) collective-permute-start(f32[8,2,256]{2,1,0:T(2,128)S(1)} %get-tuple-element.139), channel_id=1, source_target_pairs={{0,1},{1,2},{2,3},{3,0},{4,5},{5,6},{6,7},{7,4},{8,9},{9,10},{10,1... | collective-permute-start | bytes 49160 | tf_op jit(solution)/shard_map/ppermute | solution.py:158
  54.8 2.2 %collective-permute-start.27 = (f32[8,2,256]{2,1,0:T(2,128)S(1)}, f32[8,2,256]{2,1,0:T(2,128)S(1)}, u32[]{:S(2)}, u32[]{:S(2)}) collective-permute-start(f32[8,2,256]{2,1,0:T(2,128)S(1)} %get-tuple-element.140), channel_id=1, source_target_pairs={{0,3},{1,0},{2,1},{3,2},{4,7},{5,4},{6,5},{7,6},{8,11},{9,8},{10,9... | collective-permute-start | bytes 49160 | tf_op jit(solution)/shard_map/ppermute | solution.py:159
  57.1 7.1 %collective-permute-start.28 = (f32[2,32,256]{2,1,0:T(8,128)S(1)}, f32[2,32,256]{2,1,0:T(8,128)S(1)}, u32[]{:S(2)}, u32[]{:S(2)}) collective-permute-start(f32[2,32,256]{2,1,0:T(8,128)S(1)} %get-tuple-element.147), channel_id=1, source_target_pairs={{0,4},{4,8},{8,12},{12,0},{1,5},{5,9},{9,13},{13,1},{2,6},{6,10},{... | collective-permute-start | bytes 196616 | tf_op jit(solution)/shard_map/ppermute | solution.py:156
  58.2 6.0 %collective-permute-start.29 = (f32[2,32,256]{2,1,0:T(8,128)S(1)}, f32[2,32,256]{2,1,0:T(8,128)S(1)}, u32[]{:S(2)}, u32[]{:S(2)}) collective-permute-start(f32[2,32,256]{2,1,0:T(8,128)S(1)} %get-tuple-element.148), channel_id=1, source_target_pairs={{0,12},{4,0},{8,4},{12,8},{1,13},{5,1},{9,5},{13,9},{2,14},{6,2},{... | collective-permute-start | bytes 196616 | tf_op jit(solution)/shard_map/ppermute | solution.py:157
  61.0 3.2 %collective-permute-start.30 = (f32[8,2,256]{2,1,0:T(2,128)S(1)}, f32[8,2,256]{2,1,0:T(2,128)S(1)}, u32[]{:S(2)}, u32[]{:S(2)}) collective-permute-start(f32[8,2,256]{2,1,0:T(2,128)S(1)} %get-tuple-element.149), channel_id=1, source_target_pairs={{0,1},{1,2},{2,3},{3,0},{4,5},{5,6},{6,7},{7,4},{8,9},{9,10},{10,1... | collective-permute-start | bytes 49160 | tf_op jit(solution)/shard_map/ppermute | solution.py:158
  62.0 2.2 %collective-permute-start.31 = (f32[8,2,256]{2,1,0:T(2,128)S(1)}, f32[8,2,256]{2,1,0:T(2,128)S(1)}, u32[]{:S(2)}, u32[]{:S(2)}) collective-permute-start(f32[8,2,256]{2,1,0:T(2,128)S(1)} %get-tuple-element.150), channel_id=1, source_target_pairs={{0,3},{1,0},{2,1},{3,2},{4,7},{5,4},{6,5},{7,6},{8,11},{9,8},{10,9... | collective-permute-start | bytes 49160 | tf_op jit(solution)/shard_map/ppermute | solution.py:159
  64.3 7.1 %collective-permute-start.32 = (f32[2,32,256]{2,1,0:T(8,128)S(1)}, f32[2,32,256]{2,1,0:T(8,128)S(1)}, u32[]{:S(2)}, u32[]{:S(2)}) collective-permute-start(f32[2,32,256]{2,1,0:T(8,128)S(1)} %get-tuple-element.156), channel_id=1, source_target_pairs={{0,4},{4,8},{8,12},{12,0},{1,5},{5,9},{9,13},{13,1},{2,6},{6,10},{... | collective-permute-start | bytes 196616 | tf_op jit(solution)/shard_map/ppermute | solution.py:156
  65.4 6.0 %collective-permute-start.33 = (f32[2,32,256]{2,1,0:T(8,128)S(1)}, f32[2,32,256]{2,1,0:T(8,128)S(1)}, u32[]{:S(2)}, u32[]{:S(2)}) collective-permute-start(f32[2,32,256]{2,1,0:T(8,128)S(1)} %get-tuple-element.157), channel_id=1, source_target_pairs={{0,12},{4,0},{8,4},{12,8},{1,13},{5,1},{9,5},{13,9},{2,14},{6,2},{... | collective-permute-start | bytes 196616 | tf_op jit(solution)/shard_map/ppermute | solution.py:157
  68.2 3.2 %collective-permute-start.34 = (f32[8,2,256]{2,1,0:T(2,128)S(1)}, f32[8,2,256]{2,1,0:T(2,128)S(1)}, u32[]{:S(2)}, u32[]{:S(2)}) collective-permute-start(f32[8,2,256]{2,1,0:T(2,128)S(1)} %get-tuple-element.158), channel_id=1, source_target_pairs={{0,1},{1,2},{2,3},{3,0},{4,5},{5,6},{6,7},{7,4},{8,9},{9,10},{10,1... | collective-permute-start | bytes 49160 | tf_op jit(solution)/shard_map/ppermute | solution.py:158
  69.2 2.2 %collective-permute-start.35 = (f32[8,2,256]{2,1,0:T(2,128)S(1)}, f32[8,2,256]{2,1,0:T(2,128)S(1)}, u32[]{:S(2)}, u32[]{:S(2)}) collective-permute-start(f32[8,2,256]{2,1,0:T(2,128)S(1)} %get-tuple-element.159), channel_id=1, source_target_pairs={{0,3},{1,0},{2,1},{3,2},{4,7},{5,4},{6,5},{7,6},{8,11},{9,8},{10,9... | collective-permute-start | bytes 49160 | tf_op jit(solution)/shard_map/ppermute | solution.py:159

commit v2 on v0

v2 whole, which is shorter than its diff:
```python
import jax
import jax.numpy as jnp
from jax import lax
from jax.experimental import pallas as pl
from jax.experimental.pallas import tpu as pltpu
from jax.sharding import PartitionSpec as P

STEPS = 8

time_step = 0.12
damping = 0.05
second = 0.5 * STEPS * time_step * time_step

NEAR = 4.0 / 3.0
FAR = -1.0 / 12.0

TILE = 8
WIDE = 6
MID = 4

VMEM = pl.BlockSpec(memory_space=pltpu.VMEM)
SMEM = pl.BlockSpec(memory_space=pltpu.SMEM)


def spec(*shape):
    return jax.ShapeDtypeStruct(shape, jnp.float32)


def call(kernel, outs, args, scalars=(), scratch=(), flops=0):
    moved = 4 * (sum(a.size for a in args) + sum(o.size for o in outs))
    return pl.pallas_call(
        kernel,
        out_shape=outs,
        in_specs=[SMEM] * len(scalars) + [VMEM] * len(args),
        out_specs=[VMEM] * len(outs),
        scratch_shapes=[pltpu.VMEM(shape, jnp.float32) for shape in scratch],
        compiler_params=pltpu.CompilerParams(vmem_limit_bytes=10 << 20),
        cost_estimate=pl.CostEstimate(flops=flops, bytes_accessed=moved, transcendentals=0),
    )(*scalars, *args)


def lap(ref, i):
    w = ref[i]
    rows, depth = w.shape
    near = ref[i - 1] + ref[i + 1]
    far = ref[i - 2] + ref[i + 2]
    near += pltpu.roll(w, 1, 1) + pltpu.roll(w, depth - 1, 1)
    far += pltpu.roll(w, 2, 1) + pltpu.roll(w, depth - 2, 1)
    near += pltpu.roll(w, 1, 0) + pltpu.roll(w, rows - 1, 0)
    far += pltpu.roll(w, 2, 0) + pltpu.roll(w, rows - 2, 0)
    return -7.5 * w + NEAR * near + FAR * far


def widen(out, width, centre, yl, yh, at, xl, xh, x_at, cl, ch, c_at):
    planes, half, depth = centre.shape
    inner = pl.ds(width, planes)
    out[inner, 0:TILE, :] = yl[pl.ds(at, planes)]
    out[inner, TILE : TILE + half, :] = centre[...]
    out[inner, TILE + half :, :] = yh[pl.ds(at, planes)]
    near = width - 2
    for side, x, c in ((0, xl, cl), (width + planes, xh, ch)):
        out[pl.ds(side, width), TILE : TILE + half, :] = x[pl.ds(x_at, width)]
        corner = side + (2 if side == 0 else 0)
        beyond = side + (0 if side == 0 else near)
        for rows in (slice(0, TILE), slice(TILE + half, None)):
            out[pl.ds(corner, near), rows, :] = c[pl.ds(c_at, near)]
            out[pl.ds(beyond, 2), rows, :] = jnp.zeros((2, TILE, depth), jnp.float32)


def pack_first(h, u, v, s, y_up, y_down, x_up, x_down):
    planes, rows, depth = u.shape
    half = rows // 2
    start = h[0] * half
    low = pl.ds(pl.multiple_of(start, TILE), TILE)
    high = pl.ds(pl.multiple_of(start + half - TILE, TILE), TILE)
    own = pl.ds(pl.multiple_of(start, TILE), half)
    at = 0
    for k, (f, width) in enumerate(((u, WIDE), (v, WIDE), (s, MID))):
        part = pl.ds(k * planes, planes)
        y_up[part] = f[:, high, :]
        y_down[part] = f[:, low, :]
        x_up[pl.ds(at, width)] = f[planes - width :, own, :]
        x_down[pl.ds(at, width)] = f[0:width, own, :]
        at += width


def pack_edges(v, q, y_up, y_down, x_up, x_down):
    planes, half, depth = v.shape
    at = 0
    for k, (f, width) in enumerate(((v, WIDE), (q, MID))):
        part = pl.ds(k * planes, planes)
        y_up[part] = f[:, half - TILE :, :]
        y_down[part] = f[:, 0:TILE, :]
        x_up[pl.ds(at, width)] = f[planes - width :]
        x_down[pl.ds(at, width)] = f[0:width]
        at += width


def pack_corners(widths, planes, yl, yh, c_up, c_down):
    depth = yl.shape[-1]
    below = lax.broadcasted_iota(jnp.int32, (TILE, depth), 0) >= TILE // 2
    at = 0
    for k, width in enumerate(widths):
        count = width - 2
        for i in range(count):
            top = k * planes + planes - count + i
            c_up[at + i] = jnp.where(below, yl[top], yh[top])
            c_down[at + i] = jnp.where(below, yl[k * planes + i], yh[k * planes + i])
        at += count


def two_steps(planes, half, v0, q0, s, v1, q1, v2, q2):
    for i in range(planes + 2 * MID):
        l = lap(v0, i + 2)
        v1[i] = v0[i + 2] + time_step * (s[i] * q0[i] + damping * l)
        if 2 <= i < planes + 2 * MID - 2:
            q1[i - 2] = q0[i] + time_step * l
    for i in range(planes + 4):
        l = lap(v1, i + 2)
        v2[i] = v1[i + 2] + time_step * (s[i + 2] * q1[i] + damping * l)
        if 2 <= i < planes + 2:
            q2[i - 2] = q1[i] + time_step * l


def third_step(planes, half, u_of, v0, v1, v2, q2, s, u_out, v_out, q_out):
    own = slice(TILE, TILE + half)
    for i in range(planes):
        l = lap(v2, i + 2)[own]
        v_out[i] = v2[i + 2, own, :] + time_step * (s[i + MID, own, :] * q2[i, own, :] + damping * l)
        q_out[i] = q2[i, own, :] + time_step * l
        moved = v0[i + WIDE, own, :] + v1[i + MID, own, :] + v2[i + 2, own, :]
        u_out[i] = u_of(i) + time_step * moved


def first_steps(h, u, v, s, yl, yh, xl, xh, cl, ch, u_out, v_out, q_out, s_wide, *rest):
    sends, (u0, v0, q0, v1, q1, v2, q2) = rest[:4], rest[4:]
    planes, rows, depth = u.shape
    half = rows // 2
    own = pl.ds(pl.multiple_of(h[0] * half, TILE), half)
    widen(u0, WIDE, u.at[:, own, :], yl, yh, 0, xl, xh, 0, cl, ch, 0)
    widen(v0, WIDE, v.at[:, own, :], yl, yh, planes, xl, xh, WIDE, cl, ch, WIDE - 2)
    widen(s_wide, MID, s.at[:, own, :], yl, yh, 2 * planes, xl, xh, 2 * WIDE, cl, ch, 2 * WIDE - 4)
    for i in range(planes + 2 * MID):
        q0[i] = lap(u0, i + 2)
    two_steps(planes, half, v0, q0, s_wide, v1, q1, v2, q2)
    third_step(
        planes, half, lambda i: u[i, own, :], v0, v1, v2, q2, s_wide, u_out, v_out, q_out
    )
    pack_edges(v_out, q_out, *sends)


def widen_both(v, q, yl, yh, xl, xh, cl, ch, v0, q0):
    planes = v.shape[0]
    widen(v0, WIDE, v, yl, yh, 0, xl, xh, 0, cl, ch, 0)
    widen(q0, MID, q, yl, yh, planes, xl, xh, WIDE, cl, ch, WIDE - 2)


def middle_steps(u, v, q, s_wide, yl, yh, xl, xh, cl, ch, u_out, v_out, q_out, *rest):
    sends, (v0, q0, v1, q1, v2, q2) = rest[:4], rest[4:]
    planes, half, depth = v.shape
    widen_both(v, q, yl, yh, xl, xh, cl, ch, v0, q0)
    two_steps(planes, half, v0, q0, s_wide, v1, q1, v2, q2)
    third_step(planes, half, lambda i: u[i], v0, v1, v2, q2, s_wide, u_out, v_out, q_out)
    pack_edges(v_out, q_out, *sends)


def last_steps(scale, u, v, q, s_wide, yl, yh, xl, xh, cl, ch, keep, send, *scratch):
    v0, q0, v1, q1, rate, l7 = scratch
    planes, half, depth = v.shape
    own = slice(TILE, TILE + half)
    widen_both(v, q, yl, yh, xl, xh, cl, ch, v0, q0)
    for i in range(planes + 2 * MID):
        l = lap(v0, i + 2)
        v1[i] = v0[i + 2] + time_step * (s_wide[i] * q0[i] + damping * l)
        if 2 <= i < planes + 2 * MID - 2:
            q1[i - 2] = q0[i] + time_step * l
    for i in range(planes + 4):
        l = lap(v1, i + 2)
        rate[i] = s_wide[i + 2] * q1[i] + damping * l
        if 2 <= i < planes + 2:
            l7[i - 2] = l[own]
    for i in range(planes):
        l = lap(rate, i + 2)[own]
        r = rate[i + 2, own, :]
        u8 = u[i] + time_step * (v[i] + v1[i + MID, own, :])
        v8 = v1[i + MID, own, :] + time_step * r
        more = s_wide[i + MID, own, :] * l7[i] + damping * l
        keep[i] = u8 + scale[0] * r
        keep[planes + i] = v8 + scale[0] * more
        send[i] = u8 + scale[1] * r
        send[planes + i] = v8 + scale[1] * more


def join(h, keep, got, out_u, out_v):
    planes, rows, depth = out_u.shape
    half = rows // 2
    own = pl.ds(pl.multiple_of(h[0] * half, TILE), half)
    other = pl.ds(pl.multiple_of((1 - h[0]) * half, TILE), half)
    for k, out in enumerate((out_u, out_v)):
        part = pl.ds(k * planes, planes)
        out[:, own, :] = keep[part]
        out[:, other, :] = got[part]


def ring(count, step):
    return [(i, (i + step) % count) for i in range(count)]


def strips(gy, step):
    def place(t):
        j, h = divmod(t % (2 * gy), 2)
        return ((h + j) % 2) * gy + j

    return [(place(t), place(t + step)) for t in range(2 * gy)]


def exchange(sends, widths, planes):
    y_up, y_down, x_up, x_down = sends
    depth = y_up.shape[-1]
    gx, gy = lax.axis_size("gx"), lax.axis_size("gy")
    xl = lax.ppermute(x_up, "gx", ring(gx, 1))
    xh = lax.ppermute(x_down, "gx", ring(gx, -1))
    yl = lax.ppermute(y_up, ("level", "gy"), strips(gy, 1))
    yh = lax.ppermute(y_down, ("level", "gy"), strips(gy, -1))
    count = sum(width - 2 for width in widths)

    def corners(*refs):
        pack_corners(widths, planes, *refs)

    c_up, c_down = call(corners, [spec(count, TILE, depth)] * 2, (yl, yh))
    cl = lax.ppermute(c_up, "gx", ring(gx, 1))
    ch = lax.ppermute(c_down, "gx", ring(gx, -1))
    return yl, yh, xl, xh, cl, ch


def edge_specs(planes, half, depth, widths):
    y = spec(len(widths) * planes, TILE, depth)
    x = spec(sum(widths), half, depth)
    return [y, y, x, x]


def body(u, v, s):
    planes, rows, depth = u.shape
    half = rows // 2
    assert lax.axis_size("level") == 2 and planes >= WIDE and half % TILE == 0
    level = lax.axis_index("level")
    h = ((level + lax.axis_index("gy")) % 2).astype(jnp.int32).reshape(1)
    mine = jnp.where(level == 0, 0.0, second).astype(jnp.float32)
    scale = jnp.stack([mine, second - mine])

    tall = half + 2 * TILE
    block = spec(planes, half, depth)
    wide = (planes + 2 * WIDE, tall, depth)
    mid = (planes + 2 * MID, tall, depth)
    thin = (planes + 4, tall, depth)
    bare = (planes, tall, depth)
    work = 100 * u.size
    first, later = (WIDE, WIDE, MID), (WIDE, MID)
    sent = edge_specs(planes, half, depth, later)

    sends = call(pack_first, edge_specs(planes, half, depth, first), (u, v, s), (h,))
    halos = exchange(sends, first, planes)
    u1, v1, q1, s_wide, *sends = call(
        first_steps,
        [block] * 3 + [spec(*mid)] + sent,
        (u, v, s, *halos),
        (h,),
        (wide, wide, mid, mid, thin, thin, bare),
        work,
    )
    halos = exchange(sends, later, planes)
    u2, v2, q2, *sends = call(
        middle_steps,
        [block] * 3 + sent,
        (u1, v1, q1, s_wide, *halos),
        (),
        (wide, mid, mid, thin, thin, bare),
        work,
    )
    halos = exchange(sends, later, planes)
    both = spec(2 * planes, half, depth)
    keep, send = call(
        last_steps,
        [both, both],
        (u2, v2, q2, s_wide, *halos),
        (scale,),
        (wide, mid, mid, thin, thin, (planes, half, depth)),
        work,
    )
    got = lax.ppermute(send, "level", ring(2, 1))
    out_u, out_v = call(join, [spec(planes, rows, depth)] * 2, (keep, got), (h,))
    return out_u[None], out_v[None]


def solution(mesh):
    placed = (P("gx", "gy", None),) * 3
    return jax.shard_map(
        body,
        mesh=mesh,
        in_specs=placed,
        out_specs=(P("level", "gx", "gy", None), P("level", "gx", "gy", None)),
        check_vma=False,
    )
```

time: 208 us -> 65.9 us (0.32)
  waiting for transfers between devices: 114 us -> 26.8 us
  other arithmetic: 30.3 us -> 0.07 us
  starting transfers between devices: 52.3 us -> 29.8 us
  local copies, waits for them, and re-layouts: 9.76 us -> 2.86 us
  Pallas kernels: 0 us -> 5.43 us
    ppermute x36 -> x19, waiting for transfers between devices: 114 us -> 26.8 us  [the longest x3 8.93 us: exchange(): xh = lax.ppermute(x_down, 'gx', ring(gx, -1))]
    ppermute x36 -> x19, starting transfers between devices: 52.3 us -> 29.8 us  [the longest x3 8.92 us: exchange(): ch = lax.ppermute(c_down, 'gx', ring(gx, -1))]
    sub x9 -> x0, other arithmetic: 13.2 us -> none  [stencil(): total = total + 4.0 / 3.0 * near_z - far_z / 12.0]
    slice x40 -> x0, local copies, waits for them, and re-layouts: 9.47 us -> none  [the longest x16 4.59 us: stencil(): far_z = jnp.roll(centre, 2, 3) + jnp.roll(centre, -2, 3)]
    concatenate x18 -> x0, other arithmetic: 7.69 us -> none  [with_halo(): block = jnp.concatenate([low, block, high], axis=dim)]
    another operation x21 -> x1, other arithmetic: 6.12 us -> 0.07 us  [body(): scale = jnp.stack([mine, second - mine])]
    pallas_call x0 -> x8, Pallas kernels: none -> 5.43 us  [call(): pl.pallas_call(kernel, out_shape=outs, in_specs=[SMEM] * len(scalars) + [...]
    unnamed x6 -> x12, local copies, waits for them, and re-layouts: 0.29 us -> 2.86 us
  transfers between devices with their start and end apart: 36 -> 19, of which waited for: 27 -> 13; matrix products, arithmetic and copies ran while one was open for 3% -> 0% of each run, Pallas kernels for 0% -> 0%
where the time goes in v2:
time: 65.9 us; the launch traced here: 65.7 us
  starting transfers between devices  29.8 us (45%)
  waiting for transfers between devices  26.8 us (41%)
  Pallas kernels  5.43 us (8%)
  local copies, waits for them, and re-layouts  2.86 us (4%)
  between operations  0.75 us (1%)
    ppermute x3, waiting for transfers between devices, exchange(): xh = lax.ppermute(x_down, 'gx', ring(gx, -1))  8.93 us
    ppermute x3, starting transfers between devices, exchange(): ch = lax.ppermute(c_down, 'gx', ring(gx, -1))  8.92 us
    ppermute x3, starting transfers between devices, exchange(): xh = lax.ppermute(x_down, 'gx', ring(gx, -1))  8.55 us
    ppermute x1, waiting for transfers between devices, body(): got = lax.ppermute(send, 'level', ring(2, 1))  6.36 us
    ppermute x3, waiting for transfers between devices, exchange(): cl = lax.ppermute(c_up, 'gx', ring(gx, 1))  5.59 us
    pallas_call x8, Pallas kernels, call(): pl.pallas_call(kernel, out_shape=outs, in_specs=[SMEM] * len(scalars) + [...  5.43 us
    ppermute x3, waiting for transfers between devices, exchange(): xl = lax.ppermute(x_up, 'gx', ring(gx, 1))  3.71 us
    ppermute x3, starting transfers between devices, exchange(): yl = lax.ppermute(y_up, ('level', 'gy'), strips(gy, 1))  3.59 us
  transfers between devices with their start and end apart: 19, of which 13 were waited for; matrix products, arithmetic and copies ran while one was open for 0% of the time, Pallas kernels for 0%

profile of v2, /device:TPU:0, one launch (start us, length us, event | category | flops | bytes accessed | tf_op | source)
XLA Modules:
  0.0 65.7 jit_solution(3229276608774853959)
XLA Ops:
  0.6 0.0 copy-start
  0.7 0.9 %copy-done = f32[8,32,256]{2,1,0:T(8,128)S(1)} copy-done((f32[8,32,256]{2,1,0:T(8,128)S(1)}, f32[8,32,256]{2,1,0:T(8,128)}, u32[]{:S(2)}) %copy-start) | copy-done | bytes 262168
  1.6 0.0 copy-start.2
  1.6 0.9 %copy-done.2 = f32[8,32,256]{2,1,0:T(8,128)S(1)} copy-done((f32[8,32,256]{2,1,0:T(8,128)S(1)}, f32[8,32,256]{2,1,0:T(8,128)}, u32[]{:S(2)}) %copy-start.2) | copy-done | bytes 262168
  2.5 0.0 copy-start.4
  2.5 0.9 %copy-done.4 = f32[8,32,256]{2,1,0:T(8,128)S(1)} copy-done((f32[8,32,256]{2,1,0:T(8,128)S(1)}, f32[8,32,256]{2,1,0:T(8,128)}, u32[]{:S(2)}) %copy-start.4) | copy-done | bytes 262168
  3.5 0.0 copy-start.3
  3.5 0.0 copy-start.5
  3.5 0.1 shard_map.50
  3.6 0.0 copy-start.1
  3.6 3.0 %collective-permute-start = (f32[24,8,256]{2,1,0:T(8,128)S(1)}, f32[24,8,256]{2,1,0:T(8,128)S(1)}, u32[]{:S(2)}, u32[]{:S(2)}) collective-permute-start(f32[24,8,256]{2,1,0:T(8,128)S(1)} %get-tuple-element.31), channel_id=1, source_target_pairs={{0,16},{16,17},{17,1},{1,2},{2,18},{18,19},{19,3},{3,0},{4,20},{20... | collective-permute-start | bytes 589832 | tf_op jit(solution)/shard_map/ppermute | solution.py:223
  6.6 0.0 collective-permute-start.1
  6.6 1.8 %collective-permute-start.2 = (f32[16,16,256]{2,1,0:T(8,128)S(1)}, f32[16,16,256]{2,1,0:T(8,128)S(1)}, u32[]{:S(2)}, u32[]{:S(2)}) collective-permute-start(f32[16,16,256]{2,1,0:T(8,128)S(1)} %get-tuple-element.33), channel_id=1, source_target_pairs={{0,4},{4,8},{8,12},{12,0},{1,5},{5,9},{9,13},{13,1},{2,6},{6,10},{... | collective-permute-start | bytes 786440 | tf_op jit(solution)/shard_map/ppermute | solution.py:221
  8.4 2.0 %collective-permute-start.3 = (f32[16,16,256]{2,1,0:T(8,128)S(1)}, f32[16,16,256]{2,1,0:T(8,128)S(1)}, u32[]{:S(2)}, u32[]{:S(2)}) collective-permute-start(f32[16,16,256]{2,1,0:T(8,128)S(1)} %get-tuple-element.34), channel_id=1, source_target_pairs={{0,12},{4,0},{8,4},{12,8},{1,13},{5,1},{9,5},{13,9},{2,14},{6,2},{... | collective-permute-start | bytes 786440 | tf_op jit(solution)/shard_map/ppermute | solution.py:222
  10.5 0.9 %collective-permute-done.refs_0_.yl = f32[24,8,256]{2,1,0:T(8,128)S(1)} collective-permute-done((f32[24,8,256]{2,1,0:T(8,128)S(1)}, f32[24,8,256]{2,1,0:T(8,128)S(1)}, u32[]{:S(2)}, u32[]{:S(2)}) %collective-permute-start) | collective-permute-done | bytes 196640 | tf_op jit(solution)/shard_map/ppermute | solution.py:223
  11.4 0.9 %collective-permute-done.1.refs_1_.yh = f32[24,8,256]{2,1,0:T(8,128)S(1)} collective-permute-done((f32[24,8,256]{2,1,0:T(8,128)S(1)}, f32[24,8,256]{2,1,0:T(8,128)S(1)}, u32[]{:S(2)}, u32[]{:S(2)}) %collective-permute-start.1) | collective-permute-done | bytes 196640 | tf_op jit(solution)/shard_map/ppermute | solution.py:224
  12.3 1.6 %collective-permute-start.4 = (f32[10,8,256]{2,1,0:T(8,128)S(1)}, f32[10,8,256]{2,1,0:T(8,128)S(1)}, u32[]{:S(2)}, u32[]{:S(2)}) collective-permute-start(f32[10,8,256]{2,1,0:T(8,128)S(1)} %get-tuple-element.35), channel_id=1, source_target_pairs={{0,4},{4,8},{8,12},{12,0},{1,5},{5,9},{9,13},{13,1},{2,6},{6,10},{... | collective-permute-start | bytes 245768 | tf_op jit(solution)/shard_map/ppermute | solution.py:231
  13.9 2.2 %collective-permute-start.5 = (f32[10,8,256]{2,1,0:T(8,128)S(1)}, f32[10,8,256]{2,1,0:T(8,128)S(1)}, u32[]{:S(2)}, u32[]{:S(2)}) collective-permute-start(f32[10,8,256]{2,1,0:T(8,128)S(1)} %get-tuple-element.36), channel_id=1, source_target_pairs={{0,12},{4,0},{8,4},{12,8},{1,13},{5,1},{9,5},{13,9},{2,14},{6,2},{... | collective-permute-start | bytes 245768 | tf_op jit(solution)/shard_map/ppermute | solution.py:232
  16.2 1.5 %collective-permute-done.2.xl = f32[16,16,256]{2,1,0:T(8,128)S(1)} collective-permute-done((f32[16,16,256]{2,1,0:T(8,128)S(1)}, f32[16,16,256]{2,1,0:T(8,128)S(1)}, u32[]{:S(2)}, u32[]{:S(2)}) %collective-permute-start.2) | collective-permute-done | bytes 262176 | tf_op jit(solution)/shard_map/ppermute | solution.py:221
  17.7 5.7 %collective-permute-done.3.xh = f32[16,16,256]{2,1,0:T(8,128)S(1)} collective-permute-done((f32[16,16,256]{2,1,0:T(8,128)S(1)}, f32[16,16,256]{2,1,0:T(8,128)S(1)}, u32[]{:S(2)}, u32[]{:S(2)}) %collective-permute-start.3) | collective-permute-done | bytes 262176 | tf_op jit(solution)/shard_map/ppermute | solution.py:222
  23.3 1.7 %collective-permute-done.4.cl = f32[10,8,256]{2,1,0:T(8,128)S(1)} collective-permute-done((f32[10,8,256]{2,1,0:T(8,128)S(1)}, f32[10,8,256]{2,1,0:T(8,128)S(1)}, u32[]{:S(2)}, u32[]{:S(2)}) %collective-permute-start.4) | collective-permute-done | bytes 81952 | tf_op jit(solution)/shard_map/ppermute | solution.py:231
  25.0 0.4 collective-permute-done.5.ch
  25.4 0.0 copy-done.3
  25.4 0.0 copy-done.5
  25.4 0.0 copy-done.1
  25.4 1.7 %shard_map.52 = (f32[8,16,256]{2,1,0:T(8,128)S(1)}, f32[8,16,256]{2,1,0:T(8,128)S(1)}, f32[8,16,256]{2,1,0:T(8,128)S(1)}, f32[16,32,256]{2,1,0:T(8,128)S(1)}, f3...) custom-call(s32[1]{0:T(128)} %bitcast.h, ...), custom_call_target="tpu_custom_call" | custom-call | flops 6553600 | bytes 3375104 | tf_op jit(solution)/shard_map/pallas_call | solution.py:31
  27.1 0.5 collective-permute-start.6
  27.6 1.3 %collective-permute-start.7 = (f32[16,8,256]{2,1,0:T(8,128)S(1)}, f32[16,8,256]{2,1,0:T(8,128)S(1)}, u32[]{:S(2)}, u32[]{:S(2)}) collective-permute-start(f32[16,8,256]{2,1,0:T(8,128)S(1)} %get-tuple-element.42), channel_id=1, source_target_pairs={{0,3},{16,0},{17,16},{1,17},{2,1},{18,2},{19,18},{3,19},{4,7},{20,... | collective-permute-start | bytes 393224 | tf_op jit(solution)/shard_map/ppermute | solution.py:224
  28.9 1.1 %collective-permute-start.8 = (f32[10,16,256]{2,1,0:T(8,128)S(1)}, f32[10,16,256]{2,1,0:T(8,128)S(1)}, u32[]{:S(2)}, u32[]{:S(2)}) collective-permute-start(f32[10,16,256]{2,1,0:T(8,128)S(1)} %get-tuple-element.43), channel_id=1, source_target_pairs={{0,4},{4,8},{8,12},{12,0},{1,5},{5,9},{9,13},{13,1},{2,6},{6,10},{... | collective-permute-start | bytes 491528 | tf_op jit(solution)/shard_map/ppermute | solution.py:221
  30.1 2.7 %collective-permute-start.9 = (f32[10,16,256]{2,1,0:T(8,128)S(1)}, f32[10,16,256]{2,1,0:T(8,128)S(1)}, u32[]{:S(2)}, u32[]{:S(2)}) collective-permute-start(f32[10,16,256]{2,1,0:T(8,128)S(1)} %get-tuple-element.44), channel_id=1, source_target_pairs={{0,12},{4,0},{8,4},{12,8},{1,13},{5,1},{9,5},{13,9},{2,14},{6,2},{... | collective-permute-start | bytes 491528 | tf_op jit(solution)/shard_map/ppermute | solution.py:222
  32.8 0.0 collective-permute-done.6.refs_0_.yl
  32.8 0.0 collective-permute-done.7.refs_1_.yh
  32.8 1.0 %collective-permute-start.10 = (f32[6,8,256]{2,1,0:T(8,128)S(1)}, f32[6,8,256]{2,1,0:T(8,128)S(1)}, u32[]{:S(2)}, u32[]{:S(2)}) collective-permute-start(f32[6,8,256]{2,1,0:T(8,128)S(1)} %get-tuple-element.45), channel_id=1, source_target_pairs={{0,4},{4,8},{8,12},{12,0},{1,5},{5,9},{9,13},{13,1},{2,6},{6,10},{... | collective-permute-start | bytes 147464 | tf_op jit(solution)/shard_map/ppermute | solution.py:231
  33.8 2.9 %collective-permute-start.11 = (f32[6,8,256]{2,1,0:T(8,128)S(1)}, f32[6,8,256]{2,1,0:T(8,128)S(1)}, u32[]{:S(2)}, u32[]{:S(2)}) collective-permute-start(f32[6,8,256]{2,1,0:T(8,128)S(1)} %get-tuple-element.46), channel_id=1, source_target_pairs={{0,12},{4,0},{8,4},{12,8},{1,13},{5,1},{9,5},{13,9},{2,14},{6,2},{... | collective-permute-start | bytes 147464 | tf_op jit(solution)/shard_map/ppermute | solution.py:232
  36.7 1.1 %collective-permute-done.8.xl = f32[10,16,256]{2,1,0:T(8,128)S(1)} collective-permute-done((f32[10,16,256]{2,1,0:T(8,128)S(1)}, f32[10,16,256]{2,1,0:T(8,128)S(1)}, u32[]{:S(2)}, u32[]{:S(2)}) %collective-permute-start.8) | collective-permute-done | bytes 163872 | tf_op jit(solution)/shard_map/ppermute | solution.py:221
  37.8 2.4 %collective-permute-done.9.xh = f32[10,16,256]{2,1,0:T(8,128)S(1)} collective-permute-done((f32[10,16,256]{2,1,0:T(8,128)S(1)}, f32[10,16,256]{2,1,0:T(8,128)S(1)}, u32[]{:S(2)}, u32[]{:S(2)}) %collective-permute-start.9) | collective-permute-done | bytes 163872 | tf_op jit(solution)/shard_map/ppermute | solution.py:222
  40.2 1.3 %collective-permute-done.10.cl = f32[6,8,256]{2,1,0:T(8,128)S(1)} collective-permute-done((f32[6,8,256]{2,1,0:T(8,128)S(1)}, f32[6,8,256]{2,1,0:T(8,128)S(1)}, u32[]{:S(2)}, u32[]{:S(2)}) %collective-permute-start.10) | collective-permute-done | bytes 49184 | tf_op jit(solution)/shard_map/ppermute | solution.py:231
  41.5 0.0 collective-permute-done.11.ch
  41.5 1.1 %shard_map.54 = (f32[8,16,256]{2,1,0:T(8,128)S(1)}, f32[8,16,256]{2,1,0:T(8,128)S(1)}, f32[8,16,256]{2,1,0:T(8,128)S(1)}, f32[16,8,256]{2,1,0:T(8,128)S(1)}, f32...) custom-call(f32[8,16,256]{2,1,0:T(8,128)S(1)} %get-tuple-element.37.u, ...), custom_call_target="tpu_custom_call" | custom-call | flops 6553600 | bytes 2588672 | tf_op jit(solution)/shard_map/pallas_call | solution.py:31
  42.7 0.1 collective-permute-start.12
  42.7 1.7 %collective-permute-start.13 = (f32[16,8,256]{2,1,0:T(8,128)S(1)}, f32[16,8,256]{2,1,0:T(8,128)S(1)}, u32[]{:S(2)}, u32[]{:S(2)}) collective-permute-start(f32[16,8,256]{2,1,0:T(8,128)S(1)} %get-tuple-element.51), channel_id=1, source_target_pairs={{0,3},{16,0},{17,16},{1,17},{2,1},{18,2},{19,18},{3,19},{4,7},{20,... | collective-permute-start | bytes 393224 | tf_op jit(solution)/shard_map/ppermute | solution.py:224
  44.5 0.0 collective-permute-start.14
  44.5 3.8 %collective-permute-start.15 = (f32[10,16,256]{2,1,0:T(8,128)S(1)}, f32[10,16,256]{2,1,0:T(8,128)S(1)}, u32[]{:S(2)}, u32[]{:S(2)}) collective-permute-start(f32[10,16,256]{2,1,0:T(8,128)S(1)} %get-tuple-element.53), channel_id=1, source_target_pairs={{0,12},{4,0},{8,4},{12,8},{1,13},{5,1},{9,5},{13,9},{2,14},{6,2},{... | collective-permute-start | bytes 491528 | tf_op jit(solution)/shard_map/ppermute | solution.py:222
  48.3 0.0 collective-permute-done.12.refs_0_.yl
  48.3 0.0 collective-permute-done.13.refs_1_.yh
  48.3 0.1 collective-permute-start.16
  48.4 3.8 %collective-permute-start.17 = (f32[6,8,256]{2,1,0:T(8,128)S(1)}, f32[6,8,256]{2,1,0:T(8,128)S(1)}, u32[]{:S(2)}, u32[]{:S(2)}) collective-permute-start(f32[6,8,256]{2,1,0:T(8,128)S(1)} %get-tuple-element.55), channel_id=1, source_target_pairs={{0,12},{4,0},{8,4},{12,8},{1,13},{5,1},{9,5},{13,9},{2,14},{6,2},{... | collective-permute-start | bytes 147464 | tf_op jit(solution)/shard_map/ppermute | solution.py:232
  52.2 0.1 pad_maximum_fusion.scale
  52.3 1.1 %collective-permute-done.14.xl = f32[10,16,256]{2,1,0:T(8,128)S(1)} collective-permute-done((f32[10,16,256]{2,1,0:T(8,128)S(1)}, f32[10,16,256]{2,1,0:T(8,128)S(1)}, u32[]{:S(2)}, u32[]{:S(2)}) %collective-permute-start.14) | collective-permute-done | bytes 163872 | tf_op jit(solution)/shard_map/ppermute | solution.py:221
  53.4 0.9 %collective-permute-done.15.xh = f32[10,16,256]{2,1,0:T(8,128)S(1)} collective-permute-done((f32[10,16,256]{2,1,0:T(8,128)S(1)}, f32[10,16,256]{2,1,0:T(8,128)S(1)}, u32[]{:S(2)}, u32[]{:S(2)}) %collective-permute-start.15) | collective-permute-done | bytes 163872 | tf_op jit(solution)/shard_map/ppermute | solution.py:222
  54.2 2.6 %collective-permute-done.16.cl = f32[6,8,256]{2,1,0:T(8,128)S(1)} collective-permute-done((f32[6,8,256]{2,1,0:T(8,128)S(1)}, f32[6,8,256]{2,1,0:T(8,128)S(1)}, u32[]{:S(2)}, u32[]{:S(2)}) %collective-permute-start.16) | collective-permute-done | bytes 49184 | tf_op jit(solution)/shard_map/ppermute | solution.py:231
  56.8 0.0 collective-permute-done.17.ch
  56.8 1.7 %shard_map.56 = (f32[16,16,256]{2,1,0:T(8,128)S(1)}, f32[16,16,256]{2,1,0:T(8,128)S(1)}) custom-call(f32[2]{0:T(128)S(1)} %pad_maximum_fusion.scale, f32[8,16,256]{2,1,0:T(8,128)S(1)} %get-tuple-element.47.u, f32[8,16,256]{2,1,0:T(8,128)S(1)} %get-tuple-element.48.v, f32[8,16,256]{2,1,0:T(8,128)S(1)} %get-tuple-element.49.q, ...), custom_call_target="tpu_custom_call" | custom-call | flops 6553600 | bytes 2129920 | tf_op jit(solution)/shard_map/pallas_call | solution.py:31
  58.4 0.1 collective-permute-start.18
  58.5 6.4 %collective-permute-done.18.got = f32[16,16,256]{2,1,0:T(8,128)S(1)} collective-permute-done((f32[16,16,256]{2,1,0:T(8,128)S(1)}, f32[16,16,256]{2,1,0:T(8,128)S(1)}, u32[]{:S(2)}, u32[]{:S(2)}) %collective-permute-start.18) | collective-permute-done | bytes 262176 | tf_op jit(solution)/shard_map/ppermute | solution.py:290
  64.9 0.8 %shard_map.57 = (f32[8,32,256]{2,1,0:T(8,128)}, f32[8,32,256]{2,1,0:T(8,128)}) custom-call(s32[1]{0:T(128)} %bitcast.h, f32[16,16,256]{2,1,0:T(8,128)S(1)} %get-tuple-element.56.keep, f32[16,16,256]{2,1,0:T(8,128)S(1)} %collective-permute-done.18.got), custom_call_target="tpu_custom_call" | custom-call | bytes 1048576 | tf_op jit(solution)/shard_map/pallas_call | solution.py:31
  (3 shorter events, 0.0 us)
Async XLA Ops:
  0.6 1.0 %copy-start = (f32[8,32,256]{2,1,0:T(8,128)S(1)}, f32[8,32,256]{2,1,0:T(8,128)}, u32[]{:S(2)}) copy-start(f32[8,32,256]{2,1,0:T(8,128)} %u.3) | copy-start | bytes 786436
  1.6 0.9 %copy-start.2 = (f32[8,32,256]{2,1,0:T(8,128)S(1)}, f32[8,32,256]{2,1,0:T(8,128)}, u32[]{:S(2)}) copy-start(f32[8,32,256]{2,1,0:T(8,128)} %v.3) | copy-start | bytes 786436
  2.5 0.9 %copy-start.4 = (f32[8,32,256]{2,1,0:T(8,128)S(1)}, f32[8,32,256]{2,1,0:T(8,128)}, u32[]{:S(2)}) copy-start(f32[8,32,256]{2,1,0:T(8,128)} %s.3) | copy-start | bytes 786436
  3.5 21.9 %copy-start.3 = (f32[8,32,256]{2,1,0:T(8,128)S(1)}, f32[8,32,256]{2,1,0:T(8,128)}, u32[]{:S(2)}) copy-start(f32[8,32,256]{2,1,0:T(8,128)} %v.3) | copy-start | bytes 786436
  3.5 21.9 %copy-start.5 = (f32[8,32,256]{2,1,0:T(8,128)S(1)}, f32[8,32,256]{2,1,0:T(8,128)}, u32[]{:S(2)}) copy-start(f32[8,32,256]{2,1,0:T(8,128)} %s.3) | copy-start | bytes 786436
  3.6 21.8 %copy-start.1 = (f32[8,32,256]{2,1,0:T(8,128)S(1)}, f32[8,32,256]{2,1,0:T(8,128)}, u32[]{:S(2)}) copy-start(f32[8,32,256]{2,1,0:T(8,128)} %u.3) | copy-start | bytes 786436
  3.6 7.8 %collective-permute-start = (f32[24,8,256]{2,1,0:T(8,128)S(1)}, f32[24,8,256]{2,1,0:T(8,128)S(1)}, u32[]{:S(2)}, u32[]{:S(2)}) collective-permute-start(f32[24,8,256]{2,1,0:T(8,128)S(1)} %get-tuple-element.31), channel_id=1, source_target_pairs={{0,16},{16,17},{17,1},{1,2},{2,18},{18,19},{19,3},{3,0},{4,20},{20... | collective-permute-start | bytes 589832 | tf_op jit(solution)/shard_map/ppermute | solution.py:223
  6.6 5.7 %collective-permute-start.1 = (f32[24,8,256]{2,1,0:T(8,128)S(1)}, f32[24,8,256]{2,1,0:T(8,128)S(1)}, u32[]{:S(2)}, u32[]{:S(2)}) collective-permute-start(f32[24,8,256]{2,1,0:T(8,128)S(1)} %get-tuple-element.32), channel_id=1, source_target_pairs={{0,3},{16,0},{17,16},{1,17},{2,1},{18,2},{19,18},{3,19},{4,7},{20,... | collective-permute-start | bytes 589832 | tf_op jit(solution)/shard_map/ppermute | solution.py:224
  6.6 11.1 %collective-permute-start.2 = (f32[16,16,256]{2,1,0:T(8,128)S(1)}, f32[16,16,256]{2,1,0:T(8,128)S(1)}, u32[]{:S(2)}, u32[]{:S(2)}) collective-permute-start(f32[16,16,256]{2,1,0:T(8,128)S(1)} %get-tuple-element.33), channel_id=1, source_target_pairs={{0,4},{4,8},{8,12},{12,0},{1,5},{5,9},{9,13},{13,1},{2,6},{6,10},{... | collective-permute-start | bytes 786440 | tf_op jit(solution)/shard_map/ppermute | solution.py:221
  8.4 14.9 %collective-permute-start.3 = (f32[16,16,256]{2,1,0:T(8,128)S(1)}, f32[16,16,256]{2,1,0:T(8,128)S(1)}, u32[]{:S(2)}, u32[]{:S(2)}) collective-permute-start(f32[16,16,256]{2,1,0:T(8,128)S(1)} %get-tuple-element.34), channel_id=1, source_target_pairs={{0,12},{4,0},{8,4},{12,8},{1,13},{5,1},{9,5},{13,9},{2,14},{6,2},{... | collective-permute-start | bytes 786440 | tf_op jit(solution)/shard_map/ppermute | solution.py:222
  12.3 12.7 %collective-permute-start.4 = (f32[10,8,256]{2,1,0:T(8,128)S(1)}, f32[10,8,256]{2,1,0:T(8,128)S(1)}, u32[]{:S(2)}, u32[]{:S(2)}) collective-permute-start(f32[10,8,256]{2,1,0:T(8,128)S(1)} %get-tuple-element.35), channel_id=1, source_target_pairs={{0,4},{4,8},{8,12},{12,0},{1,5},{5,9},{9,13},{13,1},{2,6},{6,10},{... | collective-permute-start | bytes 245768 | tf_op jit(solution)/shard_map/ppermute | solution.py:231
  13.9 11.5 %collective-permute-start.5 = (f32[10,8,256]{2,1,0:T(8,128)S(1)}, f32[10,8,256]{2,1,0:T(8,128)S(1)}, u32[]{:S(2)}, u32[]{:S(2)}) collective-permute-start(f32[10,8,256]{2,1,0:T(8,128)S(1)} %get-tuple-element.36), channel_id=1, source_target_pairs={{0,12},{4,0},{8,4},{12,8},{1,13},{5,1},{9,5},{13,9},{2,14},{6,2},{... | collective-permute-start | bytes 245768 | tf_op jit(solution)/shard_map/ppermute | solution.py:232
  27.1 5.6 %collective-permute-start.6 = (f32[16,8,256]{2,1,0:T(8,128)S(1)}, f32[16,8,256]{2,1,0:T(8,128)S(1)}, u32[]{:S(2)}, u32[]{:S(2)}) collective-permute-start(f32[16,8,256]{2,1,0:T(8,128)S(1)} %get-tuple-element.41), channel_id=1, source_target_pairs={{0,16},{16,17},{17,1},{1,2},{2,18},{18,19},{19,3},{3,0},{4,20},{20... | collective-permute-start | bytes 393224 | tf_op jit(solution)/shard_map/ppermute | solution.py:223
  27.6 5.1 %collective-permute-start.7 = (f32[16,8,256]{2,1,0:T(8,128)S(1)}, f32[16,8,256]{2,1,0:T(8,128)S(1)}, u32[]{:S(2)}, u32[]{:S(2)}) collective-permute-start(f32[16,8,256]{2,1,0:T(8,128)S(1)} %get-tuple-element.42), channel_id=1, source_target_pairs={{0,3},{16,0},{17,16},{1,17},{2,1},{18,2},{19,18},{3,19},{4,7},{20,... | collective-permute-start | bytes 393224 | tf_op jit(solution)/shard_map/ppermute | solution.py:224
  28.9 8.9 %collective-permute-start.8 = (f32[10,16,256]{2,1,0:T(8,128)S(1)}, f32[10,16,256]{2,1,0:T(8,128)S(1)}, u32[]{:S(2)}, u32[]{:S(2)}) collective-permute-start(f32[10,16,256]{2,1,0:T(8,128)S(1)} %get-tuple-element.43), channel_id=1, source_target_pairs={{0,4},{4,8},{8,12},{12,0},{1,5},{5,9},{9,13},{13,1},{2,6},{6,10},{... | collective-permute-start | bytes 491528 | tf_op jit(solution)/shard_map/ppermute | solution.py:221
  30.1 10.1 %collective-permute-start.9 = (f32[10,16,256]{2,1,0:T(8,128)S(1)}, f32[10,16,256]{2,1,0:T(8,128)S(1)}, u32[]{:S(2)}, u32[]{:S(2)}) collective-permute-start(f32[10,16,256]{2,1,0:T(8,128)S(1)} %get-tuple-element.44), channel_id=1, source_target_pairs={{0,12},{4,0},{8,4},{12,8},{1,13},{5,1},{9,5},{13,9},{2,14},{6,2},{... | collective-permute-start | bytes 491528 | tf_op jit(solution)/shard_map/ppermute | solution.py:222
  32.8 8.7 %collective-permute-start.10 = (f32[6,8,256]{2,1,0:T(8,128)S(1)}, f32[6,8,256]{2,1,0:T(8,128)S(1)}, u32[]{:S(2)}, u32[]{:S(2)}) collective-permute-start(f32[6,8,256]{2,1,0:T(8,128)S(1)} %get-tuple-element.45), channel_id=1, source_target_pairs={{0,4},{4,8},{8,12},{12,0},{1,5},{5,9},{9,13},{13,1},{2,6},{6,10},{... | collective-permute-start | bytes 147464 | tf_op jit(solution)/shard_map/ppermute | solution.py:231
  33.8 7.7 %collective-permute-start.11 = (f32[6,8,256]{2,1,0:T(8,128)S(1)}, f32[6,8,256]{2,1,0:T(8,128)S(1)}, u32[]{:S(2)}, u32[]{:S(2)}) collective-permute-start(f32[6,8,256]{2,1,0:T(8,128)S(1)} %get-tuple-element.46), channel_id=1, source_target_pairs={{0,12},{4,0},{8,4},{12,8},{1,13},{5,1},{9,5},{13,9},{2,14},{6,2},{... | collective-permute-start | bytes 147464 | tf_op jit(solution)/shard_map/ppermute | solution.py:232
  42.7 5.6 %collective-permute-start.12 = (f32[16,8,256]{2,1,0:T(8,128)S(1)}, f32[16,8,256]{2,1,0:T(8,128)S(1)}, u32[]{:S(2)}, u32[]{:S(2)}) collective-permute-start(f32[16,8,256]{2,1,0:T(8,128)S(1)} %get-tuple-element.50), channel_id=1, source_target_pairs={{0,16},{16,17},{17,1},{1,2},{2,18},{18,19},{19,3},{3,0},{4,20},{20... | collective-permute-start | bytes 393224 | tf_op jit(solution)/shard_map/ppermute | solution.py:223
  42.7 5.6 %collective-permute-start.13 = (f32[16,8,256]{2,1,0:T(8,128)S(1)}, f32[16,8,256]{2,1,0:T(8,128)S(1)}, u32[]{:S(2)}, u32[]{:S(2)}) collective-permute-start(f32[16,8,256]{2,1,0:T(8,128)S(1)} %get-tuple-element.51), channel_id=1, source_target_pairs={{0,3},{16,0},{17,16},{1,17},{2,1},{18,2},{19,18},{3,19},{4,7},{20,... | collective-permute-start | bytes 393224 | tf_op jit(solution)/shard_map/ppermute | solution.py:224
  44.5 8.9 %collective-permute-start.14 = (f32[10,16,256]{2,1,0:T(8,128)S(1)}, f32[10,16,256]{2,1,0:T(8,128)S(1)}, u32[]{:S(2)}, u32[]{:S(2)}) collective-permute-start(f32[10,16,256]{2,1,0:T(8,128)S(1)} %get-tuple-element.52), channel_id=1, source_target_pairs={{0,4},{4,8},{8,12},{12,0},{1,5},{5,9},{9,13},{13,1},{2,6},{6,10},{... | collective-permute-start | bytes 491528 | tf_op jit(solution)/shard_map/ppermute | solution.py:221
  44.5 9.7 %collective-permute-start.15 = (f32[10,16,256]{2,1,0:T(8,128)S(1)}, f32[10,16,256]{2,1,0:T(8,128)S(1)}, u32[]{:S(2)}, u32[]{:S(2)}) collective-permute-start(f32[10,16,256]{2,1,0:T(8,128)S(1)} %get-tuple-element.53), channel_id=1, source_target_pairs={{0,12},{4,0},{8,4},{12,8},{1,13},{5,1},{9,5},{13,9},{2,14},{6,2},{... | collective-permute-start | bytes 491528 | tf_op jit(solution)/shard_map/ppermute | solution.py:222
  48.3 8.5 %collective-permute-start.16 = (f32[6,8,256]{2,1,0:T(8,128)S(1)}, f32[6,8,256]{2,1,0:T(8,128)S(1)}, u32[]{:S(2)}, u32[]{:S(2)}) collective-permute-start(f32[6,8,256]{2,1,0:T(8,128)S(1)} %get-tuple-element.54), channel_id=1, source_target_pairs={{0,4},{4,8},{8,12},{12,0},{1,5},{5,9},{9,13},{13,1},{2,6},{6,10},{... | collective-permute-start | bytes 147464 | tf_op jit(solution)/shard_map/ppermute | solution.py:231
  48.4 8.4 %collective-permute-start.17 = (f32[6,8,256]{2,1,0:T(8,128)S(1)}, f32[6,8,256]{2,1,0:T(8,128)S(1)}, u32[]{:S(2)}, u32[]{:S(2)}) collective-permute-start(f32[6,8,256]{2,1,0:T(8,128)S(1)} %get-tuple-element.55), channel_id=1, source_target_pairs={{0,12},{4,0},{8,4},{12,8},{1,13},{5,1},{9,5},{13,9},{2,14},{6,2},{... | collective-permute-start | bytes 147464 | tf_op jit(solution)/shard_map/ppermute | solution.py:232
  58.4 6.4 %collective-permute-start.18 = (f32[16,16,256]{2,1,0:T(8,128)S(1)}, f32[16,16,256]{2,1,0:T(8,128)S(1)}, u32[]{:S(2)}, u32[]{:S(2)}) collective-permute-start(f32[16,16,256]{2,1,0:T(8,128)S(1)} %get-tuple-element.57), channel_id=1, source_target_pairs={{0,16},{16,0},{1,17},{17,1},{2,18},{18,2},{3,19},{19,3},{4,20},{20... | collective-permute-start | bytes 786440 | tf_op jit(solution)/shard_map/ppermute | solution.py:290

commit v3 on v2

v3 whole, which is shorter than its diff:
```python
import functools

import jax
import jax.numpy as jnp
from jax import lax
from jax.experimental import pallas as pl
from jax.experimental.pallas import tpu as pltpu
from jax.sharding import PartitionSpec as P


STEPS = 8

time_step = 0.12
damping = 0.05
second = 0.5 * STEPS * time_step * time_step

NEAR = 4.0 / 3.0
FAR = -1.0 / 12.0

TILE = 8
WIDE = 6
MID = 4

FIRST = (WIDE, WIDE, MID)
LATER = (WIDE, MID)

VMEM = pl.BlockSpec(memory_space=pltpu.VMEM)
SMEM = pl.BlockSpec(memory_space=pltpu.SMEM)


def spec(*shape):
    return jax.ShapeDtypeStruct(shape, jnp.float32)


def call(kernel, outs, args, scalars=(), scratch=(), flops=0):
    moved = 4 * (sum(a.size for a in args) + sum(o.size for o in outs))
    return pl.pallas_call(
        kernel,
        out_shape=outs,
        in_specs=[SMEM] * len(scalars) + [VMEM] * len(args),
        out_specs=[VMEM] * len(outs),
        scratch_shapes=[pltpu.VMEM(shape, jnp.float32) for shape in scratch],
        compiler_params=pltpu.CompilerParams(vmem_limit_bytes=10 << 20),
        cost_estimate=pl.CostEstimate(flops=flops, bytes_accessed=moved, transcendentals=0),
    )(*scalars, *args)


def lap(ref, i):
    w = ref[i]
    rows, depth = w.shape
    near = ref[i - 1] + ref[i + 1]
    far = ref[i - 2] + ref[i + 2]
    near += pltpu.roll(w, 1, 1) + pltpu.roll(w, depth - 1, 1)
    far += pltpu.roll(w, 2, 1) + pltpu.roll(w, depth - 2, 1)
    near += pltpu.roll(w, 1, 0) + pltpu.roll(w, rows - 1, 0)
    far += pltpu.roll(w, 2, 0) + pltpu.roll(w, rows - 2, 0)
    return -7.5 * w + NEAR * near + FAR * far


def first_rows(shape):
    return lax.broadcasted_iota(jnp.int32, shape, 0) < TILE // 2


def offsets(widths, change):
    return [sum(w + change for w in widths[:k]) for k in range(len(widths))]


def widen(out, k, widths, centre, halos):
    yl, yh, xla, xha, xlb, xhb = halos
    planes, half, depth = centre.shape
    width = widths[k]
    y_at, c_at = y_offsets(widths, planes)
    y_at, c_at = y_at[k], c_at[k]
    a_at, b_at = offsets(widths, -2)[k], offsets(widths, 2)[k]
    upper = first_rows((TILE, depth))
    none = jnp.zeros((TILE, depth), jnp.float32)
    for i in range(planes):
        for y, rows in ((yl, slice(0, TILE)), (yh, slice(TILE + half, None))):
            if width == WIDE:
                tile = y[y_at + i]
            elif i < planes // 2:
                tile = y[y_at + i]
            else:
                tile = pltpu.roll(y[y_at + i - planes // 2], TILE // 2, 0)
            out[width + i, rows, :] = tile
        out[width + i, TILE : TILE + half, :] = centre[i]
    for i in range(width):
        for low in (True, False):
            xa, xb = (xla, xlb) if low else (xha, xhb)
            j = i - 2 if low else i
            to = i if low else width + planes + i
            if 0 <= j < width - 2:
                a = xa[a_at + j]
                below, above = yl[c_at + j], yh[c_at + j]
                if not low:
                    below, above = pltpu.roll(below, TILE // 2, 0), pltpu.roll(above, TILE // 2, 0)
            else:
                a = xb[b_at + width + (i if low else j - (width - 2))]
                below = above = none
            b = xb[b_at + i]
            out[to, 0:TILE, :] = below
            out[to, TILE : 2 * TILE, :] = jnp.where(upper, a, b)
            out[to, 2 * TILE : 3 * TILE, :] = jnp.where(upper, b, a)
            out[to, 3 * TILE :, :] = above


def pack_x(fields, widths, sends):
    a_up, a_down, b_up, b_down = sends
    for k, (f, width) in enumerate(zip(fields, widths)):
        planes, _, depth = f.shape
        upper = first_rows((TILE, depth))
        a_at, b_at = offsets(widths, -2)[k], offsets(widths, 2)[k]
        for i in range(width):
            for up in (True, False):
                plane = planes - width + i if up else i
                xa, xb = (a_up, b_up) if up else (a_down, b_down)
                j = i - 2 if up else i
                first, last = f[plane, 0:TILE, :], f[plane, TILE:, :]
                a = jnp.where(upper, first, last)
                if 0 <= j < width - 2:
                    xa[a_at + j] = a
                else:
                    xb[b_at + width + (i if up else j - (width - 2))] = a
                xb[b_at + i] = jnp.where(upper, last, first)


def y_offsets(widths, planes):
    own, at = [], 0
    for width in widths:
        own.append(at)
        at += planes if width == WIDE else planes // 2
    corners = [at + c for c in offsets(widths, -2)]
    return own, corners


def y_length(widths, planes):
    return y_offsets(widths, planes)[1][-1] + widths[-1] - 2


def pack_y(widths, *refs):
    count = len(widths)
    fields, (xla, xha, y_up, y_down) = refs[:count], refs[count:]
    planes, _, depth = fields[0].shape
    own, corners = y_offsets(widths, planes)
    upper = first_rows((TILE, depth))

    def pair(at, last, first, last_turned, first_turned):
        y_up[at] = jnp.where(upper, pltpu.roll(last_turned, TILE // 2, 0), last)
        y_down[at] = jnp.where(upper, first, pltpu.roll(first_turned, TILE // 2, 0))

    for k, (f, width) in enumerate(zip(fields, widths)):
        if width == WIDE:
            y_up[pl.ds(own[k], planes)] = f[:, TILE:, :]
            y_down[pl.ds(own[k], planes)] = f[:, 0:TILE, :]
        else:
            for i in range(planes // 2):
                g = f.at[i + planes // 2]
                pair(own[k] + i, f[i, TILE:, :], f[i, 0:TILE, :], g[TILE:, :], g[0:TILE, :])
        for i in range(width - 2):
            low, high = xla[offsets(widths, -2)[k] + i], xha[offsets(widths, -2)[k] + i]
            pair(corners[k] + i, low, low, high, high)


def load_first(h, u, v, s, u_own, v_own, s_own, *rest):
    sends, sems = rest[:4], rest[4]
    half = u_own.shape[1]
    own = pl.ds(pl.multiple_of(h[0] * half, TILE), half)
    fields = (u_own, v_own, s_own)
    copies = [
        pltpu.make_async_copy(f.at[:, own, :], to, sems.at[k])
        for k, (f, to) in enumerate(zip((u, v, s), fields))
    ]
    for copy in copies:
        copy.start()
    for copy in copies:
        copy.wait()
    pack_x(fields, FIRST, sends)


def own_rows(i, count):
    return slice(TILE, 3 * TILE) if i < 2 or i >= count - 2 else slice(0, 4 * TILE)


def first_step(planes, v0, q0, s, v1, q1):
    count = planes + 2 * MID
    for i in range(count):
        rows = own_rows(i, count)
        l = lap(v0, i + 2)[rows]
        v1[i, rows, :] = v0[i + 2, rows, :] + time_step * (s[i, rows, :] * q0[i, rows, :] + damping * l)
        if 2 <= i < count - 2:
            q1[i - 2] = q0[i] + time_step * l


def two_steps(planes, v0, q0, s, v1, q1, v2, q2):
    first_step(planes, v0, q0, s, v1, q1)
    count = planes + 4
    own = slice(TILE, 3 * TILE)
    for i in range(count):
        rows = own_rows(i, count)
        l = lap(v1, i + 2)
        rate = s[i + 2, rows, :] * q1[i, rows, :] + damping * l[rows]
        v2[i, rows, :] = v1[i + 2, rows, :] + time_step * rate
        if 2 <= i < count - 2:
            q2[i - 2] = q1[i, own, :] + time_step * l[own]


def third_step(planes, u, v0, v1, v2, q2, s, u_out, v_out, q_out):
    own = slice(TILE, 3 * TILE)
    for i in range(planes):
        l = lap(v2, i + 2)[own]
        v_out[i] = v2[i + 2, own, :] + time_step * (s[i + MID, own, :] * q2[i] + damping * l)
        q_out[i] = q2[i] + time_step * l
        moved = v0[i + WIDE, own, :] + v1[i + MID, own, :] + v2[i + 2, own, :]
        u_out[i] = u[i] + time_step * moved


def first_steps(u, v, s, *rest):
    halos, (u_out, v_out, q_out, s_wide), sends = rest[:6], rest[6:10], rest[10:14]
    u0, v0, q0, v1, q1, v2, q2 = rest[14:]
    planes, _, _ = u.shape
    for k, (f, out) in enumerate(((u, u0), (v, v0), (s, s_wide))):
        widen(out, k, FIRST, f, halos)
    count = planes + 2 * MID
    for i in range(count):
        rows = own_rows(i, count)
        q0[i, rows, :] = lap(u0, i + 2)[rows]
    two_steps(planes, v0, q0, s_wide, v1, q1, v2, q2)
    third_step(planes, u, v0, v1, v2, q2, s_wide, u_out, v_out, q_out)
    pack_x((v_out, q_out), LATER, sends)


def middle_steps(u, v, q, s_wide, *rest):
    halos, (u_out, v_out, q_out), sends = rest[:6], rest[6:9], rest[9:13]
    v0, q0, v1, q1, v2, q2 = rest[13:]
    planes, _, _ = v.shape
    widen(v0, 0, LATER, v, halos)
    widen(q0, 1, LATER, q, halos)
    two_steps(planes, v0, q0, s_wide, v1, q1, v2, q2)
    third_step(planes, u, v0, v1, v2, q2, s_wide, u_out, v_out, q_out)
    pack_x((v_out, q_out), LATER, sends)


def last_steps(scale, u, v, q, s_wide, *rest):
    halos, (keep, send), (v0, q0, v1, q1, rate, l7) = rest[:6], rest[6:8], rest[8:]
    planes, _, _ = v.shape
    own = slice(TILE, 3 * TILE)
    widen(v0, 0, LATER, v, halos)
    widen(q0, 1, LATER, q, halos)
    first_step(planes, v0, q0, s_wide, v1, q1)
    count = planes + 4
    for i in range(count):
        rows = own_rows(i, count)
        l = lap(v1, i + 2)
        rate[i, rows, :] = s_wide[i + 2, rows, :] * q1[i, rows, :] + damping * l[rows]
        if 2 <= i < count - 2:
            l7[i - 2] = l[own]
    for i in range(planes):
        l = lap(rate, i + 2)[own]
        r = rate[i + 2, own, :]
        u8 = u[i] + time_step * (v[i] + v1[i + MID, own, :])
        v8 = v1[i + MID, own, :] + time_step * r
        more = s_wide[i + MID, own, :] * l7[i] + damping * l
        keep[i] = u8 + scale[0] * r
        keep[planes + i] = v8 + scale[0] * more
        send[i] = u8 + scale[1] * r
        send[planes + i] = v8 + scale[1] * more


def join(h, keep, got, out_u, out_v):
    planes, rows, _ = out_u.shape
    half = rows // 2
    own = pl.ds(pl.multiple_of(h[0] * half, TILE), half)
    other = pl.ds(pl.multiple_of((1 - h[0]) * half, TILE), half)
    for k, out in enumerate((out_u, out_v)):
        part = pl.ds(k * planes, planes)
        out[:, own, :] = keep[part]
        out[:, other, :] = got[part]


def ring(count, step):
    return [(i, (i + step) % count) for i in range(count)]


def strips(gy, step):
    def place(t):
        j, h = divmod(t % (2 * gy), 2)
        return ((h + j) % 2) * gy + j

    return [(place(t), place(t + step)) for t in range(2 * gy)]


STARTS = ("a_up", "a_down", "b_up", "b_down", "y_up", "y_down")


def exchange(fields, widths, sends):
    gx, gy = lax.axis_size("gx"), lax.axis_size("gy")
    planes, _, depth = fields[0].shape
    got = {}

    def move(name, sent, axis, pairs):
        got[name] = lax.ppermute(sent, axis, pairs)

    for name, sent in zip(STARTS, sends):
        move(name, sent, "gx", ring(gx, 1 if name.endswith("up") else -1))
    y = spec(y_length(widths, planes), TILE, depth)
    args = (*fields, got["a_up"], got["a_down"])
    y_up, y_down = call(functools.partial(pack_y, widths), [y, y], args)
    move("y_up", y_up, ("level", "gy"), strips(gy, 1))
    move("y_down", y_down, ("level", "gy"), strips(gy, -1))
    return [got[name] for name in ("y_up", "y_down", "a_up", "a_down", "b_up", "b_down")]


def edge_specs(depth, widths):
    counts = sum(w - 2 for w in widths), sum(w + 2 for w in widths)
    return [spec(count, TILE, depth) for count in counts for _ in range(2)]


def body(u, v, s):
    planes, rows, depth = u.shape
    half = rows // 2
    assert lax.axis_size("level") == 2 and planes >= WIDE and half == 2 * TILE
    level = lax.axis_index("level")
    h = ((level + lax.axis_index("gy")) % 2).astype(jnp.int32).reshape(1)
    mine = jnp.where(level == 0, 0.0, second).astype(jnp.float32)
    scale = jnp.stack([mine, second - mine])

    tall = half + 2 * TILE
    block = spec(planes, half, depth)
    wide = (planes + 2 * WIDE, tall, depth)
    mid = (planes + 2 * MID, tall, depth)
    thin = (planes + 4, tall, depth)
    bare = (planes, half, depth)
    work = 100 * u.size
    sent = edge_specs(depth, LATER)

    outs = [block] * 3 + edge_specs(depth, FIRST)
    u, v, s, *sends = pl.pallas_call(
        load_first,
        out_shape=outs,
        in_specs=[SMEM] + [pl.BlockSpec(memory_space=pltpu.HBM)] * 3,
        out_specs=[VMEM] * len(outs),
        scratch_shapes=[pltpu.SemaphoreType.DMA((3,))],
        compiler_params=pltpu.CompilerParams(vmem_limit_bytes=10 << 20),
    )(h, *(pltpu.with_memory_space_constraint(f, pltpu.HBM) for f in (u, v, s)))
    halos = exchange((u, v, s), FIRST, sends)
    u, v, q, s_wide, *sends = call(
        first_steps,
        [block] * 3 + [spec(*mid)] + sent,
        (u, v, s, *halos),
        (),
        (wide, wide, mid, mid, thin, thin, bare),
        work,
    )
    halos = exchange((v, q), LATER, sends)
    u, v, q, *sends = call(
        middle_steps,
        [block] * 3 + sent,
        (u, v, q, s_wide, *halos),
        (),
        (wide, mid, mid, thin, thin, bare),
        work,
    )
    halos = exchange((v, q), LATER, sends)
    both = spec(2 * planes, half, depth)
    keep, send = call(
        last_steps,
        [both, both],
        (u, v, q, s_wide, *halos),
        (scale,),
        (wide, mid, mid, thin, thin, (planes, half, depth)),
        work,
    )
    got = lax.ppermute(send, "level", ring(2, 1))
    out_u, out_v = call(join, [spec(planes, rows, depth)] * 2, (keep, got), (h,))
    return out_u[None], out_v[None]


def solution(mesh):
    placed = (P("gx", "gy", None),) * 3
    return jax.shard_map(
        body,
        mesh=mesh,
        in_specs=placed,
        out_specs=(P("level", "gx", "gy", None), P("level", "gx", "gy", None)),
        check_vma=False,
    )
```

time: 65.9 us -> 67 us (1.017)
  local copies, waits for them, and re-layouts: 2.86 us -> 0 us
  waiting for transfers between devices: 26.8 us -> 29.3 us
  Pallas kernels: 5.43 us -> 6.6 us
    unnamed x12 -> x0, local copies, waits for them, and re-layouts: 2.86 us -> none
    ppermute x18, waiting for transfers between devices: 20.4 us -> 23 us  [move(): got[name] = lax.ppermute(sent, axis, pairs)]
    pallas_call x0 -> x1, Pallas kernels: none -> 1.1 us  [body(): pl.pallas_call(load_first, out_shape=outs, in_specs=[SMEM] + [pl.BlockSpe...]
    pallas_call x8 -> x7, Pallas kernels: 5.43 us -> 5.51 us  [call(): pl.pallas_call(kernel, out_shape=outs, in_specs=[SMEM] * len(scalars) + [...]
  transfers between devices with their start and end apart: 19 -> 19, of which waited for: 13 -> 10; matrix products, arithmetic and copies ran while one was open for 0% -> 0% of each run, Pallas kernels for 0% -> 0%
where the time goes in v3:
time: 67 us; the launch traced here: 66.6 us
  starting transfers between devices  29.9 us (45%)
  waiting for transfers between devices  29.3 us (44%)
  Pallas kernels  6.6 us (10%)
  between operations  0.73 us (1%)
    ppermute x18, starting transfers between devices, move(): got[name] = lax.ppermute(sent, axis, pairs)  29.8 us
    ppermute x18, waiting for transfers between devices, move(): got[name] = lax.ppermute(sent, axis, pairs)  23 us
    ppermute x1, waiting for transfers between devices, body(): got = lax.ppermute(send, 'level', ring(2, 1))  6.36 us
    pallas_call x7, Pallas kernels, call(): pl.pallas_call(kernel, out_shape=outs, in_specs=[SMEM] * len(scalars) + [...  5.51 us
  transfers between devices with their start and end apart: 19, of which 10 were waited for; matrix products, arithmetic and copies ran while one was open for 0% of the time, Pallas kernels for 0%

profile of v3, /device:TPU:0, one launch (start us, length us, event | category | flops | bytes accessed | tf_op | source)
XLA Modules:
  0.0 66.6 jit_solution(113575006066509599)
XLA Ops:
  0.6 1.1 %shard_map.50 = (f32[8,16,256]{2,1,0:T(8,128)S(1)}, f32[8,16,256]{2,1,0:T(8,128)S(1)}, f32[8,16,256]{2,1,0:T(8,128)S(1)}, f32[10,8,256]{2,1,0:T(8,128)S(1)}, f32...) custom-call(s32[1]{0:T(128)} %bitcast.h, f32[8,32,256]{2,1,0:T(8,128)} %u.1, ...), custom_call_target="tpu_custom_call" | custom-call | tf_op jit(solution)/shard_map/pallas_call | solution.py:337
  1.7 3.1 %collective-permute-start = (f32[10,8,256]{2,1,0:T(8,128)S(1)}, f32[10,8,256]{2,1,0:T(8,128)S(1)}, u32[]{:S(2)}, u32[]{:S(2)}) collective-permute-start(f32[10,8,256]{2,1,0:T(8,128)S(1)} %get-tuple-element.37), channel_id=1, source_target_pairs={{0,4},{4,8},{8,12},{12,0},{1,5},{5,9},{9,13},{13,1},{2,6},{6,10},{... | collective-permute-start | bytes 245768 | tf_op jit(solution)/shard_map/ppermute | solution.py:301
  4.9 2.1 %collective-permute-start.1 = (f32[10,8,256]{2,1,0:T(8,128)S(1)}, f32[10,8,256]{2,1,0:T(8,128)S(1)}, u32[]{:S(2)}, u32[]{:S(2)}) collective-permute-start(f32[10,8,256]{2,1,0:T(8,128)S(1)} %get-tuple-element.38), channel_id=1, source_target_pairs={{0,12},{4,0},{8,4},{12,8},{1,13},{5,1},{9,5},{13,9},{2,14},{6,2},{... | collective-permute-start | bytes 245768 | tf_op jit(solution)/shard_map/ppermute | solution.py:301
  6.9 2.7 %collective-permute-done.refs_3_.rest_2_ = f32[10,8,256]{2,1,0:T(8,128)S(1)} collective-permute-done((f32[10,8,256]{2,1,0:T(8,128)S(1)}, f32[10,8,256]{2,1,0:T(8,128)S(1)}, u32[]{:S(2)}, u32[]{:S(2)}) %collective-permute-start) | collective-permute-done | bytes 81952 | tf_op jit(solution)/shard_map/ppermute | solution.py:301
  9.6 0.9 %collective-permute-done.1.refs_4_.rest_3_ = f32[10,8,256]{2,1,0:T(8,128)S(1)} collective-permute-done((f32[10,8,256]{2,1,0:T(8,128)S(1)}, f32[10,8,256]{2,1,0:T(8,128)S(1)}, u32[]{:S(2)}, u32[]{:S(2)}) %collective-permute-start.1) | collective-permute-done | bytes 81952 | tf_op jit(solution)/shard_map/ppermute | solution.py:301
  10.6 1.6 %collective-permute-start.2 = (f32[30,8,256]{2,1,0:T(8,128)S(1)}, f32[30,8,256]{2,1,0:T(8,128)S(1)}, u32[]{:S(2)}, u32[]{:S(2)}) collective-permute-start(f32[30,8,256]{2,1,0:T(8,128)S(1)} %get-tuple-element.39), channel_id=1, source_target_pairs={{0,16},{16,17},{17,1},{1,2},{2,18},{18,19},{19,3},{3,0},{4,20},{20... | collective-permute-start | bytes 737288 | tf_op jit(solution)/shard_map/ppermute | solution.py:301
  12.1 0.3 collective-permute-start.3
  12.4 1.1 %collective-permute-start.4 = (f32[22,8,256]{2,1,0:T(8,128)S(1)}, f32[22,8,256]{2,1,0:T(8,128)S(1)}, u32[]{:S(2)}, u32[]{:S(2)}) collective-permute-start(f32[22,8,256]{2,1,0:T(8,128)S(1)} %get-tuple-element.41), channel_id=1, source_target_pairs={{0,4},{4,8},{8,12},{12,0},{1,5},{5,9},{9,13},{13,1},{2,6},{6,10},{... | collective-permute-start | bytes 540680 | tf_op jit(solution)/shard_map/ppermute | solution.py:301
  13.5 2.7 %collective-permute-start.5 = (f32[22,8,256]{2,1,0:T(8,128)S(1)}, f32[22,8,256]{2,1,0:T(8,128)S(1)}, u32[]{:S(2)}, u32[]{:S(2)}) collective-permute-start(f32[22,8,256]{2,1,0:T(8,128)S(1)} %get-tuple-element.42), channel_id=1, source_target_pairs={{0,12},{4,0},{8,4},{12,8},{1,13},{5,1},{9,5},{13,9},{2,14},{6,2},{... | collective-permute-start | bytes 540680 | tf_op jit(solution)/shard_map/ppermute | solution.py:301
  16.2 5.4 %collective-permute-done.4.rest_4_ = f32[22,8,256]{2,1,0:T(8,128)S(1)} collective-permute-done((f32[22,8,256]{2,1,0:T(8,128)S(1)}, f32[22,8,256]{2,1,0:T(8,128)S(1)}, u32[]{:S(2)}, u32[]{:S(2)}) %collective-permute-start.4) | collective-permute-done | bytes 180256 | tf_op jit(solution)/shard_map/ppermute | solution.py:301
  21.6 1.8 %collective-permute-done.5.rest_5_ = f32[22,8,256]{2,1,0:T(8,128)S(1)} collective-permute-done((f32[22,8,256]{2,1,0:T(8,128)S(1)}, f32[22,8,256]{2,1,0:T(8,128)S(1)}, u32[]{:S(2)}, u32[]{:S(2)}) %collective-permute-start.5) | collective-permute-done | bytes 180256 | tf_op jit(solution)/shard_map/ppermute | solution.py:301
  23.4 0.0 collective-permute-done.2.rest_0_
  23.4 0.0 collective-permute-done.3.rest_1_
  23.4 1.7 %shard_map.52 = (f32[8,16,256]{2,1,0:T(8,128)S(1)}, f32[8,16,256]{2,1,0:T(8,128)S(1)}, f32[8,16,256]{2,1,0:T(8,128)S(1)}, f32[16,32,256]{2,1,0:T(8,128)S(1)}, f3...) custom-call(f32[8,16,256]{2,1,0:T(8,128)S(1)} %get-tuple-element.34.re, ...), custom_call_target="tpu_custom_call" | custom-call | flops 6553600 | bytes 2654208 | tf_op jit(solution)/shard_map/pallas_call | solution.py:37
  25.2 1.1 %collective-permute-start.6 = (f32[6,8,256]{2,1,0:T(8,128)S(1)}, f32[6,8,256]{2,1,0:T(8,128)S(1)}, u32[]{:S(2)}, u32[]{:S(2)}) collective-permute-start(f32[6,8,256]{2,1,0:T(8,128)S(1)} %get-tuple-element.47), channel_id=1, source_target_pairs={{0,4},{4,8},{8,12},{12,0},{1,5},{5,9},{9,13},{13,1},{2,6},{6,10},{... | collective-permute-start | bytes 147464 | tf_op jit(solution)/shard_map/ppermute | solution.py:301
  26.3 2.7 %collective-permute-start.7 = (f32[6,8,256]{2,1,0:T(8,128)S(1)}, f32[6,8,256]{2,1,0:T(8,128)S(1)}, u32[]{:S(2)}, u32[]{:S(2)}) collective-permute-start(f32[6,8,256]{2,1,0:T(8,128)S(1)} %get-tuple-element.48), channel_id=1, source_target_pairs={{0,12},{4,0},{8,4},{12,8},{1,13},{5,1},{9,5},{13,9},{2,14},{6,2},{... | collective-permute-start | bytes 147464 | tf_op jit(solution)/shard_map/ppermute | solution.py:301
  29.0 2.2 %collective-permute-done.6.refs_2_.rest_2_ = f32[6,8,256]{2,1,0:T(8,128)S(1)} collective-permute-done((f32[6,8,256]{2,1,0:T(8,128)S(1)}, f32[6,8,256]{2,1,0:T(8,128)S(1)}, u32[]{:S(2)}, u32[]{:S(2)}) %collective-permute-start.6) | collective-permute-done | bytes 49184 | tf_op jit(solution)/shard_map/ppermute | solution.py:301
  31.2 0.0 collective-permute-done.7.refs_3_.rest_3_
  31.2 0.5 collective-permute-start.8
  31.7 1.3 %collective-permute-start.9 = (f32[18,8,256]{2,1,0:T(8,128)S(1)}, f32[18,8,256]{2,1,0:T(8,128)S(1)}, u32[]{:S(2)}, u32[]{:S(2)}) collective-permute-start(f32[18,8,256]{2,1,0:T(8,128)S(1)} %get-tuple-element.50), channel_id=1, source_target_pairs={{0,3},{16,0},{17,16},{1,17},{2,1},{18,2},{19,18},{3,19},{4,7},{20,... | collective-permute-start | bytes 442376 | tf_op jit(solution)/shard_map/ppermute | solution.py:301
  33.1 0.7 %collective-permute-start.10 = (f32[14,8,256]{2,1,0:T(8,128)S(1)}, f32[14,8,256]{2,1,0:T(8,128)S(1)}, u32[]{:S(2)}, u32[]{:S(2)}) collective-permute-start(f32[14,8,256]{2,1,0:T(8,128)S(1)} %get-tuple-element.51), channel_id=1, source_target_pairs={{0,4},{4,8},{8,12},{12,0},{1,5},{5,9},{9,13},{13,1},{2,6},{6,10},{... | collective-permute-start | bytes 344072 | tf_op jit(solution)/shard_map/ppermute | solution.py:301
  33.8 3.1 %collective-permute-start.11 = (f32[14,8,256]{2,1,0:T(8,128)S(1)}, f32[14,8,256]{2,1,0:T(8,128)S(1)}, u32[]{:S(2)}, u32[]{:S(2)}) collective-permute-start(f32[14,8,256]{2,1,0:T(8,128)S(1)} %get-tuple-element.52), channel_id=1, source_target_pairs={{0,12},{4,0},{8,4},{12,8},{1,13},{5,1},{9,5},{13,9},{2,14},{6,2},{... | collective-permute-start | bytes 344072 | tf_op jit(solution)/shard_map/ppermute | solution.py:301
  36.9 3.9 %collective-permute-done.10.rest_4_ = f32[14,8,256]{2,1,0:T(8,128)S(1)} collective-permute-done((f32[14,8,256]{2,1,0:T(8,128)S(1)}, f32[14,8,256]{2,1,0:T(8,128)S(1)}, u32[]{:S(2)}, u32[]{:S(2)}) %collective-permute-start.10) | collective-permute-done | bytes 114720 | tf_op jit(solution)/shard_map/ppermute | solution.py:301
  40.8 0.0 collective-permute-done.11.rest_5_
  40.8 0.0 collective-permute-done.8.rest_0_
  40.8 0.0 collective-permute-done.9.rest_1_
  40.8 1.2 %shard_map.54 = (f32[8,16,256]{2,1,0:T(8,128)S(1)}, f32[8,16,256]{2,1,0:T(8,128)S(1)}, f32[8,16,256]{2,1,0:T(8,128)S(1)}, f32[6,8,256]{2,1,0:T(8,128)S(1)}, f32[...) custom-call(f32[8,16,256]{2,1,0:T(8,128)S(1)} %get-tuple-element.43.u, ...), custom_call_target="tpu_custom_call" | custom-call | flops 6553600 | bytes 2260992 | tf_op jit(solution)/shard_map/pallas_call | solution.py:37
  42.0 1.8 %collective-permute-start.12 = (f32[6,8,256]{2,1,0:T(8,128)S(1)}, f32[6,8,256]{2,1,0:T(8,128)S(1)}, u32[]{:S(2)}, u32[]{:S(2)}) collective-permute-start(f32[6,8,256]{2,1,0:T(8,128)S(1)} %get-tuple-element.56), channel_id=1, source_target_pairs={{0,4},{4,8},{8,12},{12,0},{1,5},{5,9},{9,13},{13,1},{2,6},{6,10},{... | collective-permute-start | bytes 147464 | tf_op jit(solution)/shard_map/ppermute | solution.py:301
  43.8 2.1 %collective-permute-start.13 = (f32[6,8,256]{2,1,0:T(8,128)S(1)}, f32[6,8,256]{2,1,0:T(8,128)S(1)}, u32[]{:S(2)}, u32[]{:S(2)}) collective-permute-start(f32[6,8,256]{2,1,0:T(8,128)S(1)} %get-tuple-element.57), channel_id=1, source_target_pairs={{0,12},{4,0},{8,4},{12,8},{1,13},{5,1},{9,5},{13,9},{2,14},{6,2},{... | collective-permute-start | bytes 147464 | tf_op jit(solution)/shard_map/ppermute | solution.py:301
  45.8 2.2 %collective-permute-done.12.refs_2_.rest_2_ = f32[6,8,256]{2,1,0:T(8,128)S(1)} collective-permute-done((f32[6,8,256]{2,1,0:T(8,128)S(1)}, f32[6,8,256]{2,1,0:T(8,128)S(1)}, u32[]{:S(2)}, u32[]{:S(2)}) %collective-permute-start.12) | collective-permute-done | bytes 49184 | tf_op jit(solution)/shard_map/ppermute | solution.py:301
  48.0 0.4 collective-permute-done.13.refs_3_.rest_3_
  48.4 0.1 collective-permute-start.14
  48.5 1.7 %collective-permute-start.15 = (f32[18,8,256]{2,1,0:T(8,128)S(1)}, f32[18,8,256]{2,1,0:T(8,128)S(1)}, u32[]{:S(2)}, u32[]{:S(2)}) collective-permute-start(f32[18,8,256]{2,1,0:T(8,128)S(1)} %get-tuple-element.59), channel_id=1, source_target_pairs={{0,3},{16,0},{17,16},{1,17},{2,1},{18,2},{19,18},{3,19},{4,7},{20,... | collective-permute-start | bytes 442376 | tf_op jit(solution)/shard_map/ppermute | solution.py:301
  50.2 0.6 collective-permute-start.16
  50.8 3.2 %collective-permute-start.17 = (f32[14,8,256]{2,1,0:T(8,128)S(1)}, f32[14,8,256]{2,1,0:T(8,128)S(1)}, u32[]{:S(2)}, u32[]{:S(2)}) collective-permute-start(f32[14,8,256]{2,1,0:T(8,128)S(1)} %get-tuple-element.61), channel_id=1, source_target_pairs={{0,12},{4,0},{8,4},{12,8},{1,13},{5,1},{9,5},{13,9},{2,14},{6,2},{... | collective-permute-start | bytes 344072 | tf_op jit(solution)/shard_map/ppermute | solution.py:301
  54.1 0.1 pad_maximum_fusion.scale
  54.1 3.5 %collective-permute-done.16.rest_4_ = f32[14,8,256]{2,1,0:T(8,128)S(1)} collective-permute-done((f32[14,8,256]{2,1,0:T(8,128)S(1)}, f32[14,8,256]{2,1,0:T(8,128)S(1)}, u32[]{:S(2)}, u32[]{:S(2)}) %collective-permute-start.16) | collective-permute-done | bytes 114720 | tf_op jit(solution)/shard_map/ppermute | solution.py:301
  57.7 0.0 collective-permute-done.17.rest_5_
  57.7 0.0 collective-permute-done.14.rest_0_
  57.7 0.0 collective-permute-done.15.rest_1_
  57.7 1.7 %shard_map.56 = (f32[16,16,256]{2,1,0:T(8,128)S(1)}, f32[16,16,256]{2,1,0:T(8,128)S(1)}) custom-call(f32[2]{0:T(128)S(1)} %pad_maximum_fusion.scale, f32[8,16,256]{2,1,0:T(8,128)S(1)} %get-tuple-element.53.u, f32[8,16,256]{2,1,0:T(8,128)S(1)} %get-tuple-element.54.refs_0_.v, f32[8,16,256]{2,1,0:T(8,128)S(1)} %get-tuple-element.55.refs_1_.q, ...), custom_call_target="tpu_custom_call" | custom-call | flops 6553600 | bytes 2064384 | tf_op jit(solution)/shard_map/pallas_call | solution.py:37
  59.4 0.1 collective-permute-start.18
  59.5 6.4 %collective-permute-done.18.got = f32[16,16,256]{2,1,0:T(8,128)S(1)} collective-permute-done((f32[16,16,256]{2,1,0:T(8,128)S(1)}, f32[16,16,256]{2,1,0:T(8,128)S(1)}, u32[]{:S(2)}, u32[]{:S(2)}) %collective-permute-start.18) | collective-permute-done | bytes 262176 | tf_op jit(solution)/shard_map/ppermute | solution.py:373
  65.8 0.8 %shard_map.57 = (f32[8,32,256]{2,1,0:T(8,128)}, f32[8,32,256]{2,1,0:T(8,128)}) custom-call(s32[1]{0:T(128)} %bitcast.h, f32[16,16,256]{2,1,0:T(8,128)S(1)} %get-tuple-element.62.keep, f32[16,16,256]{2,1,0:T(8,128)S(1)} %collective-permute-done.18.got), custom_call_target="tpu_custom_call" | custom-call | bytes 1048576 | tf_op jit(solution)/shard_map/pallas_call | solution.py:37
  (3 shorter events, 0.1 us)
Async XLA Ops:
  1.7 7.9 %collective-permute-start = (f32[10,8,256]{2,1,0:T(8,128)S(1)}, f32[10,8,256]{2,1,0:T(8,128)S(1)}, u32[]{:S(2)}, u32[]{:S(2)}) collective-permute-start(f32[10,8,256]{2,1,0:T(8,128)S(1)} %get-tuple-element.37), channel_id=1, source_target_pairs={{0,4},{4,8},{8,12},{12,0},{1,5},{5,9},{9,13},{13,1},{2,6},{6,10},{... | collective-permute-start | bytes 245768 | tf_op jit(solution)/shard_map/ppermute | solution.py:301
  4.9 5.7 %collective-permute-start.1 = (f32[10,8,256]{2,1,0:T(8,128)S(1)}, f32[10,8,256]{2,1,0:T(8,128)S(1)}, u32[]{:S(2)}, u32[]{:S(2)}) collective-permute-start(f32[10,8,256]{2,1,0:T(8,128)S(1)} %get-tuple-element.38), channel_id=1, source_target_pairs={{0,12},{4,0},{8,4},{12,8},{1,13},{5,1},{9,5},{13,9},{2,14},{6,2},{... | collective-permute-start | bytes 245768 | tf_op jit(solution)/shard_map/ppermute | solution.py:301
  10.6 12.9 %collective-permute-start.2 = (f32[30,8,256]{2,1,0:T(8,128)S(1)}, f32[30,8,256]{2,1,0:T(8,128)S(1)}, u32[]{:S(2)}, u32[]{:S(2)}) collective-permute-start(f32[30,8,256]{2,1,0:T(8,128)S(1)} %get-tuple-element.39), channel_id=1, source_target_pairs={{0,16},{16,17},{17,1},{1,2},{2,18},{18,19},{19,3},{3,0},{4,20},{20... | collective-permute-start | bytes 737288 | tf_op jit(solution)/shard_map/ppermute | solution.py:301
  12.1 11.3 %collective-permute-start.3 = (f32[30,8,256]{2,1,0:T(8,128)S(1)}, f32[30,8,256]{2,1,0:T(8,128)S(1)}, u32[]{:S(2)}, u32[]{:S(2)}) collective-permute-start(f32[30,8,256]{2,1,0:T(8,128)S(1)} %get-tuple-element.40), channel_id=1, source_target_pairs={{0,3},{16,0},{17,16},{1,17},{2,1},{18,2},{19,18},{3,19},{4,7},{20,... | collective-permute-start | bytes 737288 | tf_op jit(solution)/shard_map/ppermute | solution.py:301
  12.4 9.2 %collective-permute-start.4 = (f32[22,8,256]{2,1,0:T(8,128)S(1)}, f32[22,8,256]{2,1,0:T(8,128)S(1)}, u32[]{:S(2)}, u32[]{:S(2)}) collective-permute-start(f32[22,8,256]{2,1,0:T(8,128)S(1)} %get-tuple-element.41), channel_id=1, source_target_pairs={{0,4},{4,8},{8,12},{12,0},{1,5},{5,9},{9,13},{13,1},{2,6},{6,10},{... | collective-permute-start | bytes 540680 | tf_op jit(solution)/shard_map/ppermute | solution.py:301
  13.5 9.9 %collective-permute-start.5 = (f32[22,8,256]{2,1,0:T(8,128)S(1)}, f32[22,8,256]{2,1,0:T(8,128)S(1)}, u32[]{:S(2)}, u32[]{:S(2)}) collective-permute-start(f32[22,8,256]{2,1,0:T(8,128)S(1)} %get-tuple-element.42), channel_id=1, source_target_pairs={{0,12},{4,0},{8,4},{12,8},{1,13},{5,1},{9,5},{13,9},{2,14},{6,2},{... | collective-permute-start | bytes 540680 | tf_op jit(solution)/shard_map/ppermute | solution.py:301
  25.2 6.0 %collective-permute-start.6 = (f32[6,8,256]{2,1,0:T(8,128)S(1)}, f32[6,8,256]{2,1,0:T(8,128)S(1)}, u32[]{:S(2)}, u32[]{:S(2)}) collective-permute-start(f32[6,8,256]{2,1,0:T(8,128)S(1)} %get-tuple-element.47), channel_id=1, source_target_pairs={{0,4},{4,8},{8,12},{12,0},{1,5},{5,9},{9,13},{13,1},{2,6},{6,10},{... | collective-permute-start | bytes 147464 | tf_op jit(solution)/shard_map/ppermute | solution.py:301
  26.3 4.9 %collective-permute-start.7 = (f32[6,8,256]{2,1,0:T(8,128)S(1)}, f32[6,8,256]{2,1,0:T(8,128)S(1)}, u32[]{:S(2)}, u32[]{:S(2)}) collective-permute-start(f32[6,8,256]{2,1,0:T(8,128)S(1)} %get-tuple-element.48), channel_id=1, source_target_pairs={{0,12},{4,0},{8,4},{12,8},{1,13},{5,1},{9,5},{13,9},{2,14},{6,2},{... | collective-permute-start | bytes 147464 | tf_op jit(solution)/shard_map/ppermute | solution.py:301
  31.2 9.5 %collective-permute-start.8 = (f32[18,8,256]{2,1,0:T(8,128)S(1)}, f32[18,8,256]{2,1,0:T(8,128)S(1)}, u32[]{:S(2)}, u32[]{:S(2)}) collective-permute-start(f32[18,8,256]{2,1,0:T(8,128)S(1)} %get-tuple-element.49), channel_id=1, source_target_pairs={{0,16},{16,17},{17,1},{1,2},{2,18},{18,19},{19,3},{3,0},{4,20},{20... | collective-permute-start | bytes 442376 | tf_op jit(solution)/shard_map/ppermute | solution.py:301
  31.7 9.0 %collective-permute-start.9 = (f32[18,8,256]{2,1,0:T(8,128)S(1)}, f32[18,8,256]{2,1,0:T(8,128)S(1)}, u32[]{:S(2)}, u32[]{:S(2)}) collective-permute-start(f32[18,8,256]{2,1,0:T(8,128)S(1)} %get-tuple-element.50), channel_id=1, source_target_pairs={{0,3},{16,0},{17,16},{1,17},{2,1},{18,2},{19,18},{3,19},{4,7},{20,... | collective-permute-start | bytes 442376 | tf_op jit(solution)/shard_map/ppermute | solution.py:301
  33.1 7.7 %collective-permute-start.10 = (f32[14,8,256]{2,1,0:T(8,128)S(1)}, f32[14,8,256]{2,1,0:T(8,128)S(1)}, u32[]{:S(2)}, u32[]{:S(2)}) collective-permute-start(f32[14,8,256]{2,1,0:T(8,128)S(1)} %get-tuple-element.51), channel_id=1, source_target_pairs={{0,4},{4,8},{8,12},{12,0},{1,5},{5,9},{9,13},{13,1},{2,6},{6,10},{... | collective-permute-start | bytes 344072 | tf_op jit(solution)/shard_map/ppermute | solution.py:301
  33.8 7.0 %collective-permute-start.11 = (f32[14,8,256]{2,1,0:T(8,128)S(1)}, f32[14,8,256]{2,1,0:T(8,128)S(1)}, u32[]{:S(2)}, u32[]{:S(2)}) collective-permute-start(f32[14,8,256]{2,1,0:T(8,128)S(1)} %get-tuple-element.52), channel_id=1, source_target_pairs={{0,12},{4,0},{8,4},{12,8},{1,13},{5,1},{9,5},{13,9},{2,14},{6,2},{... | collective-permute-start | bytes 344072 | tf_op jit(solution)/shard_map/ppermute | solution.py:301
  42.0 6.0 %collective-permute-start.12 = (f32[6,8,256]{2,1,0:T(8,128)S(1)}, f32[6,8,256]{2,1,0:T(8,128)S(1)}, u32[]{:S(2)}, u32[]{:S(2)}) collective-permute-start(f32[6,8,256]{2,1,0:T(8,128)S(1)} %get-tuple-element.56), channel_id=1, source_target_pairs={{0,4},{4,8},{8,12},{12,0},{1,5},{5,9},{9,13},{13,1},{2,6},{6,10},{... | collective-permute-start | bytes 147464 | tf_op jit(solution)/shard_map/ppermute | solution.py:301
  43.8 4.6 %collective-permute-start.13 = (f32[6,8,256]{2,1,0:T(8,128)S(1)}, f32[6,8,256]{2,1,0:T(8,128)S(1)}, u32[]{:S(2)}, u32[]{:S(2)}) collective-permute-start(f32[6,8,256]{2,1,0:T(8,128)S(1)} %get-tuple-element.57), channel_id=1, source_target_pairs={{0,12},{4,0},{8,4},{12,8},{1,13},{5,1},{9,5},{13,9},{2,14},{6,2},{... | collective-permute-start | bytes 147464 | tf_op jit(solution)/shard_map/ppermute | solution.py:301
  48.4 9.3 %collective-permute-start.14 = (f32[18,8,256]{2,1,0:T(8,128)S(1)}, f32[18,8,256]{2,1,0:T(8,128)S(1)}, u32[]{:S(2)}, u32[]{:S(2)}) collective-permute-start(f32[18,8,256]{2,1,0:T(8,128)S(1)} %get-tuple-element.58), channel_id=1, source_target_pairs={{0,16},{16,17},{17,1},{1,2},{2,18},{18,19},{19,3},{3,0},{4,20},{20... | collective-permute-start | bytes 442376 | tf_op jit(solution)/shard_map/ppermute | solution.py:301
  48.5 9.2 %collective-permute-start.15 = (f32[18,8,256]{2,1,0:T(8,128)S(1)}, f32[18,8,256]{2,1,0:T(8,128)S(1)}, u32[]{:S(2)}, u32[]{:S(2)}) collective-permute-start(f32[18,8,256]{2,1,0:T(8,128)S(1)} %get-tuple-element.59), channel_id=1, source_target_pairs={{0,3},{16,0},{17,16},{1,17},{2,1},{18,2},{19,18},{3,19},{4,7},{20,... | collective-permute-start | bytes 442376 | tf_op jit(solution)/shard_map/ppermute | solution.py:301
  50.2 7.4 %collective-permute-start.16 = (f32[14,8,256]{2,1,0:T(8,128)S(1)}, f32[14,8,256]{2,1,0:T(8,128)S(1)}, u32[]{:S(2)}, u32[]{:S(2)}) collective-permute-start(f32[14,8,256]{2,1,0:T(8,128)S(1)} %get-tuple-element.60), channel_id=1, source_target_pairs={{0,4},{4,8},{8,12},{12,0},{1,5},{5,9},{9,13},{13,1},{2,6},{6,10},{... | collective-permute-start | bytes 344072 | tf_op jit(solution)/shard_map/ppermute | solution.py:301
  50.8 6.8 %collective-permute-start.17 = (f32[14,8,256]{2,1,0:T(8,128)S(1)}, f32[14,8,256]{2,1,0:T(8,128)S(1)}, u32[]{:S(2)}, u32[]{:S(2)}) collective-permute-start(f32[14,8,256]{2,1,0:T(8,128)S(1)} %get-tuple-element.61), channel_id=1, source_target_pairs={{0,12},{4,0},{8,4},{12,8},{1,13},{5,1},{9,5},{13,9},{2,14},{6,2},{... | collective-permute-start | bytes 344072 | tf_op jit(solution)/shard_map/ppermute | solution.py:301
  59.4 6.4 %collective-permute-start.18 = (f32[16,16,256]{2,1,0:T(8,128)S(1)}, f32[16,16,256]{2,1,0:T(8,128)S(1)}, u32[]{:S(2)}, u32[]{:S(2)}) collective-permute-start(f32[16,16,256]{2,1,0:T(8,128)S(1)} %get-tuple-element.63), channel_id=1, source_target_pairs={{0,16},{16,0},{1,17},{17,1},{2,18},{18,2},{3,19},{19,3},{4,20},{20... | collective-permute-start | bytes 786440 | tf_op jit(solution)/shard_map/ppermute | solution.py:373

commit v4 on v0

v4 whole, which is shorter than its diff:
```python
import functools

import jax
import jax.numpy as jnp
from jax import lax
from jax.experimental import pallas as pl
from jax.experimental.pallas import tpu as pltpu
from jax.sharding import PartitionSpec as P


STEPS = 8

time_step = 0.12
damping = 0.05
second = 0.5 * STEPS * time_step * time_step

NEAR = 4.0 / 3.0
FAR = -1.0 / 12.0

TILE = 8
WIDE = 8
MID = 6
LATER = (WIDE, MID)

VMEM = pl.BlockSpec(memory_space=pltpu.VMEM)
SMEM = pl.BlockSpec(memory_space=pltpu.SMEM)
OWN = slice(TILE, 3 * TILE)
ALL = slice(0, 4 * TILE)


def spec(*shape):
    return jax.ShapeDtypeStruct(shape, jnp.float32)


def call(kernel, outs, args, scalars=(), scratch=(), flops=0):
    moved = 4 * (sum(a.size for a in args) + sum(o.size for o in outs))
    return pl.pallas_call(
        kernel,
        out_shape=outs,
        in_specs=[SMEM] * len(scalars) + [VMEM] * len(args),
        out_specs=[VMEM] * len(outs),
        scratch_shapes=[pltpu.VMEM(shape, jnp.float32) for shape in scratch],
        compiler_params=pltpu.CompilerParams(vmem_limit_bytes=14 << 20),
        cost_estimate=pl.CostEstimate(flops=flops, bytes_accessed=moved, transcendentals=0),
    )(*scalars, *args)


def upper():
    return lax.broadcasted_iota(jnp.int32, (TILE, 1), 0) < TILE // 2


def turned(tile):
    return pltpu.roll(tile, TILE // 2, 0)


def lap(ref, i, rows):
    full = ref[i]
    count, depth = full.shape
    w = full[rows]
    near = ref[i - 1, rows, :] + ref[i + 1, rows, :]
    far = ref[i - 2, rows, :] + ref[i + 2, rows, :]
    near += pltpu.roll(w, 1, 1) + pltpu.roll(w, depth - 1, 1)
    far += pltpu.roll(w, 2, 1) + pltpu.roll(w, depth - 2, 1)
    near += pltpu.roll(full, 1, 0)[rows] + pltpu.roll(full, count - 1, 0)[rows]
    far += pltpu.roll(full, 2, 0)[rows] + pltpu.roll(full, count - 2, 0)[rows]
    return -7.5 * w + NEAR * near + FAR * far


def beyond(width, d):
    return max(0, width - 2 * ((d + 1) // 2))


def x_layout(widths):
    first, rest = {}, {}
    for k, width in enumerate(widths):
        for d in range(1, width + 1):
            for part, least in (("A", 0), ("B", TILE // 2)):
                into = first if beyond(width, d) > least else rest
                into[k, d, part] = len(into)
    return first, rest


def y_layout(planes, widths, corners):
    at = len(widths) * planes
    where = {}
    for k, width in enumerate(corners):
        for d in range(1, width + 1):
            rows = beyond(width, d)
            if rows > 0:
                where[k, d] = at
                at += 2 if rows > TILE // 2 else 1
    return where, at


def pack_x(fields, widths, sends):
    a_up, a_down, b_up, b_down = sends
    first, rest = x_layout(widths)
    for k, (f, width) in enumerate(zip(fields, widths)):
        planes = f.shape[0]
        for d in range(1, width + 1):
            for plane, xa, xb in ((planes - d, a_up, b_up), (d - 1, a_down, b_down)):
                low, high = f[plane, 0:TILE, :], f[plane, TILE:, :]
                for part, tile in (
                    ("A", jnp.where(upper(), low, high)),
                    ("B", jnp.where(upper(), high, low)),
                ):
                    if (k, d, part) in first:
                        xa[first[k, d, part]] = tile
                    else:
                        xb[rest[k, d, part]] = tile


def pack_y(extra, *refs):
    planes = refs[0].shape[0]
    v, q, xla, xha = refs[:4]
    y_up, y_down = refs[-2:]
    corners = LATER + ((MID,) if extra else ())
    where, _ = y_layout(planes, LATER, corners)
    first, _ = x_layout(LATER)
    for k, f in enumerate((v, q)):
        y_up[pl.ds(k * planes, planes)] = f[:, TILE:, :]
        y_down[pl.ds(k * planes, planes)] = f[:, 0:TILE, :]
    for (k, d), at in where.items():
        if k == 2:
            low, high = refs[4], refs[5]
            i, j = 4 + MID - d, 4 + d - 1
            a_low = jnp.where(upper(), low[i, 0:TILE, :], low[i, TILE:, :])
            a_high = jnp.where(upper(), high[j, 0:TILE, :], high[j, TILE:, :])
        else:
            a_low, a_high = xla[first[k, d, "A"]], xha[first[k, d, "A"]]
        if beyond(corners[k], d) > TILE // 2:
            for side, a, x in ((0, a_low, xla), (1, a_high, xha)):
                b = x[first[k, d, "B"]]
                y_up[at + side] = jnp.where(upper(), b, a)
                y_down[at + side] = jnp.where(upper(), a, b)
        else:
            y_up[at] = jnp.where(upper(), turned(a_high), a_low)
            y_down[at] = jnp.where(upper(), a_low, turned(a_high))


def widen(out, width, centre, y_tile, x_tiles, corner):
    planes, _, depth = centre.shape
    for i in range(planes):
        out[width + i, 0:TILE, :] = y_tile(0, i)
        out[width + i, OWN, :] = centre[i]
        out[width + i, 3 * TILE :, :] = y_tile(1, i)
    for d in range(1, width + 1):
        for side, to in ((0, width - d), (1, width + planes - 1 + d)):
            low, high = x_tiles(side, d)
            out[to, TILE : 2 * TILE, :] = low
            out[to, 2 * TILE : 3 * TILE, :] = high
            if beyond(width, d) > 0:
                out[to, 0:TILE, :] = corner(side, 0, d)
                out[to, 3 * TILE :, :] = corner(side, 1, d)
            else:
                out[to, 0:TILE, :] = jnp.zeros((TILE, depth), jnp.float32)
                out[to, 3 * TILE :, :] = jnp.zeros((TILE, depth), jnp.float32)


def corner_of(k, corners, where, y):
    def corner(side, y_side, d):
        at = where[k, d]
        if beyond(corners[k], d) > TILE // 2:
            return y[y_side][at + side]
        tile = y[y_side][at]
        return turned(tile) if side else tile

    return corner


def widen_moved(outs, fields, corners, y, xa, xb):
    planes = fields[0].shape[0]
    where, _ = y_layout(planes, LATER, corners)
    first, rest = x_layout(LATER)
    for k, (out, f) in enumerate(zip(outs, fields)):

        def tile(side, d, part):
            key = k, d, part
            return xa[side][first[key]] if key in first else xb[side][rest[key]]

        def x_tiles(side, d):
            a, b = tile(side, d, "A"), tile(side, d, "B")
            return jnp.where(upper(), a, b), jnp.where(upper(), b, a)

        widen(
            out,
            LATER[k],
            f,
            lambda side, i: y[side][k * planes + i],
            x_tiles,
            corner_of(k, corners, where, y),
        )


def load_first(h, u, v, s, u_own, v_own, s_own, y_up, y_down, x_up, x_down, sems):
    planes, half, _ = u_own.shape
    own = pl.ds(pl.multiple_of(h[0] * half, TILE), half)
    fields = (u_own, v_own, s_own)
    copies = [
        pltpu.make_async_copy(f.at[:, own, :], to, sems.at[k])
        for k, (f, to) in enumerate(zip((u, v, s), fields))
    ]
    for copy in copies:
        copy.start()
    for copy in copies:
        copy.wait()
    at = 0
    for k, (f, width) in enumerate(zip(fields, (2, 2, MID))):
        x_up[pl.ds(at, width)] = f[planes - width :]
        x_down[pl.ds(at, width)] = f[0:width]
        y_up[pl.ds(k * planes, planes)] = f[:, TILE:, :]
        y_down[pl.ds(k * planes, planes)] = f[:, 0:TILE, :]
        at += width


def first_step(u, v, s, yl, yh, xl, xh, u_out, v_out, q_out, *rest):
    sends, (u0, v0) = rest[:4], rest[4:]
    planes, _, _ = u.shape
    for k, (f, out) in enumerate(((u, u0), (v, v0))):
        inner = pl.ds(2, planes)
        out[inner, 0:TILE, :] = yl[pl.ds(k * planes, planes)]
        out[inner, OWN, :] = f[...]
        out[inner, 3 * TILE :, :] = yh[pl.ds(k * planes, planes)]
        out[0:2, OWN, :] = xl[pl.ds(2 * k, 2)]
        out[planes + 2 :, OWN, :] = xh[pl.ds(2 * k, 2)]
    for i in range(planes):
        q, l = lap(u0, i + 2, OWN), lap(v0, i + 2, OWN)
        u_out[i] = u[i] + time_step * v[i]
        v_out[i] = v[i] + time_step * (s[i] * q + damping * l)
        q_out[i] = q + time_step * l
    pack_x((v_out, q_out), LATER, sends)


def advance(planes, width, v, q, s, v_out, q_out):
    count = planes + 2 * width - 4
    for i in range(count):
        edge = i < 2 or i >= count - 2
        rows = OWN if edge else ALL
        l = lap(v, i + 2, rows)
        now = s[i + MID + 2 - width, rows, :] * q[i, rows, :] + damping * l
        v_out[i, rows, :] = v[i + 2, rows, :] + time_step * now
        if not edge:
            q_out[i - 2] = q[i] + time_step * l


def middle_steps(u, v, q, s, yl, yh, xla, xha, xlb, xhb, ysl, ysh, xsl, xsh, *rest):
    (u_out, v_out, q_out, s_wide), sends = rest[:4], rest[4:8]
    v0, q0, v1, q1, v2, q2, v3, q3 = rest[8:]
    planes, _, _ = v.shape
    corners = LATER + (MID,)
    where, _ = y_layout(planes, LATER, corners)

    def s_rows(side, d):
        ref, i = ((xsl, 4 + MID - d), (xsh, 4 + d - 1))[side]
        return ref[i, 0:TILE, :], ref[i, TILE:, :]

    widen_moved((v0, q0), (v, q), corners, (yl, yh), (xla, xha), (xlb, xhb))
    widen(
        s_wide,
        MID,
        s,
        lambda side, i: (ysl, ysh)[side][2 * planes + i],
        s_rows,
        corner_of(2, corners, where, (yl, yh)),
    )
    advance(planes, WIDE, v0, q0, s_wide, v1, q1)
    advance(planes, WIDE - 2, v1, q1, s_wide, v2, q2)
    advance(planes, WIDE - 4, v2, q2, s_wide, v3, q3)
    for i in range(planes):
        l = lap(v3, i + 2, OWN)
        now = s[i] * q3[i, OWN, :] + damping * l
        v_out[i] = v3[i + 2, OWN, :] + time_step * now
        q_out[i] = q3[i, OWN, :] + time_step * l
        moved = v[i] + v1[i + 6, OWN, :] + v2[i + 4, OWN, :] + v3[i + 2, OWN, :]
        u_out[i] = u[i] + time_step * moved
    pack_x((v_out, q_out), LATER, sends)


def last_steps(scale, u, v, q, s_wide, yl, yh, xla, xha, xlb, xhb, keep, send, *scratch):
    v0, q0, v1, q1, v2, q2, rate, l7 = scratch
    planes, _, _ = v.shape
    widen_moved((v0, q0), (v, q), LATER, (yl, yh), (xla, xha), (xlb, xhb))
    advance(planes, WIDE, v0, q0, s_wide, v1, q1)
    advance(planes, WIDE - 2, v1, q1, s_wide, v2, q2)
    count = planes + 4
    for i in range(count):
        edge = i < 2 or i >= count - 2
        rows = OWN if edge else ALL
        l = lap(v2, i + 2, rows)
        rate[i, rows, :] = s_wide[i + MID - 2, rows, :] * q2[i, rows, :] + damping * l
        if not edge:
            l7[i - 2] = l[OWN]
    for i in range(planes):
        l = lap(rate, i + 2, OWN)
        r = rate[i + 2, OWN, :]
        v7 = v2[i + 4, OWN, :]
        u8 = u[i] + time_step * (v[i] + v1[i + 6, OWN, :] + v7)
        v8 = v7 + time_step * r
        more = s_wide[i + MID, OWN, :] * l7[i] + damping * l
        keep[i] = u8 + scale[0] * r
        keep[planes + i] = v8 + scale[0] * more
        send[i] = u8 + scale[1] * r
        send[planes + i] = v8 + scale[1] * more


def join(h, keep, got, out_u, out_v):
    planes, rows, _ = out_u.shape
    half = rows // 2
    own = pl.ds(pl.multiple_of(h[0] * half, TILE), half)
    other = pl.ds(pl.multiple_of((1 - h[0]) * half, TILE), half)
    for k, out in enumerate((out_u, out_v)):
        part = pl.ds(k * planes, planes)
        out[:, own, :] = keep[part]
        out[:, other, :] = got[part]


def ring(count, step):
    return [(i, (i + step) % count) for i in range(count)]


def strips(gy, step):
    def place(t):
        j, h = divmod(t % (2 * gy), 2)
        return ((h + j) % 2) * gy + j

    return [(place(t), place(t + step)) for t in range(2 * gy)]


STARTS = ("a_up", "a_down", "b_up", "b_down", "y_up", "y_down")


def move(name, sent):
    step = 1 if name.endswith("up") else -1
    if name.startswith("y"):
        return lax.ppermute(sent, ("level", "gy"), strips(lax.axis_size("gy"), step))
    return lax.ppermute(sent, "gx", ring(lax.axis_size("gx"), step))


def exchange_first(y_up, y_down, x_up, x_down):
    xl, xh = move("a_up", x_up), move("a_down", x_down)
    return move("y_up", y_up), move("y_down", y_down), xl, xh


def exchange(v, q, sends, extra):
    planes, _, depth = v.shape
    xla, xha, xlb, xhb = (move(name, sent) for name, sent in zip(STARTS, sends))
    corners = LATER + ((MID,) if extra else ())
    y = spec(y_layout(planes, LATER, corners)[1], TILE, depth)
    kernel = functools.partial(pack_y, bool(extra))
    y_up, y_down = call(kernel, [y, y], (v, q, xla, xha, *extra))
    return move("y_up", y_up), move("y_down", y_down), xla, xha, xlb, xhb


def edge_specs(depth, widths):
    return [spec(len(part), TILE, depth) for part in x_layout(widths) for _ in range(2)]


def body(u, v, s):
    planes, rows, depth = u.shape
    half = rows // 2
    assert lax.axis_size("level") == 2 and planes >= WIDE and half == 2 * TILE
    level = lax.axis_index("level")
    h = ((level + lax.axis_index("gy")) % 2).astype(jnp.int32).reshape(1)
    mine = jnp.where(level == 0, 0.0, second).astype(jnp.float32)
    scale = jnp.stack([mine, second - mine])

    tall = half + 2 * TILE
    block = spec(planes, half, depth)
    wide, mid, thin, slim, bare = ((planes + 2 * w, tall, depth) for w in (WIDE, MID, 4, 2, 0))
    work = 100 * u.size
    sent = edge_specs(depth, LATER)

    y, x = spec(3 * planes, TILE, depth), spec(4 + MID, half, depth)
    outs = [block] * 3 + [y, y, x, x]
    u, v, s, *sends = pl.pallas_call(
        load_first,
        out_shape=outs,
        in_specs=[SMEM] + [pl.BlockSpec(memory_space=pltpu.HBM)] * 3,
        out_specs=[VMEM] * len(outs),
        scratch_shapes=[pltpu.SemaphoreType.DMA((3,))],
        compiler_params=pltpu.CompilerParams(vmem_limit_bytes=14 << 20),
    )(h, *(pltpu.with_memory_space_constraint(f, pltpu.HBM) for f in (u, v, s)))
    halos = exchange_first(*sends)
    ysl, ysh, xsl, xsh = halos
    args = (u, v, s, *halos)
    u, v, q, *sends = call(first_step, [block] * 3 + sent, args, (), (slim, slim), work)
    halos = exchange(v, q, sends, (xsl, xsh))
    u, v, q, s_wide, *sends = call(
        middle_steps,
        [block] * 3 + [spec(*mid)] + sent,
        (u, v, q, s, *halos, ysl, ysh, xsl, xsh),
        (),
        (wide, mid, mid, thin, thin, slim, slim, bare),
        work,
    )
    halos = exchange(v, q, sends, ())
    both = spec(2 * planes, half, depth)
    keep, send = call(
        last_steps,
        [both, both],
        (u, v, q, s_wide, *halos),
        (scale,),
        (wide, mid, mid, thin, thin, slim, slim, (planes, half, depth)),
        work,
    )
    got = lax.ppermute(send, "level", ring(2, 1))
    out_u, out_v = call(join, [spec(planes, rows, depth)] * 2, (keep, got), (h,))
    return out_u[None], out_v[None]


def solution(mesh):
    placed = (P("gx", "gy", None),) * 3
    return jax.shard_map(
        body,
        mesh=mesh,
        in_specs=placed,
        out_specs=(P("level", "gx", "gy", None), P("level", "gx", "gy", None)),
        check_vma=False,
    )
```

time: 208 us -> 63.6 us (0.31)
  waiting for transfers between devices: 114 us -> 30.1 us
  other arithmetic: 30.3 us -> 0.07 us
  starting transfers between devices: 52.3 us -> 26 us
  local copies, waits for them, and re-layouts: 9.76 us -> 0 us
  Pallas kernels: 0 us -> 6.63 us
    ppermute x36 -> x17, waiting for transfers between devices: 114 us -> 30.1 us  [the longest x10 23.1 us: move(): return lax.ppermute(sent, 'gx', ring(lax.axis_size('gx'), step))]
    ppermute x36 -> x17, starting transfers between devices: 52.3 us -> 26 us  [the longest x10 19.3 us: move(): return lax.ppermute(sent, 'gx', ring(lax.axis_size('gx'), step))]
    sub x9 -> x0, other arithmetic: 13.2 us -> none  [stencil(): total = total + 4.0 / 3.0 * near_z - far_z / 12.0]
    slice x40 -> x0, local copies, waits for them, and re-layouts: 9.47 us -> none  [the longest x16 4.59 us: stencil(): far_z = jnp.roll(centre, 2, 3) + jnp.roll(centre, -2, 3)]
    concatenate x18 -> x0, other arithmetic: 7.69 us -> none  [with_halo(): block = jnp.concatenate([low, block, high], axis=dim)]
    pallas_call x0 -> x7, Pallas kernels: none -> 6.63 us  [the longest x6 5.52 us: call(): pl.pallas_call(kernel, out_shape=outs, in_specs=[SMEM] * len(scalars) + [...]
    another operation x21 -> x1, other arithmetic: 6.12 us -> 0.07 us  [body(): scale = jnp.stack([mine, second - mine])]
  transfers between devices with their start and end apart: 36 -> 17, of which waited for: 27 -> 10; matrix products, arithmetic and copies ran while one was open for 3% -> 0% of each run, Pallas kernels for 0% -> 0%
where the time goes in v4:
time: 63.6 us; the launch traced here: 63.4 us
  waiting for transfers between devices  30.1 us (47%)
  starting transfers between devices  26 us (41%)
  Pallas kernels  6.63 us (10%)
  between operations  0.72 us (1%)
    ppermute x10, waiting for transfers between devices, move(): return lax.ppermute(sent, 'gx', ring(lax.axis_size('gx'), step))  23.1 us
    ppermute x10, starting transfers between devices, move(): return lax.ppermute(sent, 'gx', ring(lax.axis_size('gx'), step))  19.3 us
    ppermute x1, waiting for transfers between devices, body(): got = lax.ppermute(send, 'level', ring(2, 1))  6.93 us
    ppermute x6, starting transfers between devices, move(): lax.ppermute(sent, ('level', 'gy'), strips(lax.axis_size('gy'), step))  6.64 us
    pallas_call x6, Pallas kernels, call(): pl.pallas_call(kernel, out_shape=outs, in_specs=[SMEM] * len(scalars) + [...  5.52 us
  transfers between devices with their start and end apart: 17, of which 10 were waited for; matrix products, arithmetic and copies ran while one was open for 0% of the time, Pallas kernels for 0%

profile of v4, /device:TPU:0, one launch (start us, length us, event | category | flops | bytes accessed | tf_op | source)
XLA Modules:
  0.0 63.4 jit_solution(4756553662277157494)
XLA Ops:
  0.6 1.1 %shard_map.50 = (f32[8,16,256]{2,1,0:T(8,128)S(1)}, f32[8,16,256]{2,1,0:T(8,128)S(1)}, f32[8,16,256]{2,1,0:T(8,128)S(1)}, f32[24,8,256]{2,1,0:T(8,128)S(1)}, f32...) custom-call(s32[1]{0:T(128)} %bitcast.h, f32[8,32,256]{2,1,0:T(8,128)} %u.1, ...), custom_call_target="tpu_custom_call" | custom-call | tf_op jit(solution)/shard_map/pallas_call | solution.py:375
  1.8 3.0 %collective-permute-start = (f32[24,8,256]{2,1,0:T(8,128)S(1)}, f32[24,8,256]{2,1,0:T(8,128)S(1)}, u32[]{:S(2)}, u32[]{:S(2)}) collective-permute-start(f32[24,8,256]{2,1,0:T(8,128)S(1)} %get-tuple-element.35), channel_id=1, source_target_pairs={{0,16},{16,17},{17,1},{1,2},{2,18},{18,19},{19,3},{3,0},{4,20},{20... | collective-permute-start | bytes 589832 | tf_op jit(solution)/shard_map/ppermute | solution.py:335
  4.8 0.0 collective-permute-start.1
  4.8 1.8 %collective-permute-start.2 = (f32[10,16,256]{2,1,0:T(8,128)S(1)}, f32[10,16,256]{2,1,0:T(8,128)S(1)}, u32[]{:S(2)}, u32[]{:S(2)}) collective-permute-start(f32[10,16,256]{2,1,0:T(8,128)S(1)} %get-tuple-element.37), channel_id=1, source_target_pairs={{0,4},{4,8},{8,12},{12,0},{1,5},{5,9},{9,13},{13,1},{2,6},{6,10},{... | collective-permute-start | bytes 491528 | tf_op jit(solution)/shard_map/ppermute | solution.py:336
  6.6 2.0 %collective-permute-start.3 = (f32[10,16,256]{2,1,0:T(8,128)S(1)}, f32[10,16,256]{2,1,0:T(8,128)S(1)}, u32[]{:S(2)}, u32[]{:S(2)}) collective-permute-start(f32[10,16,256]{2,1,0:T(8,128)S(1)} %get-tuple-element.38), channel_id=1, source_target_pairs={{0,12},{4,0},{8,4},{12,8},{1,13},{5,1},{9,5},{13,9},{2,14},{6,2},{... | collective-permute-start | bytes 491528 | tf_op jit(solution)/shard_map/ppermute | solution.py:336
  8.6 5.1 %collective-permute-done.2.xl.refs_4_.xsl = f32[10,16,256]{2,1,0:T(8,128)S(1)} collective-permute-done((f32[10,16,256]{2,1,0:T(8,128)S(1)}, f32[10,16,256]{2,1,0:T(8,128)S(1)}, u32[]{:S(2)}, u32[]{:S(2)}) %collective-permute-start.2) | collective-permute-done | bytes 163872 | tf_op jit(solution)/shard_map/ppermute | solution.py:336
  13.7 2.1 %collective-permute-done.3.xh.refs_5_.xsh = f32[10,16,256]{2,1,0:T(8,128)S(1)} collective-permute-done((f32[10,16,256]{2,1,0:T(8,128)S(1)}, f32[10,16,256]{2,1,0:T(8,128)S(1)}, u32[]{:S(2)}, u32[]{:S(2)}) %collective-permute-start.3) | collective-permute-done | bytes 163872 | tf_op jit(solution)/shard_map/ppermute | solution.py:336
  15.8 0.0 collective-permute-done.yl.ysl
  15.9 0.0 collective-permute-done.1.yh.ysh
  15.9 0.4 shard_map.51
  16.2 1.2 %collective-permute-start.4 = (f32[12,8,256]{2,1,0:T(8,128)S(1)}, f32[12,8,256]{2,1,0:T(8,128)S(1)}, u32[]{:S(2)}, u32[]{:S(2)}) collective-permute-start(f32[12,8,256]{2,1,0:T(8,128)S(1)} %get-tuple-element.42), channel_id=1, source_target_pairs={{0,4},{4,8},{8,12},{12,0},{1,5},{5,9},{9,13},{13,1},{2,6},{6,10},{... | collective-permute-start | bytes 294920 | tf_op jit(solution)/shard_map/ppermute | solution.py:336
  17.4 2.7 %collective-permute-start.5 = (f32[12,8,256]{2,1,0:T(8,128)S(1)}, f32[12,8,256]{2,1,0:T(8,128)S(1)}, u32[]{:S(2)}, u32[]{:S(2)}) collective-permute-start(f32[12,8,256]{2,1,0:T(8,128)S(1)} %get-tuple-element.43), channel_id=1, source_target_pairs={{0,12},{4,0},{8,4},{12,8},{1,13},{5,1},{9,5},{13,9},{2,14},{6,2},{... | collective-permute-start | bytes 294920 | tf_op jit(solution)/shard_map/ppermute | solution.py:336
  20.1 3.2 %collective-permute-done.4.refs_2_.xla = f32[12,8,256]{2,1,0:T(8,128)S(1)} collective-permute-done((f32[12,8,256]{2,1,0:T(8,128)S(1)}, f32[12,8,256]{2,1,0:T(8,128)S(1)}, u32[]{:S(2)}, u32[]{:S(2)}) %collective-permute-start.4) | collective-permute-done | bytes 98336 | tf_op jit(solution)/shard_map/ppermute | solution.py:336
  23.3 0.6 collective-permute-done.5.refs_3_.xha
  24.0 0.1 collective-permute-start.6
  24.1 1.7 %collective-permute-start.7 = (f32[32,8,256]{2,1,0:T(8,128)S(1)}, f32[32,8,256]{2,1,0:T(8,128)S(1)}, u32[]{:S(2)}, u32[]{:S(2)}) collective-permute-start(f32[32,8,256]{2,1,0:T(8,128)S(1)} %get-tuple-element.45), channel_id=1, source_target_pairs={{0,3},{16,0},{17,16},{1,17},{2,1},{18,2},{19,18},{3,19},{4,7},{20,... | collective-permute-start | bytes 786440 | tf_op jit(solution)/shard_map/ppermute | solution.py:335
  25.8 0.3 collective-permute-start.8
  26.2 3.5 %collective-permute-start.9 = (f32[16,8,256]{2,1,0:T(8,128)S(1)}, f32[16,8,256]{2,1,0:T(8,128)S(1)}, u32[]{:S(2)}, u32[]{:S(2)}) collective-permute-start(f32[16,8,256]{2,1,0:T(8,128)S(1)} %get-tuple-element.47), channel_id=1, source_target_pairs={{0,12},{4,0},{8,4},{12,8},{1,13},{5,1},{9,5},{13,9},{2,14},{6,2},{... | collective-permute-start | bytes 393224 | tf_op jit(solution)/shard_map/ppermute | solution.py:336
  29.6 4.3 %collective-permute-done.8.xlb = f32[16,8,256]{2,1,0:T(8,128)S(1)} collective-permute-done((f32[16,8,256]{2,1,0:T(8,128)S(1)}, f32[16,8,256]{2,1,0:T(8,128)S(1)}, u32[]{:S(2)}, u32[]{:S(2)}) %collective-permute-start.8) | collective-permute-done | bytes 131104 | tf_op jit(solution)/shard_map/ppermute | solution.py:336
  34.0 0.0 collective-permute-done.9.xhb
  34.0 0.0 collective-permute-done.6.yl
  34.0 0.0 collective-permute-done.7.yh
  34.0 1.9 %shard_map.53 = (f32[8,16,256]{2,1,0:T(8,128)S(1)}, f32[8,16,256]{2,1,0:T(8,128)S(1)}, f32[8,16,256]{2,1,0:T(8,128)S(1)}, f32[20,32,256]{2,1,0:T(8,128)S(1)}, f3...) custom-call(f32[8,16,256]{2,1,0:T(8,128)S(1)} %get-tuple-element.39., ...), custom_call_target="tpu_custom_call" | custom-call | flops 6553600 | bytes 3735552 | tf_op jit(solution)/shard_map/pallas_call | solution.py:37
  35.9 1.3 %collective-permute-start.10 = (f32[12,8,256]{2,1,0:T(8,128)S(1)}, f32[12,8,256]{2,1,0:T(8,128)S(1)}, u32[]{:S(2)}, u32[]{:S(2)}) collective-permute-start(f32[12,8,256]{2,1,0:T(8,128)S(1)} %get-tuple-element.52), channel_id=1, source_target_pairs={{0,4},{4,8},{8,12},{12,0},{1,5},{5,9},{9,13},{13,1},{2,6},{6,10},{... | collective-permute-start | bytes 294920 | tf_op jit(solution)/shard_map/ppermute | solution.py:336
  37.2 2.6 %collective-permute-start.11 = (f32[12,8,256]{2,1,0:T(8,128)S(1)}, f32[12,8,256]{2,1,0:T(8,128)S(1)}, u32[]{:S(2)}, u32[]{:S(2)}) collective-permute-start(f32[12,8,256]{2,1,0:T(8,128)S(1)} %get-tuple-element.53), channel_id=1, source_target_pairs={{0,12},{4,0},{8,4},{12,8},{1,13},{5,1},{9,5},{13,9},{2,14},{6,2},{... | collective-permute-start | bytes 294920 | tf_op jit(solution)/shard_map/ppermute | solution.py:336
  39.7 2.7 %collective-permute-done.10.refs_2_.xla = f32[12,8,256]{2,1,0:T(8,128)S(1)} collective-permute-done((f32[12,8,256]{2,1,0:T(8,128)S(1)}, f32[12,8,256]{2,1,0:T(8,128)S(1)}, u32[]{:S(2)}, u32[]{:S(2)}) %collective-permute-start.10) | collective-permute-done | bytes 98336 | tf_op jit(solution)/shard_map/ppermute | solution.py:336
  42.4 0.5 collective-permute-done.11.refs_3_.xha
  43.0 0.1 collective-permute-start.12
  43.1 1.7 %collective-permute-start.13 = (f32[28,8,256]{2,1,0:T(8,128)S(1)}, f32[28,8,256]{2,1,0:T(8,128)S(1)}, u32[]{:S(2)}, u32[]{:S(2)}) collective-permute-start(f32[28,8,256]{2,1,0:T(8,128)S(1)} %get-tuple-element.55), channel_id=1, source_target_pairs={{0,3},{16,0},{17,16},{1,17},{2,1},{18,2},{19,18},{3,19},{4,7},{20,... | collective-permute-start | bytes 688136 | tf_op jit(solution)/shard_map/ppermute | solution.py:335
  44.8 1.0 %collective-permute-start.14 = (f32[16,8,256]{2,1,0:T(8,128)S(1)}, f32[16,8,256]{2,1,0:T(8,128)S(1)}, u32[]{:S(2)}, u32[]{:S(2)}) collective-permute-start(f32[16,8,256]{2,1,0:T(8,128)S(1)} %get-tuple-element.56), channel_id=1, source_target_pairs={{0,4},{4,8},{8,12},{12,0},{1,5},{5,9},{9,13},{13,1},{2,6},{6,10},{... | collective-permute-start | bytes 393224 | tf_op jit(solution)/shard_map/ppermute | solution.py:336
  45.8 2.8 %collective-permute-start.15 = (f32[16,8,256]{2,1,0:T(8,128)S(1)}, f32[16,8,256]{2,1,0:T(8,128)S(1)}, u32[]{:S(2)}, u32[]{:S(2)}) collective-permute-start(f32[16,8,256]{2,1,0:T(8,128)S(1)} %get-tuple-element.57), channel_id=1, source_target_pairs={{0,12},{4,0},{8,4},{12,8},{1,13},{5,1},{9,5},{13,9},{2,14},{6,2},{... | collective-permute-start | bytes 393224 | tf_op jit(solution)/shard_map/ppermute | solution.py:336
  48.6 0.1 pad_maximum_fusion.scale
  48.7 3.9 %collective-permute-done.14.xlb = f32[16,8,256]{2,1,0:T(8,128)S(1)} collective-permute-done((f32[16,8,256]{2,1,0:T(8,128)S(1)}, f32[16,8,256]{2,1,0:T(8,128)S(1)}, u32[]{:S(2)}, u32[]{:S(2)}) %collective-permute-start.14) | collective-permute-done | bytes 131104 | tf_op jit(solution)/shard_map/ppermute | solution.py:336
  52.6 0.7 %collective-permute-done.15.xhb = f32[16,8,256]{2,1,0:T(8,128)S(1)} collective-permute-done((f32[16,8,256]{2,1,0:T(8,128)S(1)}, f32[16,8,256]{2,1,0:T(8,128)S(1)}, u32[]{:S(2)}, u32[]{:S(2)}) %collective-permute-start.15) | collective-permute-done | bytes 131104 | tf_op jit(solution)/shard_map/ppermute | solution.py:336
  53.2 0.0 collective-permute-done.12.yl
  53.2 0.0 collective-permute-done.13.yh
  53.2 2.4 %shard_map.55 = (f32[16,16,256]{2,1,0:T(8,128)S(1)}, f32[16,16,256]{2,1,0:T(8,128)S(1)}) custom-call(f32[2]{0:T(128)S(1)} %pad_maximum_fusion.scale, f32[8,16,256]{2,1,0:T(8,128)S(1)} %get-tuple-element.48.u, f32[8,16,256]{2,1,0:T(8,128)S(1)} %get-tuple-element.49.refs_0_.v, f32[8,16,256]{2,1,0:T(8,128)S(1)} %get-tuple-element.50.refs_1_.q, ...), custom_call_target="tpu_custom_call" | custom-call | flops 6553600 | bytes 2490368 | tf_op jit(solution)/shard_map/pallas_call | solution.py:37
  55.6 0.1 collective-permute-start.16
  55.7 6.9 %collective-permute-done.16.got = f32[16,16,256]{2,1,0:T(8,128)S(1)} collective-permute-done((f32[16,16,256]{2,1,0:T(8,128)S(1)}, f32[16,16,256]{2,1,0:T(8,128)S(1)}, u32[]{:S(2)}, u32[]{:S(2)}) %collective-permute-start.16) | collective-permute-done | bytes 262176 | tf_op jit(solution)/shard_map/ppermute | solution.py:406
  62.6 0.8 %shard_map.56 = (f32[8,32,256]{2,1,0:T(8,128)}, f32[8,32,256]{2,1,0:T(8,128)}) custom-call(s32[1]{0:T(128)} %bitcast.h, f32[16,16,256]{2,1,0:T(8,128)S(1)} %get-tuple-element.58.keep, f32[16,16,256]{2,1,0:T(8,128)S(1)} %collective-permute-done.16.got), custom_call_target="tpu_custom_call" | custom-call | bytes 1048576 | tf_op jit(solution)/shard_map/pallas_call | solution.py:37
  (2 shorter events, 0.1 us)
Async XLA Ops:
  1.8 14.1 %collective-permute-start = (f32[24,8,256]{2,1,0:T(8,128)S(1)}, f32[24,8,256]{2,1,0:T(8,128)S(1)}, u32[]{:S(2)}, u32[]{:S(2)}) collective-permute-start(f32[24,8,256]{2,1,0:T(8,128)S(1)} %get-tuple-element.35), channel_id=1, source_target_pairs={{0,16},{16,17},{17,1},{1,2},{2,18},{18,19},{19,3},{3,0},{4,20},{20... | collective-permute-start | bytes 589832 | tf_op jit(solution)/shard_map/ppermute | solution.py:335
  4.8 11.1 %collective-permute-start.1 = (f32[24,8,256]{2,1,0:T(8,128)S(1)}, f32[24,8,256]{2,1,0:T(8,128)S(1)}, u32[]{:S(2)}, u32[]{:S(2)}) collective-permute-start(f32[24,8,256]{2,1,0:T(8,128)S(1)} %get-tuple-element.36), channel_id=1, source_target_pairs={{0,3},{16,0},{17,16},{1,17},{2,1},{18,2},{19,18},{3,19},{4,7},{20,... | collective-permute-start | bytes 589832 | tf_op jit(solution)/shard_map/ppermute | solution.py:335
  4.8 8.9 %collective-permute-start.2 = (f32[10,16,256]{2,1,0:T(8,128)S(1)}, f32[10,16,256]{2,1,0:T(8,128)S(1)}, u32[]{:S(2)}, u32[]{:S(2)}) collective-permute-start(f32[10,16,256]{2,1,0:T(8,128)S(1)} %get-tuple-element.37), channel_id=1, source_target_pairs={{0,4},{4,8},{8,12},{12,0},{1,5},{5,9},{9,13},{13,1},{2,6},{6,10},{... | collective-permute-start | bytes 491528 | tf_op jit(solution)/shard_map/ppermute | solution.py:336
  6.6 9.2 %collective-permute-start.3 = (f32[10,16,256]{2,1,0:T(8,128)S(1)}, f32[10,16,256]{2,1,0:T(8,128)S(1)}, u32[]{:S(2)}, u32[]{:S(2)}) collective-permute-start(f32[10,16,256]{2,1,0:T(8,128)S(1)} %get-tuple-element.38), channel_id=1, source_target_pairs={{0,12},{4,0},{8,4},{12,8},{1,13},{5,1},{9,5},{13,9},{2,14},{6,2},{... | collective-permute-start | bytes 491528 | tf_op jit(solution)/shard_map/ppermute | solution.py:336
  16.2 7.1 %collective-permute-start.4 = (f32[12,8,256]{2,1,0:T(8,128)S(1)}, f32[12,8,256]{2,1,0:T(8,128)S(1)}, u32[]{:S(2)}, u32[]{:S(2)}) collective-permute-start(f32[12,8,256]{2,1,0:T(8,128)S(1)} %get-tuple-element.42), channel_id=1, source_target_pairs={{0,4},{4,8},{8,12},{12,0},{1,5},{5,9},{9,13},{13,1},{2,6},{6,10},{... | collective-permute-start | bytes 294920 | tf_op jit(solution)/shard_map/ppermute | solution.py:336
  17.4 6.5 %collective-permute-start.5 = (f32[12,8,256]{2,1,0:T(8,128)S(1)}, f32[12,8,256]{2,1,0:T(8,128)S(1)}, u32[]{:S(2)}, u32[]{:S(2)}) collective-permute-start(f32[12,8,256]{2,1,0:T(8,128)S(1)} %get-tuple-element.43), channel_id=1, source_target_pairs={{0,12},{4,0},{8,4},{12,8},{1,13},{5,1},{9,5},{13,9},{2,14},{6,2},{... | collective-permute-start | bytes 294920 | tf_op jit(solution)/shard_map/ppermute | solution.py:336
  24.0 10.0 %collective-permute-start.6 = (f32[32,8,256]{2,1,0:T(8,128)S(1)}, f32[32,8,256]{2,1,0:T(8,128)S(1)}, u32[]{:S(2)}, u32[]{:S(2)}) collective-permute-start(f32[32,8,256]{2,1,0:T(8,128)S(1)} %get-tuple-element.44), channel_id=1, source_target_pairs={{0,16},{16,17},{17,1},{1,2},{2,18},{18,19},{19,3},{3,0},{4,20},{20... | collective-permute-start | bytes 786440 | tf_op jit(solution)/shard_map/ppermute | solution.py:335
  24.1 9.9 %collective-permute-start.7 = (f32[32,8,256]{2,1,0:T(8,128)S(1)}, f32[32,8,256]{2,1,0:T(8,128)S(1)}, u32[]{:S(2)}, u32[]{:S(2)}) collective-permute-start(f32[32,8,256]{2,1,0:T(8,128)S(1)} %get-tuple-element.45), channel_id=1, source_target_pairs={{0,3},{16,0},{17,16},{1,17},{2,1},{18,2},{19,18},{3,19},{4,7},{20,... | collective-permute-start | bytes 786440 | tf_op jit(solution)/shard_map/ppermute | solution.py:335
  25.8 8.2 %collective-permute-start.8 = (f32[16,8,256]{2,1,0:T(8,128)S(1)}, f32[16,8,256]{2,1,0:T(8,128)S(1)}, u32[]{:S(2)}, u32[]{:S(2)}) collective-permute-start(f32[16,8,256]{2,1,0:T(8,128)S(1)} %get-tuple-element.46), channel_id=1, source_target_pairs={{0,4},{4,8},{8,12},{12,0},{1,5},{5,9},{9,13},{13,1},{2,6},{6,10},{... | collective-permute-start | bytes 393224 | tf_op jit(solution)/shard_map/ppermute | solution.py:336
  26.2 7.8 %collective-permute-start.9 = (f32[16,8,256]{2,1,0:T(8,128)S(1)}, f32[16,8,256]{2,1,0:T(8,128)S(1)}, u32[]{:S(2)}, u32[]{:S(2)}) collective-permute-start(f32[16,8,256]{2,1,0:T(8,128)S(1)} %get-tuple-element.47), channel_id=1, source_target_pairs={{0,12},{4,0},{8,4},{12,8},{1,13},{5,1},{9,5},{13,9},{2,14},{6,2},{... | collective-permute-start | bytes 393224 | tf_op jit(solution)/shard_map/ppermute | solution.py:336
  35.9 6.6 %collective-permute-start.10 = (f32[12,8,256]{2,1,0:T(8,128)S(1)}, f32[12,8,256]{2,1,0:T(8,128)S(1)}, u32[]{:S(2)}, u32[]{:S(2)}) collective-permute-start(f32[12,8,256]{2,1,0:T(8,128)S(1)} %get-tuple-element.52), channel_id=1, source_target_pairs={{0,4},{4,8},{8,12},{12,0},{1,5},{5,9},{9,13},{13,1},{2,6},{6,10},{... | collective-permute-start | bytes 294920 | tf_op jit(solution)/shard_map/ppermute | solution.py:336
  37.2 5.8 %collective-permute-start.11 = (f32[12,8,256]{2,1,0:T(8,128)S(1)}, f32[12,8,256]{2,1,0:T(8,128)S(1)}, u32[]{:S(2)}, u32[]{:S(2)}) collective-permute-start(f32[12,8,256]{2,1,0:T(8,128)S(1)} %get-tuple-element.53), channel_id=1, source_target_pairs={{0,12},{4,0},{8,4},{12,8},{1,13},{5,1},{9,5},{13,9},{2,14},{6,2},{... | collective-permute-start | bytes 294920 | tf_op jit(solution)/shard_map/ppermute | solution.py:336
  43.0 10.2 %collective-permute-start.12 = (f32[28,8,256]{2,1,0:T(8,128)S(1)}, f32[28,8,256]{2,1,0:T(8,128)S(1)}, u32[]{:S(2)}, u32[]{:S(2)}) collective-permute-start(f32[28,8,256]{2,1,0:T(8,128)S(1)} %get-tuple-element.54), channel_id=1, source_target_pairs={{0,16},{16,17},{17,1},{1,2},{2,18},{18,19},{19,3},{3,0},{4,20},{20... | collective-permute-start | bytes 688136 | tf_op jit(solution)/shard_map/ppermute | solution.py:335
  43.1 10.1 %collective-permute-start.13 = (f32[28,8,256]{2,1,0:T(8,128)S(1)}, f32[28,8,256]{2,1,0:T(8,128)S(1)}, u32[]{:S(2)}, u32[]{:S(2)}) collective-permute-start(f32[28,8,256]{2,1,0:T(8,128)S(1)} %get-tuple-element.55), channel_id=1, source_target_pairs={{0,3},{16,0},{17,16},{1,17},{2,1},{18,2},{19,18},{3,19},{4,7},{20,... | collective-permute-start | bytes 688136 | tf_op jit(solution)/shard_map/ppermute | solution.py:335
  44.8 7.8 %collective-permute-start.14 = (f32[16,8,256]{2,1,0:T(8,128)S(1)}, f32[16,8,256]{2,1,0:T(8,128)S(1)}, u32[]{:S(2)}, u32[]{:S(2)}) collective-permute-start(f32[16,8,256]{2,1,0:T(8,128)S(1)} %get-tuple-element.56), channel_id=1, source_target_pairs={{0,4},{4,8},{8,12},{12,0},{1,5},{5,9},{9,13},{13,1},{2,6},{6,10},{... | collective-permute-start | bytes 393224 | tf_op jit(solution)/shard_map/ppermute | solution.py:336
  45.8 7.4 %collective-permute-start.15 = (f32[16,8,256]{2,1,0:T(8,128)S(1)}, f32[16,8,256]{2,1,0:T(8,128)S(1)}, u32[]{:S(2)}, u32[]{:S(2)}) collective-permute-start(f32[16,8,256]{2,1,0:T(8,128)S(1)} %get-tuple-element.57), channel_id=1, source_target_pairs={{0,12},{4,0},{8,4},{12,8},{1,13},{5,1},{9,5},{13,9},{2,14},{6,2},{... | collective-permute-start | bytes 393224 | tf_op jit(solution)/shard_map/ppermute | solution.py:336
  55.6 7.0 %collective-permute-start.16 = (f32[16,16,256]{2,1,0:T(8,128)S(1)}, f32[16,16,256]{2,1,0:T(8,128)S(1)}, u32[]{:S(2)}, u32[]{:S(2)}) collective-permute-start(f32[16,16,256]{2,1,0:T(8,128)S(1)} %get-tuple-element.59), channel_id=1, source_target_pairs={{0,16},{16,0},{1,17},{17,1},{2,18},{18,2},{3,19},{19,3},{4,20},{20... | collective-permute-start | bytes 786440 | tf_op jit(solution)/shard_map/ppermute | solution.py:406

commit v5 on v4

--- a/solution.py
+++ b/solution.py
@@ -1,5 +1,3 @@
-import functools
-
 import jax
 import jax.numpy as jnp
 from jax import lax
@@ -80,10 +78,9 @@
     return first, rest
 
 
-def y_layout(planes, widths, corners):
-    at = len(widths) * planes
+def corner_layout(widths, at=0):
     where = {}
-    for k, width in enumerate(corners):
+    for k, width in enumerate(widths):
         for d in range(1, width + 1):
             rows = beyond(width, d)
             if rows > 0:
@@ -110,32 +107,35 @@
                         xb[rest[k, d, part]] = tile
 
 
-def pack_y(extra, *refs):
-    planes = refs[0].shape[0]
-    v, q, xla, xha = refs[:4]
-    y_up, y_down = refs[-2:]
-    corners = LATER + ((MID,) if extra else ())
-    where, _ = y_layout(planes, LATER, corners)
-    first, _ = x_layout(LATER)
+def put_shared(at, a_low, a_high, y_up, y_down):
+    y_up[at] = jnp.where(upper(), turned(a_high), a_low)
+    y_down[at] = jnp.where(upper(), a_low, turned(a_high))
+
+
+def pack_rows(*refs):
+    (v, q, *extra), (y_up, y_down) = refs[:-2], refs[-2:]
+    planes = v.shape[0]
     for k, f in enumerate((v, q)):
         y_up[pl.ds(k * planes, planes)] = f[:, TILE:, :]
         y_down[pl.ds(k * planes, planes)] = f[:, 0:TILE, :]
-    for (k, d), at in where.items():
-        if k == 2:
-            low, high = refs[4], refs[5]
-            i, j = 4 + MID - d, 4 + d - 1
-            a_low = jnp.where(upper(), low[i, 0:TILE, :], low[i, TILE:, :])
-            a_high = jnp.where(upper(), high[j, 0:TILE, :], high[j, TILE:, :])
+    if extra:
+        for (_, d), at in corner_layout((MID,), 2 * planes)[0].items():
+            low, high = extra[0].at[MID - d], extra[1].at[d - 1]
+            a_low = jnp.where(upper(), low[0:TILE, :], low[TILE:, :])
+            a_high = jnp.where(upper(), high[0:TILE, :], high[TILE:, :])
+            put_shared(at, a_low, a_high, y_up, y_down)
+
+
+def pack_corners(xla, xha, c_up, c_down):
+    first, _ = x_layout(LATER)
+    for (k, d), at in corner_layout(LATER)[0].items():
+        if beyond(LATER[k], d) > TILE // 2:
+            for side, x in ((0, xla), (1, xha)):
+                a, b = x[first[k, d, "A"]], x[first[k, d, "B"]]
+                c_up[at + side] = jnp.where(upper(), b, a)
+                c_down[at + side] = jnp.where(upper(), a, b)
         else:
-            a_low, a_high = xla[first[k, d, "A"]], xha[first[k, d, "A"]]
-        if beyond(corners[k], d) > TILE // 2:
-            for side, a, x in ((0, a_low, xla), (1, a_high, xha)):
-                b = x[first[k, d, "B"]]
-                y_up[at + side] = jnp.where(upper(), b, a)
-                y_down[at + side] = jnp.where(upper(), a, b)
-        else:
-            y_up[at] = jnp.where(upper(), turned(a_high), a_low)
-            y_down[at] = jnp.where(upper(), a_low, turned(a_high))
+            put_shared(at, xla[first[k, d, "A"]], xha[first[k, d, "A"]], c_up, c_down)
 
 
 def widen(out, width, centre, y_tile, x_tiles, corner):
@@ -157,20 +157,21 @@
                 out[to, 3 * TILE :, :] = jnp.zeros((TILE, depth), jnp.float32)
 
 
-def corner_of(k, corners, where, y):
+def corner_of(k, widths, where, c):
     def corner(side, y_side, d):
         at = where[k, d]
-        if beyond(corners[k], d) > TILE // 2:
-            return y[y_side][at + side]
-        tile = y[y_side][at]
+        if beyond(widths[k], d) > TILE // 2:
+            return c[y_side][at + side]
+        tile = c[y_side][at]
         return turned(tile) if side else tile
 
     return corner
 
 
-def widen_moved(outs, fields, corners, y, xa, xb):
+def widen_moved(outs, fields, halos):
+    y, xa, xb, c = (halos[i : i + 2] for i in range(0, 8, 2))
     planes = fields[0].shape[0]
-    where, _ = y_layout(planes, LATER, corners)
+    where, _ = corner_layout(LATER)
     first, rest = x_layout(LATER)
     for k, (out, f) in enumerate(zip(outs, fields)):
 
@@ -188,11 +189,12 @@
             f,
             lambda side, i: y[side][k * planes + i],
             x_tiles,
-            corner_of(k, corners, where, y),
+            corner_of(k, LATER, where, c),
         )
 
 
-def load_first(h, u, v, s, u_own, v_own, s_own, y_up, y_down, x_up, x_down, sems):
+def load_first(h, u, v, s, u_own, v_own, s_own, *rest):
+    x_up, x_down, y_up, y_down, s_up, s_down, sems = rest
     planes, half, _ = u_own.shape
     own = pl.ds(pl.multiple_of(h[0] * half, TILE), half)
     fields = (u_own, v_own, s_own)
@@ -204,25 +206,44 @@
         copy.start()
     for copy in copies:
         copy.wait()
-    at = 0
-    for k, (f, width) in enumerate(zip(fields, (2, 2, MID))):
-        x_up[pl.ds(at, width)] = f[planes - width :]
-        x_down[pl.ds(at, width)] = f[0:width]
-        y_up[pl.ds(k * planes, planes)] = f[:, TILE:, :]
-        y_down[pl.ds(k * planes, planes)] = f[:, 0:TILE, :]
-        at += width
+    for k, f in enumerate((u_own, v_own)):
+        x_up[pl.ds(2 * k, 2)] = f[planes - 2 :]
+        x_down[pl.ds(2 * k, 2)] = f[0:2]
+    s_up[...] = s_own[planes - MID :]
+    s_down[...] = s_own[0:MID]
+    pairs = planes // 2
+    group = lax.broadcasted_iota(jnp.int32, (TILE, 1), 0) // 2
+    for i in range(pairs):
+        shared = (u_own, i), (v_own, i), (u_own, i + pairs), (v_own, i + pairs)
+        top = bottom = None
+        for n, (f, plane) in enumerate(shared):
+            last, first = f[plane, TILE:, :], f[plane, 0:TILE, :]
+            if n == 0:
+                top, bottom = last, first
+            else:
+                top = jnp.where(group == 3 - n, pltpu.roll(last, TILE - 2 * n, 0), top)
+                bottom = jnp.where(group == n, pltpu.roll(first, 2 * n, 0), bottom)
+        y_up[i] = top
+        y_down[i] = bottom
+    y_up[pairs:] = s_own[:, TILE:, :]
+    y_down[pairs:] = s_own[:, 0:TILE, :]
 
 
 def first_step(u, v, s, yl, yh, xl, xh, u_out, v_out, q_out, *rest):
     sends, (u0, v0) = rest[:4], rest[4:]
     planes, _, _ = u.shape
+    pairs = planes // 2
     for k, (f, out) in enumerate(((u, u0), (v, v0))):
-        inner = pl.ds(2, planes)
-        out[inner, 0:TILE, :] = yl[pl.ds(k * planes, planes)]
-        out[inner, OWN, :] = f[...]
-        out[inner, 3 * TILE :, :] = yh[pl.ds(k * planes, planes)]
+        out[pl.ds(2, planes), OWN, :] = f[...]
         out[0:2, OWN, :] = xl[pl.ds(2 * k, 2)]
         out[planes + 2 :, OWN, :] = xh[pl.ds(2 * k, 2)]
+        for i in range(planes):
+            n = k + 2 * (i // pairs)
+            below, above = yl[i % pairs], yh[i % pairs]
+            if n > 0:
+                below, above = pltpu.roll(below, 2 * n, 0), pltpu.roll(above, TILE - 2 * n, 0)
+            out[2 + i, 0:TILE, :] = below
+            out[2 + i, 3 * TILE :, :] = above
     for i in range(planes):
         q, l = lap(u0, i + 2, OWN), lap(v0, i + 2, OWN)
         u_out[i] = u[i] + time_step * v[i]
@@ -243,25 +264,25 @@
             q_out[i - 2] = q[i] + time_step * l
 
 
-def middle_steps(u, v, q, s, yl, yh, xla, xha, xlb, xhb, ysl, ysh, xsl, xsh, *rest):
+def middle_steps(u, v, q, s, *rest):
+    halos, (ysl, ysh, xsl, xsh), rest = rest[:8], rest[8:12], rest[12:]
     (u_out, v_out, q_out, s_wide), sends = rest[:4], rest[4:8]
     v0, q0, v1, q1, v2, q2, v3, q3 = rest[8:]
     planes, _, _ = v.shape
-    corners = LATER + (MID,)
-    where, _ = y_layout(planes, LATER, corners)
+    where, _ = corner_layout((MID,), 2 * planes)
 
     def s_rows(side, d):
-        ref, i = ((xsl, 4 + MID - d), (xsh, 4 + d - 1))[side]
+        ref, i = ((xsl, MID - d), (xsh, d - 1))[side]
         return ref[i, 0:TILE, :], ref[i, TILE:, :]
 
-    widen_moved((v0, q0), (v, q), corners, (yl, yh), (xla, xha), (xlb, xhb))
+    widen_moved((v0, q0), (v, q), halos)
     widen(
         s_wide,
         MID,
         s,
-        lambda side, i: (ysl, ysh)[side][2 * planes + i],
+        lambda side, i: (ysl, ysh)[side][planes // 2 + i],
         s_rows,
-        corner_of(2, corners, where, (yl, yh)),
+        corner_of(0, (MID,), where, halos[:2]),
     )
     advance(planes, WIDE, v0, q0, s_wide, v1, q1)
     advance(planes, WIDE - 2, v1, q1, s_wide, v2, q2)
@@ -276,10 +297,11 @@
     pack_x((v_out, q_out), LATER, sends)
 
 
-def last_steps(scale, u, v, q, s_wide, yl, yh, xla, xha, xlb, xhb, keep, send, *scratch):
-    v0, q0, v1, q1, v2, q2, rate, l7 = scratch
+def last_steps(scale, u, v, q, s_wide, *rest):
+    halos, (keep, send) = rest[:8], rest[8:10]
+    v0, q0, v1, q1, v2, q2, rate, l7 = rest[10:]
     planes, _, _ = v.shape
-    widen_moved((v0, q0), (v, q), LATER, (yl, yh), (xla, xha), (xlb, xhb))
+    widen_moved((v0, q0), (v, q), halos)
     advance(planes, WIDE, v0, q0, s_wide, v1, q1)
     advance(planes, WIDE - 2, v1, q1, s_wide, v2, q2)
     count = planes + 4
@@ -326,29 +348,33 @@
     return [(place(t), place(t + step)) for t in range(2 * gy)]
 
 
-STARTS = ("a_up", "a_down", "b_up", "b_down", "y_up", "y_down")
+STARTS = ("a_up", "a_down", "b_up", "b_down", "y_up", "y_down", "c_up", "c_down")
+STARTS_FIRST = ("a_up", "a_down", "y_up", "y_down", "s_up", "s_down")
 
 
 def move(name, sent):
     step = 1 if name.endswith("up") else -1
-    if name.startswith("y"):
+    if name.startswith(("y", "c")):
         return lax.ppermute(sent, ("level", "gy"), strips(lax.axis_size("gy"), step))
     return lax.ppermute(sent, "gx", ring(lax.axis_size("gx"), step))
 
 
-def exchange_first(y_up, y_down, x_up, x_down):
-    xl, xh = move("a_up", x_up), move("a_down", x_down)
-    return move("y_up", y_up), move("y_down", y_down), xl, xh
+def exchange_first(sends):
+    return [move(name, sent) for name, sent in zip(STARTS_FIRST, sends)]
 
 
 def exchange(v, q, sends, extra):
     planes, _, depth = v.shape
     xla, xha, xlb, xhb = (move(name, sent) for name, sent in zip(STARTS, sends))
-    corners = LATER + ((MID,) if extra else ())
-    y = spec(y_layout(planes, LATER, corners)[1], TILE, depth)
-    kernel = functools.partial(pack_y, bool(extra))
-    y_up, y_down = call(kernel, [y, y], (v, q, xla, xha, *extra))
-    return move("y_up", y_up), move("y_down", y_down), xla, xha, xlb, xhb
+    count = 2 * planes
+    if extra:
+        count = corner_layout((MID,), count)[1]
+    y = spec(count, TILE, depth)
+    y_up, y_down = call(pack_rows, [y, y], (v, q, *extra))
+    yl, yh = move("y_up", y_up), move("y_down", y_down)
+    c = spec(corner_layout(LATER)[1], TILE, depth)
+    c_up, c_down = call(pack_corners, [c, c], (xla, xha))
+    return yl, yh, xla, xha, xlb, xhb, move("c_up", c_up), move("c_down", c_down)
 
 
 def edge_specs(depth, widths):
@@ -370,8 +396,8 @@
     work = 100 * u.size
     sent = edge_specs(depth, LATER)
 
-    y, x = spec(3 * planes, TILE, depth), spec(4 + MID, half, depth)
-    outs = [block] * 3 + [y, y, x, x]
+    x, y, xs = spec(4, half, depth), spec(planes * 3 // 2, TILE, depth), spec(MID, half, depth)
+    outs = [block] * 3 + [x, x, y, y, xs, xs]
     u, v, s, *sends = pl.pallas_call(
         load_first,
         out_shape=outs,
@@ -380,15 +406,14 @@
         scratch_shapes=[pltpu.SemaphoreType.DMA((3,))],
         compiler_params=pltpu.CompilerParams(vmem_limit_bytes=14 << 20),
     )(h, *(pltpu.with_memory_space_constraint(f, pltpu.HBM) for f in (u, v, s)))
-    halos = exchange_first(*sends)
-    ysl, ysh, xsl, xsh = halos
-    args = (u, v, s, *halos)
+    xl, xh, yl, yh, xsl, xsh = exchange_first(sends)
+    args = (u, v, s, yl, yh, xl, xh)
     u, v, q, *sends = call(first_step, [block] * 3 + sent, args, (), (slim, slim), work)
     halos = exchange(v, q, sends, (xsl, xsh))
     u, v, q, s_wide, *sends = call(
         middle_steps,
         [block] * 3 + [spec(*mid)] + sent,
-        (u, v, q, s, *halos, ysl, ysh, xsl, xsh),
+        (u, v, q, s, *halos, yl, yh, xsl, xsh),
         (),
         (wide, mid, mid, thin, thin, slim, slim, bare),
         work,

time: 63.6 us -> 60.8 us (0.956)
  waiting for transfers between devices: 30.1 us -> 24.8 us
  starting transfers between devices: 26 us -> 28.4 us
    ppermute x10 -> x12, waiting for transfers between devices: 23.1 us -> 11.8 us  [move(): return lax.ppermute(sent, 'gx', ring(lax.axis_size('gx'), step))]
    ppermute x6 -> x10, waiting for transfers between devices: 0.02 us -> 5.46 us  [move(): lax.ppermute(sent, ('level', 'gy'), strips(lax.axis_size('gy'), step))]
    ppermute x6 -> x10, starting transfers between devices: 6.64 us -> 9.55 us  [move(): lax.ppermute(sent, ('level', 'gy'), strips(lax.axis_size('gy'), step))]
    ppermute x10 -> x12, starting transfers between devices: 19.3 us -> 18 us  [move(): return lax.ppermute(sent, 'gx', ring(lax.axis_size('gx'), step))]
    ppermute x1, starting transfers between devices: 0.07 us -> 0.85 us  [body(): got = lax.ppermute(send, 'level', ring(2, 1))]
    pallas_call x6 -> x8, Pallas kernels: 5.52 us -> 5.55 us  [call(): pl.pallas_call(kernel, out_shape=outs, in_specs=[SMEM] * len(scalars) + [...]
  transfers between devices with their start and end apart: 17 -> 23, of which waited for: 10 -> 12; matrix products, arithmetic and copies ran while one was open for 0% -> 0% of each run, Pallas kernels for 0% -> 1%
where the time goes in v5:
time: 60.8 us; the launch traced here: 60.6 us
  starting transfers between devices  28.4 us (47%)
  waiting for transfers between devices  24.8 us (41%)
  Pallas kernels  6.65 us (11%)
  between operations  0.72 us (1%)
    ppermute x12, starting transfers between devices, move(): return lax.ppermute(sent, 'gx', ring(lax.axis_size('gx'), step))  18 us
    ppermute x12, waiting for transfers between devices, move(): return lax.ppermute(sent, 'gx', ring(lax.axis_size('gx'), step))  11.8 us
    ppermute x10, starting transfers between devices, move(): lax.ppermute(sent, ('level', 'gy'), strips(lax.axis_size('gy'), step))  9.55 us
    ppermute x1, waiting for transfers between devices, body(): got = lax.ppermute(send, 'level', ring(2, 1))  7.54 us
    pallas_call x8, Pallas kernels, call(): pl.pallas_call(kernel, out_shape=outs, in_specs=[SMEM] * len(scalars) + [...  5.55 us
    ppermute x10, waiting for transfers between devices, move(): lax.ppermute(sent, ('level', 'gy'), strips(lax.axis_size('gy'), step))  5.46 us
  transfers between devices with their start and end apart: 23, of which 12 were waited for; matrix products, arithmetic and copies ran while one was open for 0% of the time, Pallas kernels for 1%

profile of v5, /device:TPU:0, one launch (start us, length us, event | category | flops | bytes accessed | tf_op | source)
XLA Modules:
  0.0 60.6 jit_solution(16100229933382299171)
XLA Ops:
  0.6 1.1 %shard_map.50 = (f32[8,16,256]{2,1,0:T(8,128)S(1)}, f32[8,16,256]{2,1,0:T(8,128)S(1)}, f32[8,16,256]{2,1,0:T(8,128)S(1)}, f32[4,16,256]{2,1,0:T(8,128)S(1)}, f32...) custom-call(s32[1]{0:T(128)} %bitcast.h, ...), custom_call_target="tpu_custom_call" | custom-call | tf_op jit(solution)/shard_map/pallas_call | solution.py:401
  1.7 3.0 %collective-permute-start = (f32[12,8,256]{2,1,0:T(8,128)S(1)}, f32[12,8,256]{2,1,0:T(8,128)S(1)}, u32[]{:S(2)}, u32[]{:S(2)}) collective-permute-start(f32[12,8,256]{2,1,0:T(8,128)S(1)} %get-tuple-element.41), channel_id=1, source_target_pairs={{0,16},{16,17},{17,1},{1,2},{2,18},{18,19},{19,3},{3,0},{4,20},{20... | collective-permute-start | bytes 294920 | tf_op jit(solution)/shard_map/ppermute | solution.py:358
  4.8 0.0 collective-permute-start.1
  4.8 1.8 %collective-permute-start.2 = (f32[4,16,256]{2,1,0:T(8,128)S(1)}, f32[4,16,256]{2,1,0:T(8,128)S(1)}, u32[]{:S(2)}, u32[]{:S(2)}) collective-permute-start(f32[4,16,256]{2,1,0:T(8,128)S(1)} %get-tuple-element.43), channel_id=1, source_target_pairs={{0,4},{4,8},{8,12},{12,0},{1,5},{5,9},{9,13},{13,1},{2,6},{6,10},{... | collective-permute-start | bytes 196616 | tf_op jit(solution)/shard_map/ppermute | solution.py:359
  6.6 2.0 %collective-permute-start.3 = (f32[4,16,256]{2,1,0:T(8,128)S(1)}, f32[4,16,256]{2,1,0:T(8,128)S(1)}, u32[]{:S(2)}, u32[]{:S(2)}) collective-permute-start(f32[4,16,256]{2,1,0:T(8,128)S(1)} %get-tuple-element.44), channel_id=1, source_target_pairs={{0,12},{4,0},{8,4},{12,8},{1,13},{5,1},{9,5},{13,9},{2,14},{6,2},{... | collective-permute-start | bytes 196616 | tf_op jit(solution)/shard_map/ppermute | solution.py:359
  8.6 0.0 collective-permute-start.4
  8.6 2.3 %collective-permute-done.2.xl = f32[4,16,256]{2,1,0:T(8,128)S(1)} collective-permute-done((f32[4,16,256]{2,1,0:T(8,128)S(1)}, f32[4,16,256]{2,1,0:T(8,128)S(1)}, u32[]{:S(2)}, u32[]{:S(2)}) %collective-permute-start.2) | collective-permute-done | bytes 65568 | tf_op jit(solution)/shard_map/ppermute | solution.py:359
  10.9 3.0 %collective-permute-start.5 = (f32[6,16,256]{2,1,0:T(8,128)S(1)}, f32[6,16,256]{2,1,0:T(8,128)S(1)}, u32[]{:S(2)}, u32[]{:S(2)}) collective-permute-start(f32[6,16,256]{2,1,0:T(8,128)S(1)} %get-tuple-element.49), channel_id=1, source_target_pairs={{0,12},{4,0},{8,4},{12,8},{1,13},{5,1},{9,5},{13,9},{2,14},{6,2},{... | collective-permute-start | bytes 294920 | tf_op jit(solution)/shard_map/ppermute | solution.py:359
  13.9 0.0 collective-permute-done.3.xh
  13.9 0.0 collective-permute-done.yl.rest_8_
  13.9 0.0 collective-permute-done.1.yh.rest_9_
  13.9 0.4 shard_map.51
  14.3 0.1 collective-permute-start.8
  14.4 0.3 collective-permute-start.10
  14.7 3.5 %collective-permute-start.9 = (f32[12,8,256]{2,1,0:T(8,128)S(1)}, f32[12,8,256]{2,1,0:T(8,128)S(1)}, u32[]{:S(2)}, u32[]{:S(2)}) collective-permute-start(f32[12,8,256]{2,1,0:T(8,128)S(1)} %get-tuple-element.53), channel_id=1, source_target_pairs={{0,12},{4,0},{8,4},{12,8},{1,13},{5,1},{9,5},{13,9},{2,14},{6,2},{... | collective-permute-start | bytes 294920 | tf_op jit(solution)/shard_map/ppermute | solution.py:359
  18.3 0.0 collective-permute-done.4.refs_2_.rest_10_
  18.3 1.7 %collective-permute-done.5.refs_3_.rest_11_ = f32[6,16,256]{2,1,0:T(8,128)S(1)} collective-permute-done((f32[6,16,256]{2,1,0:T(8,128)S(1)}, f32[6,16,256]{2,1,0:T(8,128)S(1)}, u32[]{:S(2)}, u32[]{:S(2)}) %collective-permute-start.5) | collective-permute-done | bytes 98336 | tf_op jit(solution)/shard_map/ppermute | solution.py:359
  20.0 2.0 %collective-permute-start.6 = (f32[20,8,256]{2,1,0:T(8,128)S(1)}, f32[20,8,256]{2,1,0:T(8,128)S(1)}, u32[]{:S(2)}, u32[]{:S(2)}) collective-permute-start(f32[20,8,256]{2,1,0:T(8,128)S(1)} %get-tuple-element.50), channel_id=1, source_target_pairs={{0,16},{16,17},{17,1},{1,2},{2,18},{18,19},{19,3},{3,0},{4,20},{20... | collective-permute-start | bytes 491528 | tf_op jit(solution)/shard_map/ppermute | solution.py:358
  22.0 0.0 collective-permute-start.7
  22.0 0.0 collective-permute-done.8.xla.rest_2_
  22.0 1.3 %collective-permute-start.11 = (f32[16,8,256]{2,1,0:T(8,128)S(1)}, f32[16,8,256]{2,1,0:T(8,128)S(1)}, u32[]{:S(2)}, u32[]{:S(2)}) collective-permute-start(f32[16,8,256]{2,1,0:T(8,128)S(1)} %get-tuple-element.55), channel_id=1, source_target_pairs={{0,12},{4,0},{8,4},{12,8},{1,13},{5,1},{9,5},{13,9},{2,14},{6,2},{... | collective-permute-start | bytes 393224 | tf_op jit(solution)/shard_map/ppermute | solution.py:359
  23.3 0.5 collective-permute-done.9.xha.rest_3_
  23.9 1.4 %collective-permute-start.12 = (f32[12,8,256]{2,1,0:T(8,128)S(1)}, f32[12,8,256]{2,1,0:T(8,128)S(1)}, u32[]{:S(2)}, u32[]{:S(2)}) collective-permute-start(f32[12,8,256]{2,1,0:T(8,128)S(1)} %get-tuple-element.56), channel_id=1, source_target_pairs={{0,16},{16,17},{17,1},{1,2},{2,18},{18,19},{19,3},{3,0},{4,20},{20... | collective-permute-start | bytes 294920 | tf_op jit(solution)/shard_map/ppermute | solution.py:358
  25.3 0.0 collective-permute-done.10.rest_4_
  25.3 0.4 collective-permute-start.13
  25.7 1.8 %collective-permute-done.11.rest_5_ = f32[16,8,256]{2,1,0:T(8,128)S(1)} collective-permute-done((f32[16,8,256]{2,1,0:T(8,128)S(1)}, f32[16,8,256]{2,1,0:T(8,128)S(1)}, u32[]{:S(2)}, u32[]{:S(2)}) %collective-permute-start.11) | collective-permute-done | bytes 131104 | tf_op jit(solution)/shard_map/ppermute | solution.py:359
  27.5 0.0 collective-permute-done.6.rest_0_
  27.5 0.9 %collective-permute-done.7.rest_1_ = f32[20,8,256]{2,1,0:T(8,128)S(1)} collective-permute-done((f32[20,8,256]{2,1,0:T(8,128)S(1)}, f32[20,8,256]{2,1,0:T(8,128)S(1)}, u32[]{:S(2)}, u32[]{:S(2)}) %collective-permute-start.7) | collective-permute-done | bytes 163872 | tf_op jit(solution)/shard_map/ppermute | solution.py:358
  28.4 0.0 collective-permute-done.12.rest_6_
  28.4 1.5 %collective-permute-done.13.rest_7_ = f32[12,8,256]{2,1,0:T(8,128)S(1)} collective-permute-done((f32[12,8,256]{2,1,0:T(8,128)S(1)}, f32[12,8,256]{2,1,0:T(8,128)S(1)}, u32[]{:S(2)}, u32[]{:S(2)}) %collective-permute-start.13) | collective-permute-done | bytes 98336 | tf_op jit(solution)/shard_map/ppermute | solution.py:358
  29.9 1.9 %shard_map.54 = (f32[8,16,256]{2,1,0:T(8,128)S(1)}, f32[8,16,256]{2,1,0:T(8,128)S(1)}, f32[8,16,256]{2,1,0:T(8,128)S(1)}, f32[20,32,256]{2,1,0:T(8,128)S(1)}, f3...) custom-call(f32[8,16,256]{2,1,0:T(8,128)S(1)} %get-tuple-element.45., ...), custom_call_target="tpu_custom_call" | custom-call | flops 6553600 | bytes 3407872 | tf_op jit(solution)/shard_map/pallas_call | solution.py:35
  31.8 0.9 %collective-permute-start.18 = (f32[16,8,256]{2,1,0:T(8,128)S(1)}, f32[16,8,256]{2,1,0:T(8,128)S(1)}, u32[]{:S(2)}, u32[]{:S(2)}) collective-permute-start(f32[16,8,256]{2,1,0:T(8,128)S(1)} %get-tuple-element.66), channel_id=1, source_target_pairs={{0,4},{4,8},{8,12},{12,0},{1,5},{5,9},{9,13},{13,1},{2,6},{6,10},{... | collective-permute-start | bytes 393224 | tf_op jit(solution)/shard_map/ppermute | solution.py:359
  32.7 0.8 %collective-permute-start.16 = (f32[12,8,256]{2,1,0:T(8,128)S(1)}, f32[12,8,256]{2,1,0:T(8,128)S(1)}, u32[]{:S(2)}, u32[]{:S(2)}) collective-permute-start(f32[12,8,256]{2,1,0:T(8,128)S(1)} %get-tuple-element.64), channel_id=1, source_target_pairs={{0,4},{4,8},{8,12},{12,0},{1,5},{5,9},{9,13},{13,1},{2,6},{6,10},{... | collective-permute-start | bytes 294920 | tf_op jit(solution)/shard_map/ppermute | solution.py:359
  33.5 3.0 %collective-permute-start.17 = (f32[12,8,256]{2,1,0:T(8,128)S(1)}, f32[12,8,256]{2,1,0:T(8,128)S(1)}, u32[]{:S(2)}, u32[]{:S(2)}) collective-permute-start(f32[12,8,256]{2,1,0:T(8,128)S(1)} %get-tuple-element.65), channel_id=1, source_target_pairs={{0,12},{4,0},{8,4},{12,8},{1,13},{5,1},{9,5},{13,9},{2,14},{6,2},{... | collective-permute-start | bytes 294920 | tf_op jit(solution)/shard_map/ppermute | solution.py:359
  36.5 1.2 %collective-permute-start.19 = (f32[16,8,256]{2,1,0:T(8,128)S(1)}, f32[16,8,256]{2,1,0:T(8,128)S(1)}, u32[]{:S(2)}, u32[]{:S(2)}) collective-permute-start(f32[16,8,256]{2,1,0:T(8,128)S(1)} %get-tuple-element.67), channel_id=1, source_target_pairs={{0,12},{4,0},{8,4},{12,8},{1,13},{5,1},{9,5},{13,9},{2,14},{6,2},{... | collective-permute-start | bytes 393224 | tf_op jit(solution)/shard_map/ppermute | solution.py:359
  37.7 0.9 %collective-permute-start.14 = (f32[16,8,256]{2,1,0:T(8,128)S(1)}, f32[16,8,256]{2,1,0:T(8,128)S(1)}, u32[]{:S(2)}, u32[]{:S(2)}) collective-permute-start(f32[16,8,256]{2,1,0:T(8,128)S(1)} %get-tuple-element.62), channel_id=1, source_target_pairs={{0,16},{16,17},{17,1},{1,2},{2,18},{18,19},{19,3},{3,0},{4,20},{20... | collective-permute-start | bytes 393224 | tf_op jit(solution)/shard_map/ppermute | solution.py:358
  38.6 3.5 %collective-permute-done.16.xla.rest_2_ = f32[12,8,256]{2,1,0:T(8,128)S(1)} collective-permute-done((f32[12,8,256]{2,1,0:T(8,128)S(1)}, f32[12,8,256]{2,1,0:T(8,128)S(1)}, u32[]{:S(2)}, u32[]{:S(2)}) %collective-permute-start.16) | collective-permute-done | bytes 98336 | tf_op jit(solution)/shard_map/ppermute | solution.py:359
  42.1 0.0 collective-permute-start.15
  42.1 1.5 %collective-permute-done.17.xha.rest_3_ = f32[12,8,256]{2,1,0:T(8,128)S(1)} collective-permute-done((f32[12,8,256]{2,1,0:T(8,128)S(1)}, f32[12,8,256]{2,1,0:T(8,128)S(1)}, u32[]{:S(2)}, u32[]{:S(2)}) %collective-permute-start.17) | collective-permute-done | bytes 98336 | tf_op jit(solution)/shard_map/ppermute | solution.py:359
  43.7 0.7 %collective-permute-start.20 = (f32[12,8,256]{2,1,0:T(8,128)S(1)}, f32[12,8,256]{2,1,0:T(8,128)S(1)}, u32[]{:S(2)}, u32[]{:S(2)}) collective-permute-start(f32[12,8,256]{2,1,0:T(8,128)S(1)} %get-tuple-element.68), channel_id=1, source_target_pairs={{0,16},{16,17},{17,1},{1,2},{2,18},{18,19},{19,3},{3,0},{4,20},{20... | collective-permute-start | bytes 294920 | tf_op jit(solution)/shard_map/ppermute | solution.py:358
  44.4 0.0 collective-permute-done.18.rest_4_
  44.4 1.1 %collective-permute-start.21 = (f32[12,8,256]{2,1,0:T(8,128)S(1)}, f32[12,8,256]{2,1,0:T(8,128)S(1)}, u32[]{:S(2)}, u32[]{:S(2)}) collective-permute-start(f32[12,8,256]{2,1,0:T(8,128)S(1)} %get-tuple-element.69), channel_id=1, source_target_pairs={{0,3},{16,0},{17,16},{1,17},{2,1},{18,2},{19,18},{3,19},{4,7},{20,... | collective-permute-start | bytes 294920 | tf_op jit(solution)/shard_map/ppermute | solution.py:358
  45.5 0.1 pad_maximum_fusion.scale
  45.5 0.4 collective-permute-done.19.rest_5_
  46.0 0.0 collective-permute-done.14.rest_0_
  46.0 2.0 %collective-permute-done.15.rest_1_ = f32[16,8,256]{2,1,0:T(8,128)S(1)} collective-permute-done((f32[16,8,256]{2,1,0:T(8,128)S(1)}, f32[16,8,256]{2,1,0:T(8,128)S(1)}, u32[]{:S(2)}, u32[]{:S(2)}) %collective-permute-start.15) | collective-permute-done | bytes 131104 | tf_op jit(solution)/shard_map/ppermute | solution.py:358
  48.0 0.0 collective-permute-done.20.rest_6_
  48.0 1.1 %collective-permute-done.21.rest_7_ = f32[12,8,256]{2,1,0:T(8,128)S(1)} collective-permute-done((f32[12,8,256]{2,1,0:T(8,128)S(1)}, f32[12,8,256]{2,1,0:T(8,128)S(1)}, u32[]{:S(2)}, u32[]{:S(2)}) %collective-permute-start.21) | collective-permute-done | bytes 98336 | tf_op jit(solution)/shard_map/ppermute | solution.py:358
  49.0 2.4 %shard_map.57 = (f32[16,16,256]{2,1,0:T(8,128)S(1)}, f32[16,16,256]{2,1,0:T(8,128)S(1)}) custom-call(f32[2]{0:T(128)S(1)} %pad_maximum_fusion.scale, f32[8,16,256]{2,1,0:T(8,128)S(1)} %get-tuple-element.58.u, f32[8,16,256]{2,1,0:T(8,128)S(1)} %get-tuple-element.59.refs_0_.v, f32[8,16,256]{2,1,0:T(8,128)S(1)} %get-tuple-element.60.refs_1_.q, ...), custom_call_target="tpu_custom_call" | custom-call | flops 6553600 | bytes 2490368 | tf_op jit(solution)/shard_map/pallas_call | solution.py:35
  51.4 0.9 %collective-permute-start.22 = (f32[16,16,256]{2,1,0:T(8,128)S(1)}, f32[16,16,256]{2,1,0:T(8,128)S(1)}, u32[]{:S(2)}, u32[]{:S(2)}) collective-permute-start(f32[16,16,256]{2,1,0:T(8,128)S(1)} %get-tuple-element.71), channel_id=1, source_target_pairs={{0,16},{16,0},{1,17},{17,1},{2,18},{18,2},{3,19},{19,3},{4,20},{20... | collective-permute-start | bytes 786440 | tf_op jit(solution)/shard_map/ppermute | solution.py:431
  52.3 7.5 %collective-permute-done.22.got = f32[16,16,256]{2,1,0:T(8,128)S(1)} collective-permute-done((f32[16,16,256]{2,1,0:T(8,128)S(1)}, f32[16,16,256]{2,1,0:T(8,128)S(1)}, u32[]{:S(2)}, u32[]{:S(2)}) %collective-permute-start.22) | collective-permute-done | bytes 262176 | tf_op jit(solution)/shard_map/ppermute | solution.py:431
  59.8 0.8 %shard_map.58 = (f32[8,32,256]{2,1,0:T(8,128)}, f32[8,32,256]{2,1,0:T(8,128)}) custom-call(s32[1]{0:T(128)} %bitcast.h, f32[16,16,256]{2,1,0:T(8,128)S(1)} %get-tuple-element.70.keep, f32[16,16,256]{2,1,0:T(8,128)S(1)} %collective-permute-done.22.got), custom_call_target="tpu_custom_call" | custom-call | bytes 1048576 | tf_op jit(solution)/shard_map/pallas_call | solution.py:35
  (4 shorter events, 0.1 us)
Async XLA Ops:
  1.7 12.2 %collective-permute-start = (f32[12,8,256]{2,1,0:T(8,128)S(1)}, f32[12,8,256]{2,1,0:T(8,128)S(1)}, u32[]{:S(2)}, u32[]{:S(2)}) collective-permute-start(f32[12,8,256]{2,1,0:T(8,128)S(1)} %get-tuple-element.41), channel_id=1, source_target_pairs={{0,16},{16,17},{17,1},{1,2},{2,18},{18,19},{19,3},{3,0},{4,20},{20... | collective-permute-start | bytes 294920 | tf_op jit(solution)/shard_map/ppermute | solution.py:358
  4.8 9.1 %collective-permute-start.1 = (f32[12,8,256]{2,1,0:T(8,128)S(1)}, f32[12,8,256]{2,1,0:T(8,128)S(1)}, u32[]{:S(2)}, u32[]{:S(2)}) collective-permute-start(f32[12,8,256]{2,1,0:T(8,128)S(1)} %get-tuple-element.42), channel_id=1, source_target_pairs={{0,3},{16,0},{17,16},{1,17},{2,1},{18,2},{19,18},{3,19},{4,7},{20,... | collective-permute-start | bytes 294920 | tf_op jit(solution)/shard_map/ppermute | solution.py:358
  4.8 6.1 %collective-permute-start.2 = (f32[4,16,256]{2,1,0:T(8,128)S(1)}, f32[4,16,256]{2,1,0:T(8,128)S(1)}, u32[]{:S(2)}, u32[]{:S(2)}) collective-permute-start(f32[4,16,256]{2,1,0:T(8,128)S(1)} %get-tuple-element.43), channel_id=1, source_target_pairs={{0,4},{4,8},{8,12},{12,0},{1,5},{5,9},{9,13},{13,1},{2,6},{6,10},{... | collective-permute-start | bytes 196616 | tf_op jit(solution)/shard_map/ppermute | solution.py:359
  6.6 7.3 %collective-permute-start.3 = (f32[4,16,256]{2,1,0:T(8,128)S(1)}, f32[4,16,256]{2,1,0:T(8,128)S(1)}, u32[]{:S(2)}, u32[]{:S(2)}) collective-permute-start(f32[4,16,256]{2,1,0:T(8,128)S(1)} %get-tuple-element.44), channel_id=1, source_target_pairs={{0,12},{4,0},{8,4},{12,8},{1,13},{5,1},{9,5},{13,9},{2,14},{6,2},{... | collective-permute-start | bytes 196616 | tf_op jit(solution)/shard_map/ppermute | solution.py:359
  8.6 9.6 %collective-permute-start.4 = (f32[6,16,256]{2,1,0:T(8,128)S(1)}, f32[6,16,256]{2,1,0:T(8,128)S(1)}, u32[]{:S(2)}, u32[]{:S(2)}) collective-permute-start(f32[6,16,256]{2,1,0:T(8,128)S(1)} %get-tuple-element.48), channel_id=1, source_target_pairs={{0,4},{4,8},{8,12},{12,0},{1,5},{5,9},{9,13},{13,1},{2,6},{6,10},{... | collective-permute-start | bytes 294920 | tf_op jit(solution)/shard_map/ppermute | solution.py:359
  10.9 9.1 %collective-permute-start.5 = (f32[6,16,256]{2,1,0:T(8,128)S(1)}, f32[6,16,256]{2,1,0:T(8,128)S(1)}, u32[]{:S(2)}, u32[]{:S(2)}) collective-permute-start(f32[6,16,256]{2,1,0:T(8,128)S(1)} %get-tuple-element.49), channel_id=1, source_target_pairs={{0,12},{4,0},{8,4},{12,8},{1,13},{5,1},{9,5},{13,9},{2,14},{6,2},{... | collective-permute-start | bytes 294920 | tf_op jit(solution)/shard_map/ppermute | solution.py:359
  14.3 7.7 %collective-permute-start.8 = (f32[12,8,256]{2,1,0:T(8,128)S(1)}, f32[12,8,256]{2,1,0:T(8,128)S(1)}, u32[]{:S(2)}, u32[]{:S(2)}) collective-permute-start(f32[12,8,256]{2,1,0:T(8,128)S(1)} %get-tuple-element.52), channel_id=1, source_target_pairs={{0,4},{4,8},{8,12},{12,0},{1,5},{5,9},{9,13},{13,1},{2,6},{6,10},{... | collective-permute-start | bytes 294920 | tf_op jit(solution)/shard_map/ppermute | solution.py:359
  14.4 10.9 %collective-permute-start.10 = (f32[16,8,256]{2,1,0:T(8,128)S(1)}, f32[16,8,256]{2,1,0:T(8,128)S(1)}, u32[]{:S(2)}, u32[]{:S(2)}) collective-permute-start(f32[16,8,256]{2,1,0:T(8,128)S(1)} %get-tuple-element.54), channel_id=1, source_target_pairs={{0,4},{4,8},{8,12},{12,0},{1,5},{5,9},{9,13},{13,1},{2,6},{6,10},{... | collective-permute-start | bytes 393224 | tf_op jit(solution)/shard_map/ppermute | solution.py:359
  14.7 9.1 %collective-permute-start.9 = (f32[12,8,256]{2,1,0:T(8,128)S(1)}, f32[12,8,256]{2,1,0:T(8,128)S(1)}, u32[]{:S(2)}, u32[]{:S(2)}) collective-permute-start(f32[12,8,256]{2,1,0:T(8,128)S(1)} %get-tuple-element.53), channel_id=1, source_target_pairs={{0,12},{4,0},{8,4},{12,8},{1,13},{5,1},{9,5},{13,9},{2,14},{6,2},{... | collective-permute-start | bytes 294920 | tf_op jit(solution)/shard_map/ppermute | solution.py:359
  20.0 7.5 %collective-permute-start.6 = (f32[20,8,256]{2,1,0:T(8,128)S(1)}, f32[20,8,256]{2,1,0:T(8,128)S(1)}, u32[]{:S(2)}, u32[]{:S(2)}) collective-permute-start(f32[20,8,256]{2,1,0:T(8,128)S(1)} %get-tuple-element.50), channel_id=1, source_target_pairs={{0,16},{16,17},{17,1},{1,2},{2,18},{18,19},{19,3},{3,0},{4,20},{20... | collective-permute-start | bytes 491528 | tf_op jit(solution)/shard_map/ppermute | solution.py:358
  22.0 6.4 %collective-permute-start.7 = (f32[20,8,256]{2,1,0:T(8,128)S(1)}, f32[20,8,256]{2,1,0:T(8,128)S(1)}, u32[]{:S(2)}, u32[]{:S(2)}) collective-permute-start(f32[20,8,256]{2,1,0:T(8,128)S(1)} %get-tuple-element.51), channel_id=1, source_target_pairs={{0,3},{16,0},{17,16},{1,17},{2,1},{18,2},{19,18},{3,19},{4,7},{20,... | collective-permute-start | bytes 491528 | tf_op jit(solution)/shard_map/ppermute | solution.py:358
  22.0 5.5 %collective-permute-start.11 = (f32[16,8,256]{2,1,0:T(8,128)S(1)}, f32[16,8,256]{2,1,0:T(8,128)S(1)}, u32[]{:S(2)}, u32[]{:S(2)}) collective-permute-start(f32[16,8,256]{2,1,0:T(8,128)S(1)} %get-tuple-element.55), channel_id=1, source_target_pairs={{0,12},{4,0},{8,4},{12,8},{1,13},{5,1},{9,5},{13,9},{2,14},{6,2},{... | collective-permute-start | bytes 393224 | tf_op jit(solution)/shard_map/ppermute | solution.py:359
  23.9 4.5 %collective-permute-start.12 = (f32[12,8,256]{2,1,0:T(8,128)S(1)}, f32[12,8,256]{2,1,0:T(8,128)S(1)}, u32[]{:S(2)}, u32[]{:S(2)}) collective-permute-start(f32[12,8,256]{2,1,0:T(8,128)S(1)} %get-tuple-element.56), channel_id=1, source_target_pairs={{0,16},{16,17},{17,1},{1,2},{2,18},{18,19},{19,3},{3,0},{4,20},{20... | collective-permute-start | bytes 294920 | tf_op jit(solution)/shard_map/ppermute | solution.py:358
  25.3 4.6 %collective-permute-start.13 = (f32[12,8,256]{2,1,0:T(8,128)S(1)}, f32[12,8,256]{2,1,0:T(8,128)S(1)}, u32[]{:S(2)}, u32[]{:S(2)}) collective-permute-start(f32[12,8,256]{2,1,0:T(8,128)S(1)} %get-tuple-element.57), channel_id=1, source_target_pairs={{0,3},{16,0},{17,16},{1,17},{2,1},{18,2},{19,18},{3,19},{4,7},{20,... | collective-permute-start | bytes 294920 | tf_op jit(solution)/shard_map/ppermute | solution.py:358
  31.8 12.6 %collective-permute-start.18 = (f32[16,8,256]{2,1,0:T(8,128)S(1)}, f32[16,8,256]{2,1,0:T(8,128)S(1)}, u32[]{:S(2)}, u32[]{:S(2)}) collective-permute-start(f32[16,8,256]{2,1,0:T(8,128)S(1)} %get-tuple-element.66), channel_id=1, source_target_pairs={{0,4},{4,8},{8,12},{12,0},{1,5},{5,9},{9,13},{13,1},{2,6},{6,10},{... | collective-permute-start | bytes 393224 | tf_op jit(solution)/shard_map/ppermute | solution.py:359
  32.7 9.4 %collective-permute-start.16 = (f32[12,8,256]{2,1,0:T(8,128)S(1)}, f32[12,8,256]{2,1,0:T(8,128)S(1)}, u32[]{:S(2)}, u32[]{:S(2)}) collective-permute-start(f32[12,8,256]{2,1,0:T(8,128)S(1)} %get-tuple-element.64), channel_id=1, source_target_pairs={{0,4},{4,8},{8,12},{12,0},{1,5},{5,9},{9,13},{13,1},{2,6},{6,10},{... | collective-permute-start | bytes 294920 | tf_op jit(solution)/shard_map/ppermute | solution.py:359
  33.5 10.1 %collective-permute-start.17 = (f32[12,8,256]{2,1,0:T(8,128)S(1)}, f32[12,8,256]{2,1,0:T(8,128)S(1)}, u32[]{:S(2)}, u32[]{:S(2)}) collective-permute-start(f32[12,8,256]{2,1,0:T(8,128)S(1)} %get-tuple-element.65), channel_id=1, source_target_pairs={{0,12},{4,0},{8,4},{12,8},{1,13},{5,1},{9,5},{13,9},{2,14},{6,2},{... | collective-permute-start | bytes 294920 | tf_op jit(solution)/shard_map/ppermute | solution.py:359
  36.5 9.5 %collective-permute-start.19 = (f32[16,8,256]{2,1,0:T(8,128)S(1)}, f32[16,8,256]{2,1,0:T(8,128)S(1)}, u32[]{:S(2)}, u32[]{:S(2)}) collective-permute-start(f32[16,8,256]{2,1,0:T(8,128)S(1)} %get-tuple-element.67), channel_id=1, source_target_pairs={{0,12},{4,0},{8,4},{12,8},{1,13},{5,1},{9,5},{13,9},{2,14},{6,2},{... | collective-permute-start | bytes 393224 | tf_op jit(solution)/shard_map/ppermute | solution.py:359
  37.7 8.3 %collective-permute-start.14 = (f32[16,8,256]{2,1,0:T(8,128)S(1)}, f32[16,8,256]{2,1,0:T(8,128)S(1)}, u32[]{:S(2)}, u32[]{:S(2)}) collective-permute-start(f32[16,8,256]{2,1,0:T(8,128)S(1)} %get-tuple-element.62), channel_id=1, source_target_pairs={{0,16},{16,17},{17,1},{1,2},{2,18},{18,19},{19,3},{3,0},{4,20},{20... | collective-permute-start | bytes 393224 | tf_op jit(solution)/shard_map/ppermute | solution.py:358
  42.1 5.8 %collective-permute-start.15 = (f32[16,8,256]{2,1,0:T(8,128)S(1)}, f32[16,8,256]{2,1,0:T(8,128)S(1)}, u32[]{:S(2)}, u32[]{:S(2)}) collective-permute-start(f32[16,8,256]{2,1,0:T(8,128)S(1)} %get-tuple-element.63), channel_id=1, source_target_pairs={{0,3},{16,0},{17,16},{1,17},{2,1},{18,2},{19,18},{3,19},{4,7},{20,... | collective-permute-start | bytes 393224 | tf_op jit(solution)/shard_map/ppermute | solution.py:358
  43.7 4.3 %collective-permute-start.20 = (f32[12,8,256]{2,1,0:T(8,128)S(1)}, f32[12,8,256]{2,1,0:T(8,128)S(1)}, u32[]{:S(2)}, u32[]{:S(2)}) collective-permute-start(f32[12,8,256]{2,1,0:T(8,128)S(1)} %get-tuple-element.68), channel_id=1, source_target_pairs={{0,16},{16,17},{17,1},{1,2},{2,18},{18,19},{19,3},{3,0},{4,20},{20... | collective-permute-start | bytes 294920 | tf_op jit(solution)/shard_map/ppermute | solution.py:358
  44.4 4.6 %collective-permute-start.21 = (f32[12,8,256]{2,1,0:T(8,128)S(1)}, f32[12,8,256]{2,1,0:T(8,128)S(1)}, u32[]{:S(2)}, u32[]{:S(2)}) collective-permute-start(f32[12,8,256]{2,1,0:T(8,128)S(1)} %get-tuple-element.69), channel_id=1, source_target_pairs={{0,3},{16,0},{17,16},{1,17},{2,1},{18,2},{19,18},{3,19},{4,7},{20,... | collective-permute-start | bytes 294920 | tf_op jit(solution)/shard_map/ppermute | solution.py:358
  51.4 8.4 %collective-permute-start.22 = (f32[16,16,256]{2,1,0:T(8,128)S(1)}, f32[16,16,256]{2,1,0:T(8,128)S(1)}, u32[]{:S(2)}, u32[]{:S(2)}) collective-permute-start(f32[16,16,256]{2,1,0:T(8,128)S(1)} %get-tuple-element.71), channel_id=1, source_target_pairs={{0,16},{16,0},{1,17},{17,1},{2,18},{18,2},{3,19},{19,3},{4,20},{20... | collective-permute-start | bytes 786440 | tf_op jit(solution)/shard_map/ppermute | solution.py:431

commit v6 on v5

v6 whole, which is shorter than its diff:
```python
import functools

import jax
import jax.numpy as jnp
from jax import lax
from jax.experimental import pallas as pl
from jax.experimental.pallas import tpu as pltpu
from jax.sharding import PartitionSpec as P


STEPS = 8

time_step = 0.12
damping = 0.05
second = 0.5 * STEPS * time_step * time_step

NEAR = 4.0 / 3.0
FAR = -1.0 / 12.0

TILE = 8
WIDE = 8
MID = 6
LAST = ((WIDE, 1), (MID, 1))
SECOND = LAST + ((MID, 3),)
EARLY = 20

VMEM = pl.BlockSpec(memory_space=pltpu.VMEM)
SMEM = pl.BlockSpec(memory_space=pltpu.SMEM)
OWN = slice(TILE, 3 * TILE)
ALL = slice(0, 4 * TILE)


def spec(*shape):
    return jax.ShapeDtypeStruct(shape, jnp.float32)


def call(kernel, outs, args, scalars=(), scratch=(), flops=0):
    moved = 4 * (sum(a.size for a in args) + sum(o.size for o in outs))
    return pl.pallas_call(
        kernel,
        out_shape=outs,
        in_specs=[SMEM] * len(scalars) + [VMEM] * len(args),
        out_specs=[VMEM] * len(outs),
        scratch_shapes=[pltpu.VMEM(shape, jnp.float32) for shape in scratch],
        compiler_params=pltpu.CompilerParams(vmem_limit_bytes=14 << 20),
        cost_estimate=pl.CostEstimate(flops=flops, bytes_accessed=moved, transcendentals=0),
    )(*scalars, *args)


def upper():
    return lax.broadcasted_iota(jnp.int32, (TILE, 1), 0) < TILE // 2


def lap(ref, i, rows):
    full = ref[i]
    count, depth = full.shape
    w = full[rows]
    near = ref[i - 1, rows, :] + ref[i + 1, rows, :]
    far = ref[i - 2, rows, :] + ref[i + 2, rows, :]
    near += pltpu.roll(w, 1, 1) + pltpu.roll(w, depth - 1, 1)
    far += pltpu.roll(w, 2, 1) + pltpu.roll(w, depth - 2, 1)
    near += pltpu.roll(full, 1, 0)[rows] + pltpu.roll(full, count - 1, 0)[rows]
    far += pltpu.roll(full, 2, 0)[rows] + pltpu.roll(full, count - 2, 0)[rows]
    return -7.5 * w + NEAR * near + FAR * far


def beyond(width, d):
    return max(0, width - 2 * ((d + 1) // 2))


def x_layout(fields):
    first, rest = {}, []
    for k, (width, nearest) in enumerate(fields):
        for d in range(nearest, width + 1):
            for part, least in (("A", 0), ("B", TILE // 2)):
                if beyond(width, d) > least:
                    first[k, d, part] = len(first)
                else:
                    rest.append((k, d, part))
    while len(first) < EARLY + (4 if len(fields) > 2 else 0):
        first[rest.pop(0)] = len(first)
    return first, {key: at for at, key in enumerate(rest)}


def corner_layout(fields):
    where, at = {}, 0
    for k, (width, _) in enumerate(fields):
        for d in range(1, width + 1):
            rows = beyond(width, d)
            if rows > TILE // 2:
                where[k, d], at = at, at + 2
            elif rows > TILE // 4 or (rows > 0 and d % 2):
                where[k, d], at = at, at + 1
            elif rows > 0:
                where[k, d] = where[k, d - 1]
    return where, at


def share(tiles, last):
    size = TILE // len(tiles)
    group = lax.broadcasted_iota(jnp.int32, (TILE, 1), 0) // size
    out = tiles[0]
    for n, tile in enumerate(tiles):
        if n and last:
            out = jnp.where(group == len(tiles) - 1 - n, pltpu.roll(tile, TILE - size * n, 0), out)
        elif n:
            out = jnp.where(group == n, pltpu.roll(tile, size * n, 0), out)
    return out


def unshare(tile, count, n, last):
    turn = TILE // count * n
    return pltpu.roll(tile, turn if last else TILE - turn, 0) if n else tile


def pack_edges(blocks, fields, sends):
    a_up, a_down, y_up, y_down, b_up, b_down = sends
    first, rest = x_layout(fields)
    for k, (f, (width, nearest)) in enumerate(zip(blocks, fields)):
        planes = f.shape[0]
        for d in range(nearest, width + 1):
            for plane, xa, xb in ((planes - d, a_up, b_up), (d - 1, a_down, b_down)):
                low, high = f[plane, 0:TILE, :], f[plane, TILE:, :]
                for part, tile in (
                    ("A", jnp.where(upper(), low, high)),
                    ("B", jnp.where(upper(), high, low)),
                ):
                    if (k, d, part) in first:
                        xa[first[k, d, part]] = tile
                    else:
                        xb[rest[k, d, part]] = tile
        if k < len(LAST):
            y_up[pl.ds(k * planes, planes)] = f[:, TILE:, :]
            y_down[pl.ds(k * planes, planes)] = f[:, 0:TILE, :]


def pack_corners(fields, xla, xha, *rest):
    earlier, (c_up, c_down) = rest[:-2], rest[-2:]
    first, _ = x_layout(fields)
    where, _ = corner_layout(fields)

    def tile(side, k, d):
        if (k, d, "A") in first:
            return (xla, xha)[side][first[k, d, "A"]]
        f, i = earlier[side], (earlier[0].shape[0] - d, 4 + d - 1)[side]
        return jnp.where(upper(), f[i, 0:TILE, :], f[i, TILE:, :])

    for (k, d), at in where.items():
        rows = beyond(fields[k][0], d)
        if rows > TILE // 2:
            for side, x in ((0, xla), (1, xha)):
                a, b = tile(side, k, d), x[first[k, d, "B"]]
                c_up[at + side] = jnp.where(upper(), b, a)
                c_down[at + side] = jnp.where(upper(), a, b)
        elif rows > TILE // 4 or d % 2:
            more = (d,) if rows > TILE // 4 else (d, d + 1)
            tiles = [tile(side, k, e) for side in (0, 1) for e in more]
            c_up[at] = share(tiles, True)
            c_down[at] = share(tiles, False)


def widen(out, width, centre, y_tile, x_tiles, corner):
    planes, _, depth = centre.shape
    for i in range(planes):
        out[width + i, 0:TILE, :] = y_tile(0, i)
        out[width + i, OWN, :] = centre[i]
        out[width + i, 3 * TILE :, :] = y_tile(1, i)
    for d in range(1, width + 1):
        for side, to in ((0, width - d), (1, width + planes - 1 + d)):
            low, high = x_tiles(side, d)
            out[to, TILE : 2 * TILE, :] = low
            out[to, 2 * TILE : 3 * TILE, :] = high
            if beyond(width, d) > 0:
                out[to, 0:TILE, :] = corner(side, 0, d)
                out[to, 3 * TILE :, :] = corner(side, 1, d)
            else:
                out[to, 0:TILE, :] = jnp.zeros((TILE, depth), jnp.float32)
                out[to, 3 * TILE :, :] = jnp.zeros((TILE, depth), jnp.float32)


def corner_of(k, fields, c):
    where, _ = corner_layout(fields)
    width = fields[k][0]

    def corner(side, y_side, d):
        tile, rows = where[k, d], beyond(width, d)
        if rows > TILE // 2:
            return c[y_side][tile + side]
        if rows > TILE // 4:
            return unshare(c[y_side][tile], 2, side, y_side == 0)
        return unshare(c[y_side][tile], 4, 2 * side + (d - 1) % 2, y_side == 0)

    return corner


def tiles_of(k, fields, xa, xb):
    first, rest = x_layout(fields)

    def tile(side, key):
        return xa[side][first[key]] if key in first else xb[side][rest[key]]

    def x_tiles(side, d):
        a, b = tile(side, (k, d, "A")), tile(side, (k, d, "B"))
        return jnp.where(upper(), a, b), jnp.where(upper(), b, a)

    return x_tiles


def widen_moved(outs, blocks, fields, halos):
    xa, y, xb, c = (halos[i : i + 2] for i in range(0, 8, 2))
    planes = blocks[0].shape[0]
    for k, (out, f) in enumerate(zip(outs, blocks)):
        widen(
            out,
            fields[k][0],
            f,
            lambda side, i: y[side][k * planes + i],
            tiles_of(k, fields, xa, xb),
            corner_of(k, fields, c),
        )


def load_first(h, u, v, s, u_own, v_own, s_own, *rest):
    x_up, x_down, y_up, y_down, sems = rest
    planes, half, _ = u_own.shape
    own = pl.ds(pl.multiple_of(h[0] * half, TILE), half)
    fields = (u_own, v_own, s_own)
    copies = [
        pltpu.make_async_copy(f.at[:, own, :], to, sems.at[k])
        for k, (f, to) in enumerate(zip((u, v, s), fields))
    ]
    for copy in copies:
        copy.start()
    for copy in copies:
        copy.wait()
    for k, f in enumerate(fields):
        x_up[pl.ds(2 * k, 2)] = f[planes - 2 :]
        x_down[pl.ds(2 * k, 2)] = f[0:2]
    pairs = planes // 2
    for i in range(pairs):
        shared = (u_own, i), (v_own, i), (u_own, i + pairs), (v_own, i + pairs)
        y_up[i] = share([f[plane, TILE:, :] for f, plane in shared], True)
        y_down[i] = share([f[plane, 0:TILE, :] for f, plane in shared], False)
    y_up[pairs:] = s_own[:, TILE:, :]
    y_down[pairs:] = s_own[:, 0:TILE, :]


def first_step(u, v, s, yl, yh, xl, xh, u_out, v_out, q_out, *rest):
    sends, (u0, v0) = rest[:6], rest[6:]
    planes, _, _ = u.shape
    pairs = planes // 2
    for k, (f, out) in enumerate(((u, u0), (v, v0))):
        out[pl.ds(2, planes), OWN, :] = f[...]
        out[0:2, OWN, :] = xl[pl.ds(2 * k, 2)]
        out[planes + 2 :, OWN, :] = xh[pl.ds(2 * k, 2)]
        for i in range(planes):
            n = k + 2 * (i // pairs)
            below = unshare(yl[i % pairs], 4, n, True)
            above = unshare(yh[i % pairs], 4, n, False)
            out[2 + i, 0:TILE, :] = below
            out[2 + i, 3 * TILE :, :] = above
    for i in range(planes):
        q, l = lap(u0, i + 2, OWN), lap(v0, i + 2, OWN)
        u_out[i] = u[i] + time_step * v[i]
        v_out[i] = v[i] + time_step * (s[i] * q + damping * l)
        q_out[i] = q + time_step * l
    pack_edges((v_out, q_out, s), SECOND, sends)


def advance(planes, width, v, q, s, v_out, q_out):
    count = planes + 2 * width - 4
    for i in range(count):
        edge = i < 2 or i >= count - 2
        rows = OWN if edge else ALL
        l = lap(v, i + 2, rows)
        now = s[i + MID + 2 - width, rows, :] * q[i, rows, :] + damping * l
        v_out[i, rows, :] = v[i + 2, rows, :] + time_step * now
        if not edge:
            q_out[i - 2] = q[i] + time_step * l


def middle_steps(u, v, q, s, *rest):
    halos, (ysl, ysh, xsl, xsh), rest = rest[:8], rest[8:12], rest[12:]
    (u_out, v_out, q_out, s_wide), sends = rest[:4], rest[4:10]
    v0, q0, v1, q1, v2, q2, v3, q3 = rest[10:]
    planes, _, _ = v.shape
    moved = tiles_of(2, SECOND, halos[0:2], halos[4:6])

    def s_rows(side, d):
        if d >= SECOND[2][1]:
            return moved(side, d)
        f, i = ((xsl, xsl.shape[0] - d), (xsh, 4 + d - 1))[side]
        return f[i, 0:TILE, :], f[i, TILE:, :]

    widen_moved((v0, q0), (v, q), SECOND, halos)
    widen(
        s_wide,
        MID,
        s,
        lambda side, i: (ysl, ysh)[side][planes // 2 + i],
        s_rows,
        corner_of(2, SECOND, halos[6:8]),
    )
    advance(planes, WIDE, v0, q0, s_wide, v1, q1)
    advance(planes, WIDE - 2, v1, q1, s_wide, v2, q2)
    advance(planes, WIDE - 4, v2, q2, s_wide, v3, q3)
    for i in range(planes):
        l = lap(v3, i + 2, OWN)
        now = s[i] * q3[i, OWN, :] + damping * l
        v_out[i] = v3[i + 2, OWN, :] + time_step * now
        q_out[i] = q3[i, OWN, :] + time_step * l
        moved = v[i] + v1[i + 6, OWN, :] + v2[i + 4, OWN, :] + v3[i + 2, OWN, :]
        u_out[i] = u[i] + time_step * moved
    pack_edges((v_out, q_out), LAST, sends)


def last_steps(scale, u, v, q, s_wide, *rest):
    halos, (keep, send) = rest[:8], rest[8:10]
    v0, q0, v1, q1, v2, q2, rate, l7 = rest[10:]
    planes, _, _ = v.shape
    widen_moved((v0, q0), (v, q), LAST, halos)
    advance(planes, WIDE, v0, q0, s_wide, v1, q1)
    advance(planes, WIDE - 2, v1, q1, s_wide, v2, q2)
    count = planes + 4
    for i in range(count):
        edge = i < 2 or i >= count - 2
        rows = OWN if edge else ALL
        l = lap(v2, i + 2, rows)
        rate[i, rows, :] = s_wide[i + MID - 2, rows, :] * q2[i, rows, :] + damping * l
        if not edge:
            l7[i - 2] = l[OWN]
    for i in range(planes):
        l = lap(rate, i + 2, OWN)
        r = rate[i + 2, OWN, :]
        v7 = v2[i + 4, OWN, :]
        u8 = u[i] + time_step * (v[i] + v1[i + 6, OWN, :] + v7)
        v8 = v7 + time_step * r
        more = s_wide[i + MID, OWN, :] * l7[i] + damping * l
        keep[i] = u8 + scale[0] * r
        keep[planes + i] = v8 + scale[0] * more
        send[i] = u8 + scale[1] * r
        send[planes + i] = v8 + scale[1] * more


def join(h, keep, got, out_u, out_v):
    planes, rows, _ = out_u.shape
    half = rows // 2
    own = pl.ds(pl.multiple_of(h[0] * half, TILE), half)
    other = pl.ds(pl.multiple_of((1 - h[0]) * half, TILE), half)
    for k, out in enumerate((out_u, out_v)):
        part = pl.ds(k * planes, planes)
        out[:, own, :] = keep[part]
        out[:, other, :] = got[part]


def ring(count, step):
    return [(i, (i + step) % count) for i in range(count)]


def strips(gy, step):
    def place(t):
        j, h = divmod(t % (2 * gy), 2)
        return ((h + j) % 2) * gy + j

    return [(place(t), place(t + step)) for t in range(2 * gy)]


STARTS = ("a_up", "a_down", "y_up", "y_down", "b_up", "b_down", "c_up", "c_down")


def move(name, sent):
    step = 1 if name.endswith("up") else -1
    if name.startswith(("y", "c")):
        return lax.ppermute(sent, ("level", "gy"), strips(lax.axis_size("gy"), step))
    return lax.ppermute(sent, "gx", ring(lax.axis_size("gx"), step))


def exchange(fields, sends, earlier):
    got = [move(name, sent) for name, sent in zip(STARTS, sends)]
    if fields:
        c = spec(corner_layout(fields)[1], TILE, sends[0].shape[-1])
        kernel = functools.partial(pack_corners, fields)
        corners = call(kernel, [c, c], (got[0], got[1], *earlier))
        got += [move(name, sent) for name, sent in zip(STARTS[6:], corners)]
    return got


def edge_specs(planes, depth, fields):
    first, rest = x_layout(fields)
    return [spec(n, TILE, depth) for n in (len(first), 2 * planes, len(rest)) for _ in range(2)]


def body(u, v, s):
    planes, rows, depth = u.shape
    half = rows // 2
    assert lax.axis_size("level") == 2 and planes >= WIDE and half == 2 * TILE
    level = lax.axis_index("level")
    h = ((level + lax.axis_index("gy")) % 2).astype(jnp.int32).reshape(1)
    mine = jnp.where(level == 0, 0.0, second).astype(jnp.float32)
    scale = jnp.stack([mine, second - mine])

    tall = half + 2 * TILE
    block = spec(planes, half, depth)
    wide, mid, thin, slim, bare = ((planes + 2 * w, tall, depth) for w in (WIDE, MID, 4, 2, 0))
    work = 100 * u.size

    x, y = spec(6, half, depth), spec(planes * 3 // 2, TILE, depth)
    outs = [block] * 3 + [x, x, y, y]
    u, v, s, *sends = pl.pallas_call(
        load_first,
        out_shape=outs,
        in_specs=[SMEM] + [pl.BlockSpec(memory_space=pltpu.HBM)] * 3,
        out_specs=[VMEM] * len(outs),
        scratch_shapes=[pltpu.SemaphoreType.DMA((3,))],
        compiler_params=pltpu.CompilerParams(vmem_limit_bytes=14 << 20),
    )(h, *(pltpu.with_memory_space_constraint(f, pltpu.HBM) for f in (u, v, s)))
    xl, xh, yl, yh = exchange((), sends, ())
    sent = edge_specs(planes, depth, SECOND)
    args = (u, v, s, yl, yh, xl, xh)
    u, v, q, *sends = call(first_step, [block] * 3 + sent, args, (), (slim, slim), work)
    halos = exchange(SECOND, sends, (xl, xh))
    sent = edge_specs(planes, depth, LAST)
    u, v, q, s_wide, *sends = call(
        middle_steps,
        [block] * 3 + [spec(*mid)] + sent,
        (u, v, q, s, *halos, yl, yh, xl, xh),
        (),
        (wide, mid, mid, thin, thin, slim, slim, bare),
        work,
    )
    halos = exchange(LAST, sends, ())
    both = spec(2 * planes, half, depth)
    keep, send = call(
        last_steps,
        [both, both],
        (u, v, q, s_wide, *halos),
        (scale,),
        (wide, mid, mid, thin, thin, slim, slim, (planes, half, depth)),
        work,
    )
    got = lax.ppermute(send, "level", ring(2, 1))
    out_u, out_v = call(join, [spec(planes, rows, depth)] * 2, (keep, got), (h,))
    return out_u[None], out_v[None]


def solution(mesh):
    placed = (P("gx", "gy", None),) * 3
    return jax.shard_map(
        body,
        mesh=mesh,
        in_specs=placed,
        out_specs=(P("level", "gx", "gy", None), P("level", "gx", "gy", None)),
        check_vma=False,
    )
```

time: 60.8 us -> 63.9 us (1.051)
  waiting for transfers between devices: 24.8 us -> 28.1 us
    ppermute x12 -> x10, waiting for transfers between devices: 11.8 us -> 16.6 us  [move(): return lax.ppermute(sent, 'gx', ring(lax.axis_size('gx'), step))]
    ppermute x10, waiting for transfers between devices: 5.46 us -> 3.99 us  [move(): lax.ppermute(sent, ('level', 'gy'), strips(lax.axis_size('gy'), step))]
    ppermute x12 -> x10, starting transfers between devices: 18 us -> 17.2 us  [move(): return lax.ppermute(sent, 'gx', ring(lax.axis_size('gx'), step))]
    pallas_call x8 -> x6, Pallas kernels: 5.55 us -> 5.53 us  [call(): pl.pallas_call(kernel, out_shape=outs, in_specs=[SMEM] * len(scalars) + [...]
  transfers between devices with their start and end apart: 23 -> 21, of which waited for: 12 -> 10; matrix products, arithmetic and copies ran while one was open for 0% -> 0% of each run, Pallas kernels for 1% -> 0%
where the time goes in v6:
time: 63.9 us; the launch traced here: 63.8 us
  starting transfers between devices  28.3 us (44%)
  waiting for transfers between devices  28.1 us (44%)
  Pallas kernels  6.62 us (10%)
  between operations  0.73 us (1%)
    ppermute x10, starting transfers between devices, move(): return lax.ppermute(sent, 'gx', ring(lax.axis_size('gx'), step))  17.2 us
    ppermute x10, waiting for transfers between devices, move(): return lax.ppermute(sent, 'gx', ring(lax.axis_size('gx'), step))  16.6 us
    ppermute x10, starting transfers between devices, move(): lax.ppermute(sent, ('level', 'gy'), strips(lax.axis_size('gy'), step))  10.1 us
    ppermute x1, waiting for transfers between devices, body(): got = lax.ppermute(send, 'level', ring(2, 1))  7.48 us
    pallas_call x6, Pallas kernels, call(): pl.pallas_call(kernel, out_shape=outs, in_specs=[SMEM] * len(scalars) + [...  5.53 us
    ppermute x10, waiting for transfers between devices, move(): lax.ppermute(sent, ('level', 'gy'), strips(lax.axis_size('gy'), step))  3.99 us
  transfers between devices with their start and end apart: 21, of which 10 were waited for; matrix products, arithmetic and copies ran while one was open for 0% of the time, Pallas kernels for 0%

profile of v6, /device:TPU:0, one launch (start us, length us, event | category | flops | bytes accessed | tf_op | source)
XLA Modules:
  0.0 63.8 jit_solution(5776505779585459080)
XLA Ops:
  0.6 1.1 %shard_map.50 = (f32[8,16,256]{2,1,0:T(8,128)S(1)}, f32[8,16,256]{2,1,0:T(8,128)S(1)}, f32[8,16,256]{2,1,0:T(8,128)S(1)}, f32[6,16,256]{2,1,0:T(8,128)S(1)}, f32...) custom-call(s32[1]{0:T(128)} %bitcast.h, f32[8,32,256]{2,1,0:T(8,128)} %u.1, ...), custom_call_target="tpu_custom_call" | custom-call | tf_op jit(solution)/shard_map/pallas_call | solution.py:409
  1.7 3.0 %collective-permute-start = (f32[12,8,256]{2,1,0:T(8,128)S(1)}, f32[12,8,256]{2,1,0:T(8,128)S(1)}, u32[]{:S(2)}, u32[]{:S(2)}) collective-permute-start(f32[12,8,256]{2,1,0:T(8,128)S(1)} %get-tuple-element.39), channel_id=1, source_target_pairs={{0,16},{16,17},{17,1},{1,2},{2,18},{18,19},{19,3},{3,0},{4,20},{20... | collective-permute-start | bytes 294920 | tf_op jit(solution)/shard_map/ppermute | solution.py:374
  4.8 0.0 collective-permute-start.1
  4.8 1.8 %collective-permute-start.2 = (f32[6,16,256]{2,1,0:T(8,128)S(1)}, f32[6,16,256]{2,1,0:T(8,128)S(1)}, u32[]{:S(2)}, u32[]{:S(2)}) collective-permute-start(f32[6,16,256]{2,1,0:T(8,128)S(1)} %get-tuple-element.41), channel_id=1, source_target_pairs={{0,4},{4,8},{8,12},{12,0},{1,5},{5,9},{9,13},{13,1},{2,6},{6,10},{... | collective-permute-start | bytes 294920 | tf_op jit(solution)/shard_map/ppermute | solution.py:375
  6.6 2.0 %collective-permute-start.3 = (f32[6,16,256]{2,1,0:T(8,128)S(1)}, f32[6,16,256]{2,1,0:T(8,128)S(1)}, u32[]{:S(2)}, u32[]{:S(2)}) collective-permute-start(f32[6,16,256]{2,1,0:T(8,128)S(1)} %get-tuple-element.42), channel_id=1, source_target_pairs={{0,12},{4,0},{8,4},{12,8},{1,13},{5,1},{9,5},{13,9},{2,14},{6,2},{... | collective-permute-start | bytes 294920 | tf_op jit(solution)/shard_map/ppermute | solution.py:375
  8.6 0.0 collective-permute-done.yl.rest_8_
  8.6 0.8 %collective-permute-done.1.yh.rest_9_ = f32[12,8,256]{2,1,0:T(8,128)S(1)} collective-permute-done((f32[12,8,256]{2,1,0:T(8,128)S(1)}, f32[12,8,256]{2,1,0:T(8,128)S(1)}, u32[]{:S(2)}, u32[]{:S(2)}) %collective-permute-start.1) | collective-permute-done | bytes 98336 | tf_op jit(solution)/shard_map/ppermute | solution.py:374
  9.4 2.7 %collective-permute-done.2.xl.rest_0_.rest_10_ = f32[6,16,256]{2,1,0:T(8,128)S(1)} collective-permute-done((f32[6,16,256]{2,1,0:T(8,128)S(1)}, f32[6,16,256]{2,1,0:T(8,128)S(1)}, u32[]{:S(2)}, u32[]{:S(2)}) %collective-permute-start.2) | collective-permute-done | bytes 98336 | tf_op jit(solution)/shard_map/ppermute | solution.py:375
  12.1 0.9 %collective-permute-done.3.xh.rest_1_.rest_11_ = f32[6,16,256]{2,1,0:T(8,128)S(1)} collective-permute-done((f32[6,16,256]{2,1,0:T(8,128)S(1)}, f32[6,16,256]{2,1,0:T(8,128)S(1)}, u32[]{:S(2)}, u32[]{:S(2)}) %collective-permute-start.3) | collective-permute-done | bytes 98336 | tf_op jit(solution)/shard_map/ppermute | solution.py:375
  13.0 0.4 shard_map.51
  13.4 1.2 %collective-permute-start.4 = (f32[24,8,256]{2,1,0:T(8,128)S(1)}, f32[24,8,256]{2,1,0:T(8,128)S(1)}, u32[]{:S(2)}, u32[]{:S(2)}) collective-permute-start(f32[24,8,256]{2,1,0:T(8,128)S(1)} %get-tuple-element.46), channel_id=1, source_target_pairs={{0,4},{4,8},{8,12},{12,0},{1,5},{5,9},{9,13},{13,1},{2,6},{6,10},{... | collective-permute-start | bytes 589832 | tf_op jit(solution)/shard_map/ppermute | solution.py:375
  14.6 2.7 %collective-permute-start.5 = (f32[24,8,256]{2,1,0:T(8,128)S(1)}, f32[24,8,256]{2,1,0:T(8,128)S(1)}, u32[]{:S(2)}, u32[]{:S(2)}) collective-permute-start(f32[24,8,256]{2,1,0:T(8,128)S(1)} %get-tuple-element.47), channel_id=1, source_target_pairs={{0,12},{4,0},{8,4},{12,8},{1,13},{5,1},{9,5},{13,9},{2,14},{6,2},{... | collective-permute-start | bytes 589832 | tf_op jit(solution)/shard_map/ppermute | solution.py:375
  17.3 0.0 collective-permute-start.8
  17.3 1.0 %collective-permute-start.6 = (f32[16,8,256]{2,1,0:T(8,128)S(1)}, f32[16,8,256]{2,1,0:T(8,128)S(1)}, u32[]{:S(2)}, u32[]{:S(2)}) collective-permute-start(f32[16,8,256]{2,1,0:T(8,128)S(1)} %get-tuple-element.48), channel_id=1, source_target_pairs={{0,16},{16,17},{17,1},{1,2},{2,18},{18,19},{19,3},{3,0},{4,20},{20... | collective-permute-start | bytes 393224 | tf_op jit(solution)/shard_map/ppermute | solution.py:374
  18.3 0.7 %collective-permute-start.7 = (f32[16,8,256]{2,1,0:T(8,128)S(1)}, f32[16,8,256]{2,1,0:T(8,128)S(1)}, u32[]{:S(2)}, u32[]{:S(2)}) collective-permute-start(f32[16,8,256]{2,1,0:T(8,128)S(1)} %get-tuple-element.49), channel_id=1, source_target_pairs={{0,3},{16,0},{17,16},{1,17},{2,1},{18,2},{19,18},{3,19},{4,7},{20,... | collective-permute-start | bytes 393224 | tf_op jit(solution)/shard_map/ppermute | solution.py:374
  19.0 4.0 %collective-permute-done.4.xla.rest_0_ = f32[24,8,256]{2,1,0:T(8,128)S(1)} collective-permute-done((f32[24,8,256]{2,1,0:T(8,128)S(1)}, f32[24,8,256]{2,1,0:T(8,128)S(1)}, u32[]{:S(2)}, u32[]{:S(2)}) %collective-permute-start.4) | collective-permute-done | bytes 196640 | tf_op jit(solution)/shard_map/ppermute | solution.py:375
  23.0 3.2 %collective-permute-done.5.xha.rest_1_ = f32[24,8,256]{2,1,0:T(8,128)S(1)} collective-permute-done((f32[24,8,256]{2,1,0:T(8,128)S(1)}, f32[24,8,256]{2,1,0:T(8,128)S(1)}, u32[]{:S(2)}, u32[]{:S(2)}) %collective-permute-start.5) | collective-permute-done | bytes 196640 | tf_op jit(solution)/shard_map/ppermute | solution.py:375
  26.3 0.1 collective-permute-start.10
  26.3 1.7 %collective-permute-start.11 = (f32[13,8,256]{2,1,0:T(8,128)S(1)}, f32[13,8,256]{2,1,0:T(8,128)S(1)}, u32[]{:S(2)}, u32[]{:S(2)}) collective-permute-start(f32[13,8,256]{2,1,0:T(8,128)S(1)} %get-tuple-element.53), channel_id=1, source_target_pairs={{0,3},{16,0},{17,16},{1,17},{2,1},{18,2},{19,18},{3,19},{4,7},{20,... | collective-permute-start | bytes 319496 | tf_op jit(solution)/shard_map/ppermute | solution.py:374
  28.1 0.0 collective-permute-done.8.rest_4_
  28.1 2.2 %collective-permute-start.9 = (f32[12,8,256]{2,1,0:T(8,128)S(1)}, f32[12,8,256]{2,1,0:T(8,128)S(1)}, u32[]{:S(2)}, u32[]{:S(2)}) collective-permute-start(f32[12,8,256]{2,1,0:T(8,128)S(1)} %get-tuple-element.51), channel_id=1, source_target_pairs={{0,12},{4,0},{8,4},{12,8},{1,13},{5,1},{9,5},{13,9},{2,14},{6,2},{... | collective-permute-start | bytes 294920 | tf_op jit(solution)/shard_map/ppermute | solution.py:375
  30.3 2.4 %collective-permute-done.9.rest_5_ = f32[12,8,256]{2,1,0:T(8,128)S(1)} collective-permute-done((f32[12,8,256]{2,1,0:T(8,128)S(1)}, f32[12,8,256]{2,1,0:T(8,128)S(1)}, u32[]{:S(2)}, u32[]{:S(2)}) %collective-permute-start.9) | collective-permute-done | bytes 98336 | tf_op jit(solution)/shard_map/ppermute | solution.py:375
  32.7 0.0 collective-permute-done.6.rest_2_
  32.7 0.0 collective-permute-done.7.rest_3_
  32.7 0.0 collective-permute-done.10.rest_6_
  32.7 0.0 collective-permute-done.11.rest_7_
  32.7 1.9 %shard_map.53 = (f32[8,16,256]{2,1,0:T(8,128)S(1)}, f32[8,16,256]{2,1,0:T(8,128)S(1)}, f32[8,16,256]{2,1,0:T(8,128)S(1)}, f32[20,32,256]{2,1,0:T(8,128)S(1)}, f3...) custom-call(f32[8,16,256]{2,1,0:T(8,128)S(1)} %get-tuple-element.43., ...), custom_call_target="tpu_custom_call" | custom-call | flops 6553600 | bytes 3751936 | tf_op jit(solution)/shard_map/pallas_call | solution.py:39
  34.6 0.2 collective-permute-start.12
  34.8 3.9 %collective-permute-start.13 = (f32[20,8,256]{2,1,0:T(8,128)S(1)}, f32[20,8,256]{2,1,0:T(8,128)S(1)}, u32[]{:S(2)}, u32[]{:S(2)}) collective-permute-start(f32[20,8,256]{2,1,0:T(8,128)S(1)} %get-tuple-element.59), channel_id=1, source_target_pairs={{0,12},{4,0},{8,4},{12,8},{1,13},{5,1},{9,5},{13,9},{2,14},{6,2},{... | collective-permute-start | bytes 491528 | tf_op jit(solution)/shard_map/ppermute | solution.py:375
  38.7 0.0 collective-permute-start.16
  38.7 0.4 collective-permute-start.14
  39.1 1.4 %collective-permute-start.15 = (f32[16,8,256]{2,1,0:T(8,128)S(1)}, f32[16,8,256]{2,1,0:T(8,128)S(1)}, u32[]{:S(2)}, u32[]{:S(2)}) collective-permute-start(f32[16,8,256]{2,1,0:T(8,128)S(1)} %get-tuple-element.61), channel_id=1, source_target_pairs={{0,3},{16,0},{17,16},{1,17},{2,1},{18,2},{19,18},{3,19},{4,7},{20,... | collective-permute-start | bytes 393224 | tf_op jit(solution)/shard_map/ppermute | solution.py:374
  40.5 3.3 %collective-permute-done.12.xla.rest_0_ = f32[20,8,256]{2,1,0:T(8,128)S(1)} collective-permute-done((f32[20,8,256]{2,1,0:T(8,128)S(1)}, f32[20,8,256]{2,1,0:T(8,128)S(1)}, u32[]{:S(2)}, u32[]{:S(2)}) %collective-permute-start.12) | collective-permute-done | bytes 163872 | tf_op jit(solution)/shard_map/ppermute | solution.py:375
  43.8 3.2 %collective-permute-start.17 = (f32[8,8,256]{2,1,0:T(8,128)S(1)}, f32[8,8,256]{2,1,0:T(8,128)S(1)}, u32[]{:S(2)}, u32[]{:S(2)}) collective-permute-start(f32[8,8,256]{2,1,0:T(8,128)S(1)} %get-tuple-element.63), channel_id=1, source_target_pairs={{0,12},{4,0},{8,4},{12,8},{1,13},{5,1},{9,5},{13,9},{2,14},{6,2},{... | collective-permute-start | bytes 196616 | tf_op jit(solution)/shard_map/ppermute | solution.py:375
  47.0 0.0 collective-permute-done.13.xha.rest_1_
  47.0 0.7 %collective-permute-start.18 = (f32[10,8,256]{2,1,0:T(8,128)S(1)}, f32[10,8,256]{2,1,0:T(8,128)S(1)}, u32[]{:S(2)}, u32[]{:S(2)}) collective-permute-start(f32[10,8,256]{2,1,0:T(8,128)S(1)} %get-tuple-element.64), channel_id=1, source_target_pairs={{0,16},{16,17},{17,1},{1,2},{2,18},{18,19},{19,3},{3,0},{4,20},{20... | collective-permute-start | bytes 245768 | tf_op jit(solution)/shard_map/ppermute | solution.py:374
  47.7 0.0 collective-permute-done.16.rest_4_
  47.7 1.1 %collective-permute-start.19 = (f32[10,8,256]{2,1,0:T(8,128)S(1)}, f32[10,8,256]{2,1,0:T(8,128)S(1)}, u32[]{:S(2)}, u32[]{:S(2)}) collective-permute-start(f32[10,8,256]{2,1,0:T(8,128)S(1)} %get-tuple-element.65), channel_id=1, source_target_pairs={{0,3},{16,0},{17,16},{1,17},{2,1},{18,2},{19,18},{3,19},{4,7},{20,... | collective-permute-start | bytes 245768 | tf_op jit(solution)/shard_map/ppermute | solution.py:374
  48.9 0.1 pad_maximum_fusion.scale
  48.9 0.0 collective-permute-done.17.rest_5_
  48.9 0.0 collective-permute-done.14.rest_2_
  48.9 0.0 collective-permute-done.15.rest_3_
  48.9 2.0 %collective-permute-done.18.rest_6_ = f32[10,8,256]{2,1,0:T(8,128)S(1)} collective-permute-done((f32[10,8,256]{2,1,0:T(8,128)S(1)}, f32[10,8,256]{2,1,0:T(8,128)S(1)}, u32[]{:S(2)}, u32[]{:S(2)}) %collective-permute-start.18) | collective-permute-done | bytes 81952 | tf_op jit(solution)/shard_map/ppermute | solution.py:374
  51.0 1.2 %collective-permute-done.19.rest_7_ = f32[10,8,256]{2,1,0:T(8,128)S(1)} collective-permute-done((f32[10,8,256]{2,1,0:T(8,128)S(1)}, f32[10,8,256]{2,1,0:T(8,128)S(1)}, u32[]{:S(2)}, u32[]{:S(2)}) %collective-permute-start.19) | collective-permute-done | bytes 81952 | tf_op jit(solution)/shard_map/ppermute | solution.py:374
  52.2 2.4 %shard_map.55 = (f32[16,16,256]{2,1,0:T(8,128)S(1)}, f32[16,16,256]{2,1,0:T(8,128)S(1)}) custom-call(f32[2]{0:T(128)S(1)} %pad_maximum_fusion.scale, f32[8,16,256]{2,1,0:T(8,128)S(1)} %get-tuple-element.54.u, f32[8,16,256]{2,1,0:T(8,128)S(1)} %get-tuple-element.55.v, f32[8,16,256]{2,1,0:T(8,128)S(1)} %get-tuple-element.56.q, ...), custom_call_target="tpu_custom_call" | custom-call | flops 6553600 | bytes 2457600 | tf_op jit(solution)/shard_map/pallas_call | solution.py:39
  54.6 0.9 %collective-permute-start.20 = (f32[16,16,256]{2,1,0:T(8,128)S(1)}, f32[16,16,256]{2,1,0:T(8,128)S(1)}, u32[]{:S(2)}, u32[]{:S(2)}) collective-permute-start(f32[16,16,256]{2,1,0:T(8,128)S(1)} %get-tuple-element.67), channel_id=1, source_target_pairs={{0,16},{16,0},{1,17},{17,1},{2,18},{18,2},{3,19},{19,3},{4,20},{20... | collective-permute-start | bytes 786440 | tf_op jit(solution)/shard_map/ppermute | solution.py:441
  55.5 7.5 %collective-permute-done.20.got = f32[16,16,256]{2,1,0:T(8,128)S(1)} collective-permute-done((f32[16,16,256]{2,1,0:T(8,128)S(1)}, f32[16,16,256]{2,1,0:T(8,128)S(1)}, u32[]{:S(2)}, u32[]{:S(2)}) %collective-permute-start.20) | collective-permute-done | bytes 262176 | tf_op jit(solution)/shard_map/ppermute | solution.py:441
  63.0 0.8 %shard_map.56 = (f32[8,32,256]{2,1,0:T(8,128)}, f32[8,32,256]{2,1,0:T(8,128)}) custom-call(s32[1]{0:T(128)} %bitcast.h, f32[16,16,256]{2,1,0:T(8,128)S(1)} %get-tuple-element.66.keep, f32[16,16,256]{2,1,0:T(8,128)S(1)} %collective-permute-done.20.got), custom_call_target="tpu_custom_call" | custom-call | bytes 1048576 | tf_op jit(solution)/shard_map/pallas_call | solution.py:39
  (2 shorter events, 0.0 us)
Async XLA Ops:
  1.7 6.9 %collective-permute-start = (f32[12,8,256]{2,1,0:T(8,128)S(1)}, f32[12,8,256]{2,1,0:T(8,128)S(1)}, u32[]{:S(2)}, u32[]{:S(2)}) collective-permute-start(f32[12,8,256]{2,1,0:T(8,128)S(1)} %get-tuple-element.39), channel_id=1, source_target_pairs={{0,16},{16,17},{17,1},{1,2},{2,18},{18,19},{19,3},{3,0},{4,20},{20... | collective-permute-start | bytes 294920 | tf_op jit(solution)/shard_map/ppermute | solution.py:374
  4.8 4.6 %collective-permute-start.1 = (f32[12,8,256]{2,1,0:T(8,128)S(1)}, f32[12,8,256]{2,1,0:T(8,128)S(1)}, u32[]{:S(2)}, u32[]{:S(2)}) collective-permute-start(f32[12,8,256]{2,1,0:T(8,128)S(1)} %get-tuple-element.40), channel_id=1, source_target_pairs={{0,3},{16,0},{17,16},{1,17},{2,1},{18,2},{19,18},{3,19},{4,7},{20,... | collective-permute-start | bytes 294920 | tf_op jit(solution)/shard_map/ppermute | solution.py:374
  4.8 7.3 %collective-permute-start.2 = (f32[6,16,256]{2,1,0:T(8,128)S(1)}, f32[6,16,256]{2,1,0:T(8,128)S(1)}, u32[]{:S(2)}, u32[]{:S(2)}) collective-permute-start(f32[6,16,256]{2,1,0:T(8,128)S(1)} %get-tuple-element.41), channel_id=1, source_target_pairs={{0,4},{4,8},{8,12},{12,0},{1,5},{5,9},{9,13},{13,1},{2,6},{6,10},{... | collective-permute-start | bytes 294920 | tf_op jit(solution)/shard_map/ppermute | solution.py:375
  6.6 6.4 %collective-permute-start.3 = (f32[6,16,256]{2,1,0:T(8,128)S(1)}, f32[6,16,256]{2,1,0:T(8,128)S(1)}, u32[]{:S(2)}, u32[]{:S(2)}) collective-permute-start(f32[6,16,256]{2,1,0:T(8,128)S(1)} %get-tuple-element.42), channel_id=1, source_target_pairs={{0,12},{4,0},{8,4},{12,8},{1,13},{5,1},{9,5},{13,9},{2,14},{6,2},{... | collective-permute-start | bytes 294920 | tf_op jit(solution)/shard_map/ppermute | solution.py:375
  13.4 9.6 %collective-permute-start.4 = (f32[24,8,256]{2,1,0:T(8,128)S(1)}, f32[24,8,256]{2,1,0:T(8,128)S(1)}, u32[]{:S(2)}, u32[]{:S(2)}) collective-permute-start(f32[24,8,256]{2,1,0:T(8,128)S(1)} %get-tuple-element.46), channel_id=1, source_target_pairs={{0,4},{4,8},{8,12},{12,0},{1,5},{5,9},{9,13},{13,1},{2,6},{6,10},{... | collective-permute-start | bytes 589832 | tf_op jit(solution)/shard_map/ppermute | solution.py:375
  14.6 11.6 %collective-permute-start.5 = (f32[24,8,256]{2,1,0:T(8,128)S(1)}, f32[24,8,256]{2,1,0:T(8,128)S(1)}, u32[]{:S(2)}, u32[]{:S(2)}) collective-permute-start(f32[24,8,256]{2,1,0:T(8,128)S(1)} %get-tuple-element.47), channel_id=1, source_target_pairs={{0,12},{4,0},{8,4},{12,8},{1,13},{5,1},{9,5},{13,9},{2,14},{6,2},{... | collective-permute-start | bytes 589832 | tf_op jit(solution)/shard_map/ppermute | solution.py:375
  17.3 10.8 %collective-permute-start.8 = (f32[12,8,256]{2,1,0:T(8,128)S(1)}, f32[12,8,256]{2,1,0:T(8,128)S(1)}, u32[]{:S(2)}, u32[]{:S(2)}) collective-permute-start(f32[12,8,256]{2,1,0:T(8,128)S(1)} %get-tuple-element.50), channel_id=1, source_target_pairs={{0,4},{4,8},{8,12},{12,0},{1,5},{5,9},{9,13},{13,1},{2,6},{6,10},{... | collective-permute-start | bytes 294920 | tf_op jit(solution)/shard_map/ppermute | solution.py:375
  17.3 15.4 %collective-permute-start.6 = (f32[16,8,256]{2,1,0:T(8,128)S(1)}, f32[16,8,256]{2,1,0:T(8,128)S(1)}, u32[]{:S(2)}, u32[]{:S(2)}) collective-permute-start(f32[16,8,256]{2,1,0:T(8,128)S(1)} %get-tuple-element.48), channel_id=1, source_target_pairs={{0,16},{16,17},{17,1},{1,2},{2,18},{18,19},{19,3},{3,0},{4,20},{20... | collective-permute-start | bytes 393224 | tf_op jit(solution)/shard_map/ppermute | solution.py:374
  18.3 14.4 %collective-permute-start.7 = (f32[16,8,256]{2,1,0:T(8,128)S(1)}, f32[16,8,256]{2,1,0:T(8,128)S(1)}, u32[]{:S(2)}, u32[]{:S(2)}) collective-permute-start(f32[16,8,256]{2,1,0:T(8,128)S(1)} %get-tuple-element.49), channel_id=1, source_target_pairs={{0,3},{16,0},{17,16},{1,17},{2,1},{18,2},{19,18},{3,19},{4,7},{20,... | collective-permute-start | bytes 393224 | tf_op jit(solution)/shard_map/ppermute | solution.py:374
  26.3 6.4 %collective-permute-start.10 = (f32[13,8,256]{2,1,0:T(8,128)S(1)}, f32[13,8,256]{2,1,0:T(8,128)S(1)}, u32[]{:S(2)}, u32[]{:S(2)}) collective-permute-start(f32[13,8,256]{2,1,0:T(8,128)S(1)} %get-tuple-element.52), channel_id=1, source_target_pairs={{0,16},{16,17},{17,1},{1,2},{2,18},{18,19},{19,3},{3,0},{4,20},{20... | collective-permute-start | bytes 319496 | tf_op jit(solution)/shard_map/ppermute | solution.py:374
  26.3 6.4 %collective-permute-start.11 = (f32[13,8,256]{2,1,0:T(8,128)S(1)}, f32[13,8,256]{2,1,0:T(8,128)S(1)}, u32[]{:S(2)}, u32[]{:S(2)}) collective-permute-start(f32[13,8,256]{2,1,0:T(8,128)S(1)} %get-tuple-element.53), channel_id=1, source_target_pairs={{0,3},{16,0},{17,16},{1,17},{2,1},{18,2},{19,18},{3,19},{4,7},{20,... | collective-permute-start | bytes 319496 | tf_op jit(solution)/shard_map/ppermute | solution.py:374
  28.1 4.6 %collective-permute-start.9 = (f32[12,8,256]{2,1,0:T(8,128)S(1)}, f32[12,8,256]{2,1,0:T(8,128)S(1)}, u32[]{:S(2)}, u32[]{:S(2)}) collective-permute-start(f32[12,8,256]{2,1,0:T(8,128)S(1)} %get-tuple-element.51), channel_id=1, source_target_pairs={{0,12},{4,0},{8,4},{12,8},{1,13},{5,1},{9,5},{13,9},{2,14},{6,2},{... | collective-permute-start | bytes 294920 | tf_op jit(solution)/shard_map/ppermute | solution.py:375
  34.6 9.2 %collective-permute-start.12 = (f32[20,8,256]{2,1,0:T(8,128)S(1)}, f32[20,8,256]{2,1,0:T(8,128)S(1)}, u32[]{:S(2)}, u32[]{:S(2)}) collective-permute-start(f32[20,8,256]{2,1,0:T(8,128)S(1)} %get-tuple-element.58), channel_id=1, source_target_pairs={{0,4},{4,8},{8,12},{12,0},{1,5},{5,9},{9,13},{13,1},{2,6},{6,10},{... | collective-permute-start | bytes 491528 | tf_op jit(solution)/shard_map/ppermute | solution.py:375
  34.8 12.2 %collective-permute-start.13 = (f32[20,8,256]{2,1,0:T(8,128)S(1)}, f32[20,8,256]{2,1,0:T(8,128)S(1)}, u32[]{:S(2)}, u32[]{:S(2)}) collective-permute-start(f32[20,8,256]{2,1,0:T(8,128)S(1)} %get-tuple-element.59), channel_id=1, source_target_pairs={{0,12},{4,0},{8,4},{12,8},{1,13},{5,1},{9,5},{13,9},{2,14},{6,2},{... | collective-permute-start | bytes 491528 | tf_op jit(solution)/shard_map/ppermute | solution.py:375
  38.7 9.0 %collective-permute-start.16 = (f32[8,8,256]{2,1,0:T(8,128)S(1)}, f32[8,8,256]{2,1,0:T(8,128)S(1)}, u32[]{:S(2)}, u32[]{:S(2)}) collective-permute-start(f32[8,8,256]{2,1,0:T(8,128)S(1)} %get-tuple-element.62), channel_id=1, source_target_pairs={{0,4},{4,8},{8,12},{12,0},{1,5},{5,9},{9,13},{13,1},{2,6},{6,10},{... | collective-permute-start | bytes 196616 | tf_op jit(solution)/shard_map/ppermute | solution.py:375
  38.7 10.2 %collective-permute-start.14 = (f32[16,8,256]{2,1,0:T(8,128)S(1)}, f32[16,8,256]{2,1,0:T(8,128)S(1)}, u32[]{:S(2)}, u32[]{:S(2)}) collective-permute-start(f32[16,8,256]{2,1,0:T(8,128)S(1)} %get-tuple-element.60), channel_id=1, source_target_pairs={{0,16},{16,17},{17,1},{1,2},{2,18},{18,19},{19,3},{3,0},{4,20},{20... | collective-permute-start | bytes 393224 | tf_op jit(solution)/shard_map/ppermute | solution.py:374
  39.1 9.9 %collective-permute-start.15 = (f32[16,8,256]{2,1,0:T(8,128)S(1)}, f32[16,8,256]{2,1,0:T(8,128)S(1)}, u32[]{:S(2)}, u32[]{:S(2)}) collective-permute-start(f32[16,8,256]{2,1,0:T(8,128)S(1)} %get-tuple-element.61), channel_id=1, source_target_pairs={{0,3},{16,0},{17,16},{1,17},{2,1},{18,2},{19,18},{3,19},{4,7},{20,... | collective-permute-start | bytes 393224 | tf_op jit(solution)/shard_map/ppermute | solution.py:374
  43.8 5.1 %collective-permute-start.17 = (f32[8,8,256]{2,1,0:T(8,128)S(1)}, f32[8,8,256]{2,1,0:T(8,128)S(1)}, u32[]{:S(2)}, u32[]{:S(2)}) collective-permute-start(f32[8,8,256]{2,1,0:T(8,128)S(1)} %get-tuple-element.63), channel_id=1, source_target_pairs={{0,12},{4,0},{8,4},{12,8},{1,13},{5,1},{9,5},{13,9},{2,14},{6,2},{... | collective-permute-start | bytes 196616 | tf_op jit(solution)/shard_map/ppermute | solution.py:375
  47.0 3.9 %collective-permute-start.18 = (f32[10,8,256]{2,1,0:T(8,128)S(1)}, f32[10,8,256]{2,1,0:T(8,128)S(1)}, u32[]{:S(2)}, u32[]{:S(2)}) collective-permute-start(f32[10,8,256]{2,1,0:T(8,128)S(1)} %get-tuple-element.64), channel_id=1, source_target_pairs={{0,16},{16,17},{17,1},{1,2},{2,18},{18,19},{19,3},{3,0},{4,20},{20... | collective-permute-start | bytes 245768 | tf_op jit(solution)/shard_map/ppermute | solution.py:374
  47.7 4.4 %collective-permute-start.19 = (f32[10,8,256]{2,1,0:T(8,128)S(1)}, f32[10,8,256]{2,1,0:T(8,128)S(1)}, u32[]{:S(2)}, u32[]{:S(2)}) collective-permute-start(f32[10,8,256]{2,1,0:T(8,128)S(1)} %get-tuple-element.65), channel_id=1, source_target_pairs={{0,3},{16,0},{17,16},{1,17},{2,1},{18,2},{19,18},{3,19},{4,7},{20,... | collective-permute-start | bytes 245768 | tf_op jit(solution)/shard_map/ppermute | solution.py:374
  54.6 8.4 %collective-permute-start.20 = (f32[16,16,256]{2,1,0:T(8,128)S(1)}, f32[16,16,256]{2,1,0:T(8,128)S(1)}, u32[]{:S(2)}, u32[]{:S(2)}) collective-permute-start(f32[16,16,256]{2,1,0:T(8,128)S(1)} %get-tuple-element.67), channel_id=1, source_target_pairs={{0,16},{16,0},{1,17},{17,1},{2,18},{18,2},{3,19},{19,3},{4,20},{20... | collective-permute-start | bytes 786440 | tf_op jit(solution)/shard_map/ppermute | solution.py:441
